TPU v7x, 128 devices: a whole 4x4x4 slice. The times are simulated.
128 devices in a mesh: dp: 8 (over z_lo, y), tensor: 16 (over z_hi, x, core).
Axes of the slice: x: 4, y: 4, z: 4 (z_hi: 2, z_lo: 2; z = z_hi * 2 + z_lo), core: 2. Of those that a mesh axis runs over, the one named last changes fastest.
Arguments:
- block_input: bfloat16 [16384, 1024], P(('dp', 'tensor')), may hold values from -6 to 6
- segment_ids: int32 [16, 1024], P('dp'), may hold values from 0 to 3, never falling along the last dimension, each value on 1 to 512 neighbouring positions
- qkv_weight: bfloat16 [3, 1024, 1024], P(None, None, 'tensor'), may hold values from -1 to 1
- qv_bias: float32 [2, 1024], P(None, 'tensor'), may hold values from -3 to 3
- out_weight: bfloat16 [1024, 1024], P('tensor'), may hold values from -1.5 to 1.5
- out_bias: float32 [1024], replicated, may hold values from -3 to 3
- norm1_gain: float32 [1024], replicated, may hold values from 0.5 to 1.5
- norm1_bias: float32 [1024], replicated, may hold values from -3 to 3
- up_weight: bfloat16 [1024, 4096], P(None, 'tensor'), may hold values from -0.1875 to 0.1875
- up_bias: float32 [4096], P('tensor'), may hold values from -3 to 3
- down_weight: bfloat16 [4096, 1024], P('tensor'), may hold values from -0.09375 to 0.09375
- down_bias: float32 [1024], replicated, may hold values from -3 to 3
- norm2_gain: float32 [1024], replicated, may hold values from 0.5 to 1.5
- norm2_bias: float32 [1024], replicated, may hold values from -3 to 3
- cotangent: bfloat16 [16384, 1024], P(('dp', 'tensor')), may hold values from -6 to 6
Outputs:
- layer_output: bfloat16 [16384, 1024], P(('dp', 'tensor'))
- input_grad: bfloat16 [16384, 1024], P(('dp', 'tensor'))
- grad_qkv: float32 [3, 1024, 1024], P(None, None, 'tensor')
- grad_qv_bias: float32 [2, 1024], P(None, 'tensor')
- grad_out_proj: float32 [1024, 1024], P('tensor')
- grad_out_bias: float32 [1024], replicated
- grad_gain_one: float32 [1024], replicated
- grad_bias_one: float32 [1024], replicated
- grad_up: float32 [1024, 4096], P(None, 'tensor')
- grad_up_bias: float32 [4096], P('tensor')
- grad_down: float32 [4096, 1024], P('tensor')
- grad_down_bias: float32 [1024], replicated
- grad_gain_two: float32 [1024], replicated
- grad_bias_two: float32 [1024], replicated
Inputs may be any that keep to these rules, and one draw needn't show every extreme that they name: `segment_ids`: document numbers never fall along a sequence; each document holds 1 to 512 tokens.
All inputs are finite; a program needn't handle non-finite values.
Results may differ from a plain program's by a relative error of at most 0.023.
The roundings to bfloat16 on the way count: a program that leaves them out, or rounds other values in their place, can miss the bound.
Values may be sent and summed in bfloat16 or wider, within the bound.
A program may use at most 128 MiB of HBM per device.

v0:
```python
import jax
import jax.numpy as jnp
from jax import lax
from jax.sharding import PartitionSpec as P

HEAD_DIM = 64


EPS = 1e-12
MASKED = -1e30
ROOT_HALF = 0.7071067811865476
INV_ROOT_TAU = 0.3989422804014327


def layer_norm(rows, gain, shift):
    center = rows - jnp.mean(rows, axis=-1, keepdims=True)
    inverse = lax.rsqrt(jnp.mean(center * center, axis=-1, keepdims=True) + EPS)
    normed = center * inverse
    return (normed * gain + shift, normed, inverse)


def norm_back(grad, normed, inverse, gain):
    scaled = grad * gain
    return inverse * (
        scaled
        - jnp.mean(scaled, axis=-1, keepdims=True)
        - normed * jnp.mean(scaled * normed, axis=-1, keepdims=True)
    )


def gelu_parts(pre):
    cumul = 0.5 * (1.0 + lax.erf(pre * ROOT_HALF))
    return (pre * cumul, cumul + pre * jnp.exp(-0.5 * pre * pre) * INV_ROOT_TAU)


def masked_scores(queries, keys, segs):
    scores = jnp.einsum(
        "qhd,khd->hqk", queries, keys, preferred_element_type=jnp.float32
    ) * HEAD_DIM ** (-0.5)
    allowed = segs[:, None] == segs[None, :]
    return jnp.where(allowed[None], scores, MASKED)


def forward_seq(items):
    queries, keys, values, segs = items
    masked = masked_scores(queries, keys, segs)
    top = jnp.max(masked, axis=-1, keepdims=True)
    lse = top + jnp.log(jnp.sum(jnp.exp(masked - top), axis=-1, keepdims=True))
    probs = jnp.exp(masked - lse).astype(jnp.bfloat16)
    context = jnp.einsum("hqk,khd->qhd", probs, values, preferred_element_type=jnp.float32)
    return (context.astype(jnp.bfloat16), lse)


def backward_seq(items):
    queries, keys, values, segs, lse, d_context = items
    masked = masked_scores(queries, keys, segs)
    probs = jnp.exp(masked - lse)
    probs_half = probs.astype(jnp.bfloat16)
    d_values = jnp.einsum("hqk,qhd->khd", probs_half, d_context, preferred_element_type=jnp.float32)
    d_probs = jnp.einsum("qhd,khd->hqk", d_context, values, preferred_element_type=jnp.float32)
    d_scores = (
        probs * (d_probs - jnp.sum(probs * d_probs, axis=-1, keepdims=True)) * HEAD_DIM ** (-0.5)
    )
    d_scores = d_scores.astype(jnp.bfloat16)
    d_queries = jnp.einsum("hqk,khd->qhd", d_scores, keys, preferred_element_type=jnp.float32)
    d_keys = jnp.einsum("hqk,qhd->khd", d_scores, queries, preferred_element_type=jnp.float32)
    return (d_queries, d_keys, d_values)


def contract_rows(left, right):
    return lax.dot_general(
        left, right, (((0,), (0,)), ((), ())), preferred_element_type=jnp.float32
    )


def contract_cols(left, right):
    return lax.dot_general(
        left, right, (((1,), (1,)), ((), ())), preferred_element_type=jnp.float32
    )


def per_device(
    block_input,
    segment_ids,
    qkv_weight,
    qv_bias,
    out_weight,
    out_bias,
    norm1_gain,
    norm1_bias,
    up_weight,
    up_bias,
    down_weight,
    down_bias,
    norm2_gain,
    norm2_bias,
    cotangent,
):
    width = qkv_weight.shape[2]
    seq_count, seq_len = segment_ids.shape
    heads_here = width // HEAD_DIM
    gathered = lax.all_gather(block_input, "tensor", axis=0, tiled=True)
    tokens = gathered.shape[0]
    projected = jnp.einsum("td,cdw->ctw", gathered, qkv_weight, preferred_element_type=jnp.float32)
    queries = (projected[0] + qv_bias[0]).astype(jnp.bfloat16)
    keys = projected[1].astype(jnp.bfloat16)
    values = (projected[2] + qv_bias[1]).astype(jnp.bfloat16)

    def per_sequence(arr):
        return arr.reshape(seq_count, seq_len, heads_here, HEAD_DIM)

    seq_queries = per_sequence(queries)
    seq_keys = per_sequence(keys)
    seq_values = per_sequence(values)
    context, lse = lax.map(forward_seq, (seq_queries, seq_keys, seq_values, segment_ids))
    context = context.reshape(tokens, width)
    piece = context
    attended = lax.psum_scatter(
        jnp.dot(piece, out_weight, preferred_element_type=jnp.float32).astype(jnp.bfloat16),
        "tensor",
        scatter_dimension=0,
        tiled=True,
    ).astype(jnp.float32)
    first = block_input.astype(jnp.float32) + attended + out_bias
    hidden, normed_one, inverse_one = layer_norm(first, norm1_gain, norm1_bias)
    hidden_half = lax.all_gather(hidden.astype(jnp.bfloat16), "tensor", axis=0, tiled=True)
    pre = jnp.dot(hidden_half, up_weight, preferred_element_type=jnp.float32) + up_bias
    act, slope = gelu_parts(pre)
    act_half = act.astype(jnp.bfloat16)
    piece = act_half
    down_sum = lax.psum_scatter(
        jnp.dot(piece, down_weight, preferred_element_type=jnp.float32).astype(jnp.bfloat16),
        "tensor",
        scatter_dimension=0,
        tiled=True,
    ).astype(jnp.float32)
    second = hidden + down_sum + down_bias
    output, normed_two, inverse_two = layer_norm(second, norm2_gain, norm2_bias)
    grad = cotangent.astype(jnp.float32)
    g_gain_two = jnp.sum(grad * normed_two, axis=0)
    g_bias_two = jnp.sum(grad, axis=0)
    d_second = norm_back(grad, normed_two, inverse_two, norm2_gain)
    g_down_bias = jnp.sum(d_second, axis=0)
    d_second_all = lax.all_gather(d_second.astype(jnp.bfloat16), "tensor", axis=0, tiled=True)
    g_down = contract_rows(act_half, d_second_all)
    d_pre = contract_cols(d_second_all, down_weight) * slope
    g_up_bias = jnp.sum(d_pre, axis=0)
    d_pre_half = d_pre.astype(jnp.bfloat16)
    g_up = contract_rows(hidden_half, d_pre_half)
    piece = d_pre_half
    d_hidden = d_second + lax.psum_scatter(
        contract_cols(piece, up_weight), "tensor", scatter_dimension=0, tiled=True
    )
    g_gain_one = jnp.sum(d_hidden * normed_one, axis=0)
    g_bias_one = jnp.sum(d_hidden, axis=0)
    d_first = norm_back(d_hidden, normed_one, inverse_one, norm1_gain)
    g_out_bias = jnp.sum(d_first, axis=0)
    d_first_all = lax.all_gather(d_first.astype(jnp.bfloat16), "tensor", axis=0, tiled=True)
    g_out = contract_rows(context, d_first_all)
    d_context = contract_cols(d_first_all, out_weight).astype(jnp.bfloat16)
    d_queries, d_keys, d_values = lax.map(
        backward_seq, (seq_queries, seq_keys, seq_values, segment_ids, lse, per_sequence(d_context))
    )
    d_queries = d_queries.reshape(tokens, width)
    d_keys = d_keys.reshape(tokens, width)
    d_values = d_values.reshape(tokens, width)
    g_qv_bias = jnp.stack([jnp.sum(d_queries, axis=0), jnp.sum(d_values, axis=0)])
    d_qkv = jnp.stack([d_queries, d_keys, d_values]).astype(jnp.bfloat16)
    g_qkv = jnp.einsum("td,ctw->cdw", gathered, d_qkv, preferred_element_type=jnp.float32)
    piece = d_qkv
    input_grad = (
        d_first
        + lax.psum_scatter(
            jnp.einsum("ctw,cdw->td", piece, qkv_weight, preferred_element_type=jnp.float32).astype(
                jnp.bfloat16
            ),
            "tensor",
            scatter_dimension=0,
            tiled=True,
        ).astype(jnp.float32)
    ).astype(jnp.bfloat16)
    g_qkv, g_qv_bias, g_out, g_up, g_up_bias, g_down = (
        lax.psum(g_qkv.astype(jnp.bfloat16), "dp").astype(jnp.float32),
        lax.psum(g_qv_bias.astype(jnp.bfloat16), "dp").astype(jnp.float32),
        lax.psum(g_out.astype(jnp.bfloat16), "dp").astype(jnp.float32),
        lax.psum(g_up.astype(jnp.bfloat16), "dp").astype(jnp.float32),
        lax.psum(g_up_bias.astype(jnp.bfloat16), "dp").astype(jnp.float32),
        lax.psum(g_down.astype(jnp.bfloat16), "dp").astype(jnp.float32),
    )
    g_out_bias, g_gain_one, g_bias_one, g_down_bias, g_gain_two, g_bias_two = lax.psum(
        (g_out_bias, g_gain_one, g_bias_one, g_down_bias, g_gain_two, g_bias_two), ("dp", "tensor")
    )
    return (
        output.astype(jnp.bfloat16),
        input_grad,
        g_qkv,
        g_qv_bias,
        g_out,
        g_out_bias,
        g_gain_one,
        g_bias_one,
        g_up,
        g_up_bias,
        g_down,
        g_down_bias,
        g_gain_two,
        g_bias_two,
    )


def solution(mesh):
    placed = (
        P(("dp", "tensor"), None),
        P("dp", None),
        P(None, None, "tensor"),
        P(None, "tensor"),
        P("tensor", None),
        P(),
        P(),
        P(),
        P(None, "tensor"),
        P("tensor"),
        P("tensor", None),
        P(),
        P(),
        P(),
        P(("dp", "tensor"), None),
    )
    return jax.shard_map(
        per_device,
        mesh=mesh,
        in_specs=placed,
        out_specs=(
            P(("dp", "tensor"), None),
            P(("dp", "tensor"), None),
            P(None, None, "tensor"),
            P(None, "tensor"),
            P("tensor", None),
            P(),
            P(),
            P(),
            P(None, "tensor"),
            P("tensor"),
            P("tensor", None),
            P(),
            P(),
            P(),
        ),
        check_vma=False,
    )
```

profile of v0, /device:TPU:0, one launch (start us, length us, event | category | flops | bytes accessed | tf_op | source)
XLA Modules:
  0.0 735.6 jit_solution(5672415623791416606)
XLA Ops:
  8.8 60.3 %all-gather.5.cloned.1.call-done = bf16[2048,1024]{1,0:T(8,128)(2,1)} async-done(((bf16[128,1024]{1,0:T(8,128)(2,1)}), bf16[2048,1024]{1,0:T(8,128)(2,1)}) %all-gather.5.cloned.1.call-update) | async-done | bytes 4194320 | tf_op jit(solution)/shard_map/all_gather | solution.py:102
  69.0 3.8 fusion.50
  74.5 6.2 while.26
  81.1 3.2 convolution_convert_fusion.1
  84.4 79.2 %reduce-scatter.5.cloned.1.call-done = bf16[128,1024]{1,0:T(8,128)(2,1)} async-done(((bf16[2048,1024]{1,0:T(8,128)(2,1)}), bf16[128,1024]{1,0:T(8,128)(2,1)}) %reduce-scatter.5.cloned.1.call-update) | async-done | bytes 262160 | tf_op jit(solution)/shard_map/reduce_scatter | solution.py:118
  167.9 54.6 %all-gather.7.cloned.1.call-done = bf16[2048,1024]{1,0:T(8,128)(2,1)} async-done(((bf16[128,1024]{1,0:T(8,128)(2,1)}), bf16[2048,1024]{1,0:T(8,128)(2,1)}) %all-gather.7.cloned.1.call-update) | async-done | bytes 4194320 | tf_op jit(solution)/shard_map/all_gather | solution.py:126
  222.5 4.9 multiply_convert_fusion.1
  227.4 3.2 convolution_convert_fusion
  230.7 79.2 %reduce-scatter.7.cloned.1.call-done = bf16[128,1024]{1,0:T(8,128)(2,1)} async-done(((bf16[2048,1024]{1,0:T(8,128)(2,1)}), bf16[128,1024]{1,0:T(8,128)(2,1)}) %reduce-scatter.7.cloned.1.call-update) | async-done | bytes 262160 | tf_op jit(solution)/shard_map/reduce_scatter | solution.py:131
  312.3 2.5 fusion.77
  315.8 54.4 %all-gather.9.cloned.1.call-done = bf16[2048,1024]{1,0:T(8,128)(2,1)} async-done(((bf16[128,1024]{1,0:T(8,128)(2,1)}), bf16[2048,1024]{1,0:T(8,128)(2,1)}) %all-gather.9.cloned.1.call-update) | async-done | bytes 4194320 | tf_op jit(solution)/shard_map/all_gather | solution.py:144
  370.2 5.3 fusion.84
  376.5 4.5 fusion.73
  381.1 101.4 %reduce-scatter.9.cloned.1.call-done = f32[128,1024]{1,0:T(8,128)} async-done(((f32[2048,1024]{1,0:T(8,128)}), f32[128,1024]{1,0:T(8,128)}) %reduce-scatter.9.cloned.1.call-update) | async-done | bytes 524304 | tf_op jit(solution)/shard_map/reduce_scatter | solution.py:151
  486.9 4.4 convolution_convert_fusion.3
  491.3 3.4 convolution_convert_fusion.4
  494.7 46.9 %all-gather.11.cloned.1.call-done = bf16[2048,1024]{1,0:T(8,128)(2,1)} async-done(((bf16[128,1024]{1,0:T(8,128)(2,1)}), bf16[2048,1024]{1,0:T(8,128)(2,1)}) %all-gather.11.cloned.1.call-update) | async-done | bytes 4194320 | tf_op jit(solution)/shard_map/all_gather | solution.py:158
  541.6 3.6 convolution_convert_fusion.2
  545.5 10.9 %while.27 = (s32[]{:T(128)}, f32[2,1024,1,64]{1,3,2,0:T(8,128)S(1)}, bf16[2,1024,1,64]{1,3,2,0:T(8,128)(2,1)S(1)}, f32[2,1024,1,64]{1,3,2,0:T(8,128)S(1)}, bf16[...) while((s32[]{:T(128)}, ...), condition=%wide.region_17.18_spmd, body=%wide.region_15.17_spmd.sunk | while | flops 682621952 | bytes 33203324 | solution.py:161
  558.0 3.8 convolution_convert_fusion.5
  563.9 3.2 bitcast_convert_fusion
  567.9 66.9 %all-reduce = (f32[1024]{0:T(1024)}, f32[1024]{0:T(1024)}, f32[1024]{0:T(1024)}, f32[1024]{0:T(1024)}, f32[1024]{0:T(1024)}, /*index=5*/f32[1024]{0:T(1024)}) all-reduce(f32[1024]{0:T(1024)S(1)} %copy-done.25, f32[1024]{0:T(1024)S(1)} %copy-done.23, f32[1024]{0:T(1024)S(1)} %copy-done.24, ...), channel_id=1, replica_groups=mesh['dp'=8,'tensor'=16] {'dp','tensor'}, use_global_device_ids=true, to_apply=%region_25.26 | all-reduce | flops 6144 | bytes 49152 | tf_op jit(solution)/shard_map/psum | solution.py:190
  634.9 17.7 %all-reduce.1 = (bf16[2,64]{1,0:T(2,128)(2,1)S(1)}, bf16[256]{0:T(256)(128)(2,1)S(1)}) all-reduce(bf16[2,64]{1,0:T(2,128)(2,1)S(1)} %pad_maximum_fusion, bf16[256]{0:T(256)(128)(2,1)S(1)} %copy-done.35), channel_id=1, replica_groups=mesh['dp'=8,'tensor'=16] {'dp'}, use_global_device_ids=true, to_apply=%region_22.23 | all-reduce | flops 384 | bytes 1536 | tf_op jit(solution)/shard_map/psum | solution.py:184
  661.5 65.9 %reduce-scatter.11.cloned.1.call-done = bf16[128,1024]{1,0:T(8,128)(2,1)} async-done(((bf16[2048,1024]{1,0:T(8,128)(2,1)}), bf16[128,1024]{1,0:T(8,128)(2,1)}) %reduce-scatter.11.cloned.1.call-update) | async-done | bytes 262160 | tf_op jit(solution)/shard_map/reduce_scatter | solution.py:173
  (174 shorter events, 48.6 us)
Async XLA Ops:
  7.2 215.3 %copy-start = (bf16[1024,256]{1,0:T(8,128)(2,1)S(1)}, bf16[1024,256]{1,0:T(8,128)(2,1)}, u32[]{:S(2)}) copy-start(bf16[1024,256]{1,0:T(8,128)(2,1)} %param.27) | copy-start | bytes 1572868
  7.2 61.8 %all-gather.5.cloned.1.call-start = ((), (), s32[]{:S(2)}) async-start(), calls=%async_computation.4 | async-start | bytes 4456448 | tf_op jit(solution)/shard_map/all_gather | solution.py:102
  7.9 155.7 %reduce-scatter.5.cloned.1.call-start = ((), (), s32[]{:S(2)}) async-start(), calls=%async_computation.5 | async-start | bytes 4456448 | tf_op jit(solution)/shard_map/reduce_scatter | solution.py:118
  81.1 82.6 %copy-start.2 = (bf16[128,1024]{1,0:T(8,128)(2,1)S(1)}, bf16[128,1024]{1,0:T(8,128)(2,1)}, u32[]{:S(2)}) copy-start(bf16[128,1024]{1,0:T(8,128)(2,1)} %param.19) | copy-start | bytes 786436
  81.1 82.6 %copy-start.13 = (f32[1024]{0:T(1024)S(1)}, f32[1024]{0:T(1024)}, u32[]{:S(2)}) copy-start(f32[1024]{0:T(1024)} %param.24) | copy-start | bytes 12292
  81.1 84.9 %copy-start.14 = (f32[1024]{0:T(1024)S(1)}, f32[1024]{0:T(1024)}, u32[]{:S(2)}) copy-start(f32[1024]{0:T(1024)} %param.25) | copy-start | bytes 12292
  81.1 84.9 %copy-start.17 = (f32[1024]{0:T(1024)S(1)}, f32[1024]{0:T(1024)}, u32[]{:S(2)}) copy-start(f32[1024]{0:T(1024)} %param.26) | copy-start | bytes 12292
  84.3 138.2 %copy-start.34 = (f32[256]{0:T(256)S(1)}, f32[256]{0:T(256)}, u32[]{:S(2)}) copy-start(f32[256]{0:T(256)} %param.28) | copy-start | bytes 3076
  84.4 138.1 %all-gather.7.cloned.1.call-start = ((), (), s32[]{:S(2)}) async-start(), calls=%async_computation.6 | async-start | bytes 4456448 | tf_op jit(solution)/shard_map/all_gather | solution.py:126
  167.9 142.1 %reduce-scatter.7.cloned.1.call-start = ((), (), s32[]{:S(2)}) async-start(), calls=%async_computation.7 | async-start | bytes 4456448 | tf_op jit(solution)/shard_map/reduce_scatter | solution.py:131
  230.6 79.4 %copy-start.3 = (bf16[128,1024]{1,0:T(8,128)(2,1)S(1)}, bf16[128,1024]{1,0:T(8,128)(2,1)}, u32[]{:S(2)}) copy-start(bf16[128,1024]{1,0:T(8,128)(2,1)} %reduce-scatter.5.cloned.1.call-done) | copy-start | bytes 786436
  230.6 79.4 %copy-start.18 = (f32[1024]{0:T(1024)S(1)}, f32[1024]{0:T(1024)}, u32[]{:S(2)}) copy-start(f32[1024]{0:T(1024)} %param.26) | copy-start | bytes 12292
  230.6 79.4 %copy-start.27 = (f32[128]{0:T(128)S(1)}, f32[128]{0:T(128)}, u32[]{:S(2)}) copy-start(f32[128]{0:T(128)} %copy-done.26) | copy-start | bytes 1540
  230.6 79.4 %copy-start.29 = (f32[128]{0:T(128)S(1)}, f32[128]{0:T(128)}, u32[]{:S(2)}) copy-start(f32[128]{0:T(128)} %copy-done.28) | copy-start | bytes 1540
  230.6 79.4 %copy-start.30 = (f32[1024]{0:T(1024)S(1)}, f32[1024]{0:T(1024)}, u32[]{:S(2)}) copy-start(f32[1024]{0:T(1024)} %param.30) | copy-start | bytes 12292
  230.6 80.9 %copy-start.7 = (bf16[128,1024]{1,0:T(8,128)(2,1)S(1)}, bf16[128,1024]{1,0:T(8,128)(2,1)}, u32[]{:S(2)}) copy-start(bf16[128,1024]{1,0:T(8,128)(2,1)} %param.33) | copy-start | bytes 786436
  230.6 80.9 %copy-start.19 = (f32[1024]{0:T(1024)S(1)}, f32[1024]{0:T(1024)}, u32[]{:S(2)}) copy-start(f32[1024]{0:T(1024)} %param.31) | copy-start | bytes 12292
  230.7 139.5 %all-gather.9.cloned.1.call-start = ((), (), s32[]{:S(2)}) async-start(), calls=%async_computation.8 | async-start | bytes 4456448 | tf_op jit(solution)/shard_map/all_gather | solution.py:144
  315.5 167.0 %reduce-scatter.9.cloned.1.call-start = ((), (), s32[]{:S(2)}) async-start(), calls=%async_computation.9 | async-start | bytes 8912896 | tf_op jit(solution)/shard_map/reduce_scatter | solution.py:151
  381.0 160.6 %all-gather.11.cloned.1.call-start = ((), (), s32[]{:S(2)}) async-start(), calls=%async_computation.10 | async-start | bytes 4456448 | tf_op jit(solution)/shard_map/all_gather | solution.py:158
  486.8 166.9 %all-reduce.5.cloned.1.call-start = ((), (), s32[]{:S(2)}) async-start(), calls=%async_computation.12 | async-start | bytes 3145728 | tf_op jit(solution)/shard_map/psum | solution.py:183
  563.6 163.8 %reduce-scatter.11.cloned.1.call-start = ((), (), s32[]{:S(2)}) async-start(), calls=%async_computation.11 | async-start | bytes 4456448 | tf_op jit(solution)/shard_map/reduce_scatter | solution.py:173
  567.2 67.7 %copy-start.35 = (bf16[256]{0:T(256)(128)(2,1)S(1)}, bf16[256]{0:T(256)(128)(2,1)}, u32[]{:S(2)}) copy-start(bf16[256]{0:T(256)(128)(2,1)} %get-tuple-element.221) | copy-start | bytes 1540
  567.2 161.9 %copy-start.1 = (bf16[1024,256]{1,0:T(8,128)(2,1)S(1)}, bf16[1024,256]{1,0:T(8,128)(2,1)}, u32[]{:S(2)}) copy-start(bf16[1024,256]{1,0:T(8,128)(2,1)} %param.27) | copy-start | bytes 1572868
  (21 other events, 249.2 us)
Sparse Core Ops, SparseCore 0:
  10.5 58.5 all-gather.4
  84.5 79.1 reduce-scatter.4
  168.0 54.4 all-gather.6
  230.8 79.1 reduce-scatter.6
  315.7 54.4 all-gather.8
  381.1 101.3 reduce-scatter.8
  486.9 54.6 all-gather.10
  563.8 78.8 all-reduce.4
  646.7 80.6 reduce-scatter.10
where the time goes:
time: 736 us
  waiting for transfers between devices  543 us (74%)
  blocking collectives  84.6 us (11%)
  matrix products  57.6 us (8%)
  other arithmetic  29.4 us (4%)
  between operations  14.4 us (2%)
    reduce_scatter x1, waiting for transfers between devices, per_device(): lax.psum_scatter(contract_cols(piece, up_weight), 'tensor', scatter_dimen...  101 us
    reduce_scatter x1, waiting for transfers between devices, per_device(): lax.psum_scatter(jnp.dot(piece, down_weight, preferred_element_type=jnp.f...  79.2 us
    reduce_scatter x1, waiting for transfers between devices, per_device(): lax.psum_scatter(jnp.dot(piece, out_weight, preferred_element_type=jnp.fl...  79.2 us
    psum x1, blocking collectives, per_device(): lax.psum((g_out_bias, g_gain_one, g_bias_one, g_down_bias, g_gain_two, g_...  66.9 us
    reduce_scatter x1, waiting for transfers between devices, per_device(): lax.psum_scatter(jnp.einsum('ctw,cdw->td', piece, qkv_weight, preferred_e...  65.9 us
    all_gather x1, waiting for transfers between devices, per_device(): gathered = lax.all_gather(block_input, 'tensor', axis=0, tiled=True)  60.3 us
    all_gather x1, waiting for transfers between devices, per_device(): lax.all_gather(hidden.astype(jnp.bfloat16), 'tensor', axis=0, tiled=True)  54.6 us
    all_gather x1, waiting for transfers between devices, per_device(): lax.all_gather(d_second.astype(jnp.bfloat16), 'tensor', axis=0, tiled=True)  54.4 us
  transfers between devices with their start and end apart: 9, of which 8 were waited for; matrix products, arithmetic and copies ran while one was open for 3% of the time, Pallas kernels for 0%

commit v1 on v0

v1 whole, which is shorter than its diff:
```python
import jax
import jax.numpy as jnp
from jax import lax
from jax.experimental import pallas as pl
from jax.experimental.pallas import tpu as pltpu
from jax.sharding import PartitionSpec as P

HEAD_DIM = 64
RING = 8
BLOCK = 128
HALF = 64
MESH = pl.DeviceIdType.MESH
VMEM_WHOLE = pl.BlockSpec(memory_space=pltpu.VMEM)


EPS = 1e-12
MASKED = -1e30
ROOT_HALF = 0.7071067811865476
INV_ROOT_TAU = 0.3989422804014327


def ring_place():
    t = lax.axis_index("tensor")
    dp = lax.axis_index("dp")
    base = (t // RING) * RING
    j = t % RING
    x = j // 2
    c = j % 2

    def block_of(step, other=False):
        xx = lax.rem(x + step + 4, 4)
        return xx * 2 + ((1 - c) if other else c)

    def device_of(step, other=False):
        return (dp, base + block_of(step, other))

    return j, block_of, device_of


def greet(devices):
    barrier = pltpu.get_barrier_semaphore()
    for device in devices:
        pl.semaphore_signal(barrier, inc=1, device_id=device, device_id_type=MESH)
    pl.semaphore_wait(barrier, len(devices))


def remote(src, dst, send, recv, slot, device):
    return pltpu.make_async_remote_copy(
        src_ref=src,
        dst_ref=dst,
        send_sem=send.at[slot],
        recv_sem=recv.at[slot],
        device_id=device,
        device_id_type=MESH,
    )


FIRST = pl.ds(0, HALF)
SECOND = pl.ds(HALF, HALF)


def gather_kernel(x_ref, o_ref, send, recv):
    j, block_of, device_of = ring_place()
    right, left, partner = device_of(1), device_of(-1), device_of(0, True)
    mine, from_left, from_right, across = block_of(0), block_of(-1), block_of(1), block_of(2)
    greet((right, left, partner))
    o_at = o_ref.at
    ra = remote(x_ref.at[FIRST], o_at[mine, FIRST], send, recv, 0, right)
    lb = remote(x_ref.at[SECOND], o_at[mine, SECOND], send, recv, 3, left)
    rb = remote(x_ref.at[SECOND], o_at[mine, SECOND], send, recv, 1, right)
    la = remote(x_ref.at[FIRST], o_at[mine, FIRST], send, recv, 2, left)
    own = remote(x_ref, o_at[mine], send, recv, 6, partner)
    started = [ra, lb, rb, la, own]
    for copy in started:
        copy.start()
    o_ref[pl.ds(mine, 1)] = x_ref[...].reshape(1, BLOCK, x_ref.shape[1])

    def pass_on(slot, block, half, partner_slot, device=None, device_slot=None):
        arrived = remote(o_at[block, half], o_at[block, half], send, recv, slot, partner)
        arrived.wait_recv()
        if device is not None:
            on = remote(o_at[block, half], o_at[block, half], send, recv, device_slot, device)
            on.start()
            started.append(on)
        share = remote(o_at[block, half], o_at[block, half], send, recv, partner_slot, partner)
        share.start()
        started.append(share)

    pass_on(0, from_left, FIRST, 7, right, 4)
    pass_on(3, from_right, SECOND, 10, left, 5)
    pass_on(1, from_left, SECOND, 8)
    pass_on(2, from_right, FIRST, 9)
    pass_on(4, across, FIRST, 11)
    pass_on(5, across, SECOND, 12)
    other = {
        6: o_at[block_of(0, True)],
        7: o_at[block_of(-1, True), FIRST],
        8: o_at[block_of(-1, True), SECOND],
        9: o_at[block_of(1, True), FIRST],
        10: o_at[block_of(1, True), SECOND],
        11: o_at[block_of(2, True), FIRST],
        12: o_at[block_of(2, True), SECOND],
    }
    for slot, place in other.items():
        remote(place, place, send, recv, slot, partner).wait_recv()
    for copy in started:
        copy.wait_send()


def gather_rows(x):
    rows, width = x.shape
    out = pl.pallas_call(
        gather_kernel,
        out_shape=jax.ShapeDtypeStruct((RING, rows, width), x.dtype),
        in_specs=[VMEM_WHOLE],
        out_specs=VMEM_WHOLE,
        scratch_shapes=[pltpu.SemaphoreType.DMA((13,)), pltpu.SemaphoreType.DMA((13,))],
        compiler_params=pltpu.CompilerParams(collective_id=0, has_side_effects=True),
    )(x)
    return out.reshape(RING * rows, width)


def scatter_kernel(y_ref, o_ref, pair, stage, transit, final, send, recv):
    j, block_of, device_of = ring_place()
    right, left, partner = device_of(1), device_of(-1), device_of(0, True)
    greet((right, left, partner))
    wide = jnp.float32
    started = []

    def go(src, dst, slot, device):
        copy = remote(src, dst, send, recv, slot, device)
        copy.start()
        started.append(copy)

    def arrived(place, slot):
        remote(place, place, send, recv, slot, partner).wait_recv()

    for k in (2, 1, 3, 0):
        go(y_ref.at[block_of(k, True)], pair.at[k], k, partner)

    def chip_sum(k, half):
        return y_ref[block_of(k), half].astype(wide) + pair[k, half].astype(wide)

    arrived(pair.at[2], 2)
    stage[0] = chip_sum(2, FIRST).astype(stage.dtype)
    go(stage.at[0], transit.at[0], 4, right)
    stage[1] = chip_sum(2, SECOND).astype(stage.dtype)
    go(stage.at[1], transit.at[1], 5, left)
    arrived(pair.at[1], 1)
    stage[2] = chip_sum(1, SECOND).astype(stage.dtype)
    go(stage.at[2], final.at[0, 1], 6, right)
    arrived(pair.at[3], 3)
    stage[3] = chip_sum(3, FIRST).astype(stage.dtype)
    go(stage.at[3], final.at[1, 0], 7, left)
    arrived(transit.at[0], 4)
    stage[4] = (chip_sum(1, FIRST) + transit[0].astype(wide)).astype(stage.dtype)
    go(stage.at[4], final.at[0, 0], 8, right)
    arrived(transit.at[1], 5)
    stage[5] = (chip_sum(3, SECOND) + transit[1].astype(wide)).astype(stage.dtype)
    go(stage.at[5], final.at[1, 1], 9, left)
    arrived(pair.at[0], 0)
    arrived(final.at[0, 1], 6)
    arrived(final.at[1, 0], 7)
    arrived(final.at[0, 0], 8)
    arrived(final.at[1, 1], 9)
    for h, half in enumerate((FIRST, SECOND)):
        o_ref[half] = chip_sum(0, half) + final[0, h].astype(wide) + final[1, h].astype(wide)
    for copy in started:
        copy.wait_send()


def scatter_rows(y):
    tokens, width = y.shape
    rows = tokens // RING
    return pl.pallas_call(
        scatter_kernel,
        out_shape=jax.ShapeDtypeStruct((rows, width), jnp.float32),
        in_specs=[VMEM_WHOLE],
        out_specs=VMEM_WHOLE,
        scratch_shapes=[
            pltpu.VMEM((4, rows, width), y.dtype),
            pltpu.VMEM((6, HALF, width), y.dtype),
            pltpu.VMEM((2, HALF, width), y.dtype),
            pltpu.VMEM((2, 2, HALF, width), y.dtype),
            pltpu.SemaphoreType.DMA((10,)),
            pltpu.SemaphoreType.DMA((10,)),
        ],
        compiler_params=pltpu.CompilerParams(collective_id=1, has_side_effects=True),
    )(y.reshape(RING, rows, width))


def layer_norm(rows, gain, shift):
    center = rows - jnp.mean(rows, axis=-1, keepdims=True)
    inverse = lax.rsqrt(jnp.mean(center * center, axis=-1, keepdims=True) + EPS)
    normed = center * inverse
    return (normed * gain + shift, normed, inverse)


def norm_back(grad, normed, inverse, gain):
    scaled = grad * gain
    return inverse * (
        scaled
        - jnp.mean(scaled, axis=-1, keepdims=True)
        - normed * jnp.mean(scaled * normed, axis=-1, keepdims=True)
    )


def gelu_parts(pre):
    cumul = 0.5 * (1.0 + lax.erf(pre * ROOT_HALF))
    return (pre * cumul, cumul + pre * jnp.exp(-0.5 * pre * pre) * INV_ROOT_TAU)


def masked_scores(queries, keys, segs):
    scores = jnp.einsum(
        "qhd,khd->hqk", queries, keys, preferred_element_type=jnp.float32
    ) * HEAD_DIM ** (-0.5)
    allowed = segs[:, None] == segs[None, :]
    return jnp.where(allowed[None], scores, MASKED)


def forward_seq(items):
    queries, keys, values, segs = items
    masked = masked_scores(queries, keys, segs)
    top = jnp.max(masked, axis=-1, keepdims=True)
    lse = top + jnp.log(jnp.sum(jnp.exp(masked - top), axis=-1, keepdims=True))
    probs = jnp.exp(masked - lse).astype(jnp.bfloat16)
    context = jnp.einsum("hqk,khd->qhd", probs, values, preferred_element_type=jnp.float32)
    return (context.astype(jnp.bfloat16), lse)


def backward_seq(items):
    queries, keys, values, segs, lse, d_context = items
    masked = masked_scores(queries, keys, segs)
    probs = jnp.exp(masked - lse)
    probs_half = probs.astype(jnp.bfloat16)
    d_values = jnp.einsum("hqk,qhd->khd", probs_half, d_context, preferred_element_type=jnp.float32)
    d_probs = jnp.einsum("qhd,khd->hqk", d_context, values, preferred_element_type=jnp.float32)
    d_scores = (
        probs * (d_probs - jnp.sum(probs * d_probs, axis=-1, keepdims=True)) * HEAD_DIM ** (-0.5)
    )
    d_scores = d_scores.astype(jnp.bfloat16)
    d_queries = jnp.einsum("hqk,khd->qhd", d_scores, keys, preferred_element_type=jnp.float32)
    d_keys = jnp.einsum("hqk,qhd->khd", d_scores, queries, preferred_element_type=jnp.float32)
    return (d_queries, d_keys, d_values)


def contract_rows(left, right):
    return lax.dot_general(
        left, right, (((0,), (0,)), ((), ())), preferred_element_type=jnp.float32
    )


def contract_cols(left, right):
    return lax.dot_general(
        left, right, (((1,), (1,)), ((), ())), preferred_element_type=jnp.float32
    )


def trade(arr):
    return lax.ppermute(arr, "tensor", [(t, (t + RING) % (2 * RING)) for t in range(2 * RING)])


def per_device(
    block_input,
    segment_ids,
    qkv_weight,
    qv_bias,
    out_weight,
    out_bias,
    norm1_gain,
    norm1_bias,
    up_weight,
    up_bias,
    down_weight,
    down_bias,
    norm2_gain,
    norm2_bias,
    cotangent,
):
    half = jnp.bfloat16
    wide = jnp.float32
    my_seq = lax.axis_index("tensor") // RING
    segs = lax.dynamic_index_in_dim(segment_ids, my_seq, 0, keepdims=False)
    seq_len = segs.shape[0]
    qkv_two = jnp.concatenate([qkv_weight, trade(qkv_weight)], axis=2)
    qv_bias_two = jnp.concatenate([qv_bias, trade(qv_bias)], axis=1)
    out_two = jnp.concatenate([out_weight, trade(out_weight)], axis=0)
    up_two = jnp.concatenate([up_weight, trade(up_weight)], axis=1)
    up_bias_two = jnp.concatenate([up_bias, trade(up_bias)], axis=0)
    down_two = jnp.concatenate([down_weight, trade(down_weight)], axis=0)

    gathered = gather_rows(block_input)
    projected = jnp.einsum("td,cdw->ctw", gathered, qkv_two, preferred_element_type=wide)
    queries = (projected[0] + qv_bias_two[0]).astype(half)
    keys = projected[1].astype(half)
    values = (projected[2] + qv_bias_two[1]).astype(half)
    width = queries.shape[1]

    def by_head(arr):
        return arr.reshape(seq_len, width // HEAD_DIM, HEAD_DIM)

    context, lse = forward_seq((by_head(queries), by_head(keys), by_head(values), segs))
    context = context.reshape(seq_len, width)
    attended = scatter_rows(jnp.dot(context, out_two, preferred_element_type=wide).astype(half))
    first = block_input.astype(wide) + attended + out_bias
    hidden, normed_one, inverse_one = layer_norm(first, norm1_gain, norm1_bias)
    hidden_half = gather_rows(hidden.astype(half))
    pre = jnp.dot(hidden_half, up_two, preferred_element_type=wide) + up_bias_two
    act, slope = gelu_parts(pre)
    act_half = act.astype(half)
    down_sum = scatter_rows(jnp.dot(act_half, down_two, preferred_element_type=wide).astype(half))
    second = hidden + down_sum + down_bias
    output, normed_two, inverse_two = layer_norm(second, norm2_gain, norm2_bias)
    grad = cotangent.astype(wide)
    g_gain_two = jnp.sum(grad * normed_two, axis=0)
    g_bias_two = jnp.sum(grad, axis=0)
    d_second = norm_back(grad, normed_two, inverse_two, norm2_gain)
    g_down_bias = jnp.sum(d_second, axis=0)
    d_second_all = gather_rows(d_second.astype(half))
    g_down = contract_rows(act_half, d_second_all)
    d_pre = contract_cols(d_second_all, down_two) * slope
    g_up_bias = jnp.sum(d_pre, axis=0)
    d_pre_half = d_pre.astype(half)
    g_up = contract_rows(hidden_half, d_pre_half)
    d_hidden = d_second + scatter_rows(contract_cols(d_pre_half, up_two).astype(half))
    g_gain_one = jnp.sum(d_hidden * normed_one, axis=0)
    g_bias_one = jnp.sum(d_hidden, axis=0)
    d_first = norm_back(d_hidden, normed_one, inverse_one, norm1_gain)
    g_out_bias = jnp.sum(d_first, axis=0)
    d_first_all = gather_rows(d_first.astype(half))
    g_out = contract_rows(context, d_first_all)
    d_context = contract_cols(d_first_all, out_two).astype(half)
    d_queries, d_keys, d_values = (
        arr.reshape(seq_len, width)
        for arr in backward_seq(
            (by_head(queries), by_head(keys), by_head(values), segs, lse, by_head(d_context))
        )
    )
    g_qv_bias = jnp.stack([jnp.sum(d_queries, axis=0), jnp.sum(d_values, axis=0)])
    d_qkv = jnp.stack([d_queries, d_keys, d_values]).astype(half)
    g_qkv = jnp.einsum("td,ctw->cdw", gathered, d_qkv, preferred_element_type=wide)
    d_rows = jnp.einsum("ctw,cdw->td", d_qkv, qkv_two, preferred_element_type=wide)
    input_grad = (d_first + scatter_rows(d_rows.astype(half))).astype(half)

    def total(grad_two, axis):
        size = grad_two.shape[axis] // 2
        own = lax.slice_in_dim(grad_two, 0, size, axis=axis)
        other = lax.slice_in_dim(grad_two, size, 2 * size, axis=axis)
        return (own + trade(other.astype(half)).astype(wide)).astype(half)

    early = lax.psum((total(g_up, 1), total(g_down, 0)), "dp")
    late = lax.psum((total(g_qkv, 2), total(g_out, 0)), "dp")
    g_up, g_down, g_qkv, g_out = (arr.astype(wide) for arr in early + late)

    sums = jnp.stack([g_out_bias, g_gain_one, g_bias_one, g_down_bias, g_gain_two, g_bias_two])
    sums = lax.psum(sums, ("dp", "tensor"))

    def total_small(grad_two, axis):
        size = grad_two.shape[axis] // 2
        own = lax.slice_in_dim(grad_two, 0, size, axis=axis)
        other = lax.slice_in_dim(grad_two, size, 2 * size, axis=axis)
        return own + trade(other)

    g_qv_bias, g_up_bias = lax.psum((total_small(g_qv_bias, 1), total_small(g_up_bias, 0)), "dp")
    return (
        output.astype(half),
        input_grad,
        g_qkv,
        g_qv_bias,
        g_out,
        sums[0],
        sums[1],
        sums[2],
        g_up,
        g_up_bias,
        g_down,
        sums[3],
        sums[4],
        sums[5],
    )


def solution(mesh):
    placed = (
        P(("dp", "tensor"), None),
        P("dp", None),
        P(None, None, "tensor"),
        P(None, "tensor"),
        P("tensor", None),
        P(),
        P(),
        P(),
        P(None, "tensor"),
        P("tensor"),
        P("tensor", None),
        P(),
        P(),
        P(),
        P(("dp", "tensor"), None),
    )
    return jax.shard_map(
        per_device,
        mesh=mesh,
        in_specs=placed,
        out_specs=(
            P(("dp", "tensor"), None),
            P(("dp", "tensor"), None),
            P(None, None, "tensor"),
            P(None, "tensor"),
            P("tensor", None),
            P(),
            P(),
            P(),
            P(None, "tensor"),
            P("tensor"),
            P("tensor", None),
            P(),
            P(),
            P(),
        ),
        check_vma=False,
    )
```

time: 736 us -> 414 us (0.56)
  waiting for transfers between devices: 543 us -> 27.9 us
  Pallas kernels: 0 us -> 130 us
  matrix products: 57.6 us -> 82.1 us
  starting transfers between devices: 0.77 us -> 21.3 us
  local copies, waits for them, and re-layouts: 5.85 us -> 18.1 us
    reduce_scatter x4 -> x0, waiting for transfers between devices: 326 us -> none  [the longest x1 101 us: per_device(): lax.psum_scatter(contract_cols(piece, up_weight), 'tensor', scatter_dimen...]
    all_gather x4 -> x0, waiting for transfers between devices: 216 us -> none  [the longest x1 60.3 us: per_device(): gathered = lax.all_gather(block_input, 'tensor', axis=0, tiled=True)]
    pallas_call x0 -> x8, Pallas kernels: none -> 130 us  [the longest x4 66 us: scatter_rows(): pl.pallas_call(scatter_kernel, out_shape=jax.ShapeDtypeStruct((rows, widt...]
    ppermute x0 -> x12, waiting for transfers between devices: none -> 27.8 us  [trade(): lax.ppermute(arr, 'tensor', [(t, (t + RING) % (2 * RING)) for t in range(...]
    ppermute x0 -> x12, starting transfers between devices: none -> 21.3 us  [trade(): lax.ppermute(arr, 'tensor', [(t, (t + RING) % (2 * RING)) for t in range(...]
    dot_general x2 -> x1, matrix products: 0.97 us -> 15.7 us  [backward_seq(): jnp.einsum('hqk,khd->qhd', d_scores, keys, preferred_element_type=jnp.flo...]
    dot_general x2 -> x1, matrix products: 1.52 us -> 15.1 us  [backward_seq(): jnp.einsum('hqk,qhd->khd', d_scores, queries, preferred_element_type=jnp....]
    convert_element_type x14 -> x12, other arithmetic: 16.6 us -> 17.4 us  [the longest x4 7.79 us: per_device(): g_up, g_down, g_qkv, g_out = (arr.astype(wide) for arr in early + late)]
  transfers between devices with their start and end apart: 9 -> 13, of which waited for: 8 -> 5; matrix products, arithmetic and copies ran while one was open for 3% -> 12% of each run, Pallas kernels for 0% -> 16%
where the time goes in v1:
time: 414 us; the launch traced here: 408 us
  Pallas kernels  130 us (31%)
  blocking collectives  86 us (21%)
  matrix products  82.1 us (20%)
  other arithmetic  27.9 us (7%)
  waiting for transfers between devices  27.9 us (7%)
  starting transfers between devices  21.3 us (5%)
  local copies, waits for them, and re-layouts  18.1 us (4%)
  between operations  15.1 us (4%)
    psum x1, blocking collectives, per_device(): sums = lax.psum(sums, ('dp', 'tensor'))  67.5 us
    pallas_call x4, Pallas kernels, scatter_rows(): pl.pallas_call(scatter_kernel, out_shape=jax.ShapeDtypeStruct((rows, widt...  66 us
    pallas_call x4, Pallas kernels, gather_rows(): pl.pallas_call(gather_kernel, out_shape=jax.ShapeDtypeStruct((RING, rows,...  63.8 us
    ppermute x12, waiting for transfers between devices, trade(): lax.ppermute(arr, 'tensor', [(t, (t + RING) % (2 * RING)) for t in range(...  27.8 us
    ppermute x12, starting transfers between devices, trade(): lax.ppermute(arr, 'tensor', [(t, (t + RING) % (2 * RING)) for t in range(...  21.3 us
    psum x1, blocking collectives, per_device(): lax.psum((total_small(g_qv_bias, 1), total_small(g_up_bias, 0)), 'dp')  18.5 us
    dot_general x1, matrix products, backward_seq(): jnp.einsum('hqk,khd->qhd', d_scores, keys, preferred_element_type=jnp.flo...  15.7 us
    dot_general x1, matrix products, backward_seq(): jnp.einsum('hqk,qhd->khd', d_scores, queries, preferred_element_type=jnp....  15.1 us
  transfers between devices with their start and end apart: 13, of which 5 were waited for; matrix products, arithmetic and copies ran while one was open for 12% of the time, Pallas kernels for 16%

profile of v1, /device:TPU:0, one launch (start us, length us, event | category | flops | bytes accessed | tf_op | source)
XLA Modules:
  0.0 408.2 jit_solution(7108467499237772822)
XLA Ops:
  7.3 4.0 collective-permute-start.1
  11.4 3.4 collective-permute-start
  14.9 3.4 collective-permute-start.5
  24.9 16.3 %shard_map.254 = bf16[8,128,1024]{2,1,0:T(8,128)(2,1)} custom-call(bf16[128,1024]{1,0:T(8,128)(2,1)} %x_ref.1), custom_call_target="tpu_custom_call" | custom-call | tf_op jit(solution)/shard_map/pallas_call | solution.py:112
  41.7 7.3 %collective-permute-done.4 = f32[256]{0:T(256)S(1)} collective-permute-done((f32[256]{0:T(256)S(1)}, f32[256]{0:T(256)S(1)}, u32[]{:S(2)}, u32[]{:S(2)}) %collective-permute-start.4) | collective-permute-done | bytes 1056 | tf_op jit(solution)/shard_map/ppermute | solution.py:260
  62.9 17.0 %shard_map.255 = f32[128,1024]{1,0:T(8,128)} custom-call(bf16[8,128,1024]{2,1,0:T(8,128)(2,1)} %bitcast.73), custom_call_target="tpu_custom_call" | custom-call | tf_op jit(solution)/shard_map/pallas_call | solution.py:175
  82.2 16.0 %shard_map.256 = bf16[8,128,1024]{2,1,0:T(8,128)(2,1)} custom-call(bf16[128,1024]{1,0:T(8,128)(2,1)} %fusion.52.x_ref), custom_call_target="tpu_custom_call" | custom-call | tf_op jit(solution)/shard_map/pallas_call | solution.py:112
  99.4 4.7 %multiply_convert_fusion.1 = (bf16[1024,512]{1,0:T(8,128)(2,1)S(1)}, f32[1024,512]{1,0:T(8,128)}) fusion(f32[512]{0:T(512)S(1)} %pad_maximum_fusion.3, bf16[1024,1024]{1,0:T(8,128)(2,1)} %bitcast.81, bf16[1024,512]{1,0:T(8,128)(2,1)S(1)} %constant_dynamic-update-slice_fusion.4), kind=kOutput, calls=%fused_computation.26 | convolution fusion | flops 1076887552 | bytes 6293504 | tf_op jit(solution)/shard_map/dot_general | solution.py:308
  108.2 16.9 %shard_map.257 = f32[128,1024]{1,0:T(8,128)} custom-call(bf16[8,128,1024]{2,1,0:T(8,128)(2,1)} %bitcast.78), custom_call_target="tpu_custom_call" | custom-call | tf_op jit(solution)/shard_map/pallas_call | solution.py:175
  129.3 15.7 %shard_map.258 = bf16[8,128,1024]{2,1,0:T(8,128)(2,1)} custom-call(bf16[128,1024]{1,0:T(8,128)(2,1)} %convert_element_type.122.x_ref), custom_call_target="tpu_custom_call" | custom-call | tf_op jit(solution)/shard_map/pallas_call | solution.py:112
  145.0 3.3 fusion.83
  148.4 4.5 %fusion.81 = (f32[512]{0:T(512)}, bf16[1024,512]{1,0:T(8,128)(2,1)S(1)}) fusion(f32[1024,512]{1,0:T(8,128)} %get-tuple-element.55, f32[512]{0:T(512)S(1)} %pad_maximum_fusion.3, bf16[1024,1024]{1,0:T(8,128)(2,1)S(1)} %bitcast.75, bf16[512,1024]{1,0:T(8,128)(2,1)} %copy-done.15), kind=kOutput, calls=%fused_computation.125 | convolution fusion | flops 1080032768 | bytes 6295552 | tf_op jit(solution)/shard_map/dot_general | solution.py:254
  155.6 16.8 %shard_map.259 = f32[128,1024]{1,0:T(8,128)} custom-call(bf16[8,128,1024]{2,1,0:T(8,128)(2,1)} %bitcast.77), custom_call_target="tpu_custom_call" | custom-call | tf_op jit(solution)/shard_map/pallas_call | solution.py:175
  176.0 15.8 %shard_map.260 = bf16[8,128,1024]{2,1,0:T(8,128)(2,1)} custom-call(bf16[128,1024]{1,0:T(8,128)(2,1)} %convert_element_type.125.x_ref), custom_call_target="tpu_custom_call" | custom-call | tf_op jit(solution)/shard_map/pallas_call | solution.py:112
  196.5 6.6 %fusion.77 = (f32[2,64]{1,0:T(2,128)S(1)}, bf16[1024,2,64]{0,2,1:T(8,128)(2,1)}) fusion(bf16[1024,2,64]{0,2,1:T(8,128)(2,1)S(1)} %bitcast.85, f32[2,1024,1024]{1,2,0:T(8,128)} %copy-done.2, f32[2,1024]{1,0:T(2,128)S(1)} %log_add_fusion, pred[1024,1024]{0,1:T(8,128)(4,1)S(1)} %copy-done.5), kind=kOutput, calls=%fused_computation.123 | convolution fusion | flops 277086080 | bytes 9970176 | tf_op jit(solution)/shard_map/hqk,qhd->khd/dot_general | solution.py:236
  203.1 4.6 %fusion.54 = f32[2,1024,1024]{1,2,0:T(8,128)} fusion(bf16[1024,2,64]{0,2,1:T(8,128)(2,1)S(1)} %bitcast.86, f32[1024,2,64]{0,2,1:T(8,128)S(1)} %bitcast.84, f32[2,64]{1,0:T(2,128)S(1)} %add.144), kind=kOutput, calls=%fused_computation.82 | convolution fusion | flops 268697600 | bytes 9175552 | tf_op jit(solution)/shard_map/qhd,khd->hqk/dot_general | solution.py:237
  207.7 15.1 %fusion.36 = bf16[2,64,1024]{2,1,0:T(8,128)(2,1)} fusion(f32[2,1024,1024]{1,2,0:T(8,128)} %fusion.54, f32[2,1024,1024]{1,2,0:T(8,128)} %copy-done.2, f32[2,1024]{1,0:T(2,128)S(1)} %log_add_fusion, pred[1024,1024]{0,1:T(8,128)(4,1)} %copy-done.4, f32[1024,2,64]{0,2,1:T(8,128)} %bitcast.90, f32[2,64]{1,0:T(2,128)S(1)} %add.148), kind=kOutput, calls=%fused_computation.38 | convolution fusion | flops 291900416 | bytes 18620928 | tf_op jit(solution)/shard_map/hqk,qhd->khd/dot_general | solution.py:243
  222.8 15.7 %fusion.76 = (f32[2,64]{1,0:T(2,128)}, bf16[1024,2,64]{0,2,1:T(8,128)(2,1)}) fusion(bf16[1024,2,64]{0,2,1:T(8,128)(2,1)S(1)} %bitcast.92, f32[2,1024,1024]{1,2,0:T(8,128)} %fusion.54, f32[2,1024,1024]{1,2,0:T(8,128)} %copy-done.2, f32[2,1024]{1,0:T(2,128)S(1)} %log_add_fusion, pred[1024,1024]{0,1:T(8,128)(4,1)} %copy-done.4), kind=kOutput, calls=%fused_computation.122 | convolution fusion | flops 291769216 | bytes 18358784 | tf_op jit(solution)/shard_map/hqk,khd->qhd/dot_general | solution.py:242
  260.4 6.7 %collective-permute-done.6 = bf16[3,1024,64]{1,2,0:T(8,128)(2,1)S(1)} collective-permute-done((bf16[3,1024,64]{1,2,0:T(8,128)(2,1)S(1)}, bf16[3,1024,64]{1,2,0:T(8,128)(2,1)S(1)}, u32[]{:S(2)}, u32[]{:S(2)}) %collective-permute-start.6) | collective-permute-done | bytes 393248 | tf_op jit(solution)/shard_map/ppermute | solution.py:260
  270.0 7.8 %collective-permute-done.9 = bf16[1024,256]{1,0:T(8,128)(2,1)S(1)} collective-permute-done((bf16[1024,256]{1,0:T(8,128)(2,1)S(1)}, bf16[1024,256]{1,0:T(8,128)(2,1)S(1)}, u32[]{:S(2)}, u32[]{:S(2)}) %collective-permute-start.9) | collective-permute-done | bytes 524320 | tf_op jit(solution)/shard_map/ppermute | solution.py:260
  280.2 3.9 bitcast_convert_fusion
  284.1 15.2 %shard_map.261 = f32[128,1024]{1,0:T(8,128)} custom-call(bf16[8,128,1024]{2,1,0:T(8,128)(2,1)} %bitcast.76), custom_call_target="tpu_custom_call" | custom-call | tf_op jit(solution)/shard_map/pallas_call | solution.py:175
  299.4 67.5 %psum.52 = f32[6,1024]{1,0:T(8,128)S(1)} all-reduce(f32[6,1024]{1,0:T(8,128)S(1)} %stack.44), channel_id=1, replica_groups=mesh['dp'=8,'tensor'=16] {'dp','tensor'}, use_global_device_ids=true, to_apply=%region_22.23 | all-reduce | flops 6144 | bytes 49152 | tf_op jit(solution)/shard_map/psum | solution.py:356
  374.6 18.5 %all-reduce = (f32[2,64]{1,0:T(2,128)}, f32[256]{0:T(256)}) all-reduce(f32[2,64]{1,0:T(2,128)S(1)} %slice_add_fusion.5, f32[256]{0:T(256)S(1)} %slice_add_fusion.4), channel_id=1, replica_groups=mesh['dp'=8,'tensor'=16] {'dp'}, use_global_device_ids=true, to_apply=%region_14.15 | all-reduce | flops 384 | bytes 3072 | tf_op jit(solution)/shard_map/psum | solution.py:364
  (167 shorter events, 85.9 us)
Async XLA Ops:
  7.2 34.2 %copy-start.33 = (f32[2,64]{1,0:T(2,128)S(1)}, f32[2,64]{1,0:T(2,128)}, u32[]{:S(2)}) copy-start(f32[2,64]{1,0:T(2,128)} %param.18) | copy-start | bytes 1540
  7.2 34.0 %copy-start.34 = (f32[256]{0:T(256)S(1)}, f32[256]{0:T(256)}, u32[]{:S(2)}) copy-start(f32[256]{0:T(256)} %param.24) | copy-start | bytes 3076
  7.2 385.9 %all-reduce.4.cloned.1.call-start = ((), (), s32[]{:S(2)}) async-start(), calls=%async_computation | async-start | bytes 3145728 | tf_op jit(solution)/shard_map/psum | solution.py:352
  7.3 33.9 %collective-permute-start.1 = (f32[2,64]{1,0:T(2,128)}, f32[2,64]{1,0:T(2,128)S(1)}, u32[]{:S(2)}, u32[]{:S(2)}) collective-permute-start(f32[2,64]{1,0:T(2,128)} %param.18), channel_id=1, source_target_pairs={{0,8},{1,9},{2,10},{3,11},{4,12},{5,13},{6,14},{7,15},{8,0},{9,1},... | collective-permute-start | bytes 1544 | tf_op jit(solution)/shard_map/ppermute | solution.py:260
  11.3 37.7 %collective-permute-start.2 = (bf16[64,1024]{1,0:T(8,128)(2,1)}, bf16[64,1024]{1,0:T(8,128)(2,1)S(1)}, u32[]{:S(2)}, u32[]{:S(2)}) collective-permute-start(bf16[64,1024]{1,0:T(8,128)(2,1)} %param.19), channel_id=1, source_target_pairs={{0,8},{1,9},{2,10},{3,11},{4,12},{5,13},{6,14},{7,15},{8,0},{9,1},... | collective-permute-start | bytes 393224 | tf_op jit(solution)/shard_map/ppermute | solution.py:260
  11.4 37.6 %collective-permute-start = (bf16[3,1024,64]{1,2,0:T(8,128)(2,1)}, bf16[3,1024,64]{1,2,0:T(8,128)(2,1)S(1)}, u32[]{:S(2)}, u32[]{:S(2)}) collective-permute-start(bf16[3,1024,64]{1,2,0:T(8,128)(2,1)} %param.17), channel_id=1, source_target_pairs={{0,8},{1,9},{2,10},{3,11},{4,12},{5,13},{6,14},{7,15},{8,0},{9,1},... | collective-permute-start | bytes 1179656 | tf_op jit(solution)/shard_map/ppermute | solution.py:260
  14.8 83.4 %collective-permute-start.3 = (bf16[1024,256]{1,0:T(8,128)(2,1)}, bf16[1024,256]{1,0:T(8,128)(2,1)}, u32[]{:S(2)}, u32[]{:S(2)}) collective-permute-start(bf16[1024,256]{1,0:T(8,128)(2,1)} %param.23), channel_id=1, source_target_pairs={{0,8},{1,9},{2,10},{3,11},{4,12},{5,13},{6,14},{7,15},{8,0},{9,1},... | collective-permute-start | bytes 1572872 | tf_op jit(solution)/shard_map/ppermute | solution.py:260
  14.9 89.2 %collective-permute-start.5 = (bf16[256,1024]{1,0:T(8,128)(2,1)}, bf16[256,1024]{1,0:T(8,128)(2,1)}, u32[]{:S(2)}, u32[]{:S(2)}) collective-permute-start(bf16[256,1024]{1,0:T(8,128)(2,1)} %param.25), channel_id=1, source_target_pairs={{0,8},{1,9},{2,10},{3,11},{4,12},{5,13},{6,14},{7,15},{8,0},{9,1},... | collective-permute-start | bytes 1572872 | tf_op jit(solution)/shard_map/ppermute | solution.py:260
  23.8 33.4 %copy-start.4 = (pred[1024,1024]{0,1:T(8,128)(4,1)}, pred[1024,1024]{0,1:T(8,128)(4,1)S(1)}, u32[]{:S(2)}) copy-start(pred[1024,1024]{0,1:T(8,128)(4,1)S(1)} %broadcast_compare_fusion) | copy-start | bytes 3145732
  41.2 7.8 %collective-permute-start.4 = (f32[256]{0:T(256)S(1)}, f32[256]{0:T(256)S(1)}, u32[]{:S(2)}, u32[]{:S(2)}) collective-permute-start(f32[256]{0:T(256)S(1)} %copy-done.34), channel_id=1, source_target_pairs={{0,8},{1,9},{2,10},{3,11},{4,12},{5,13},{6,14},{7,15},{8,0},{9,1},... | collective-permute-start | bytes 3080 | tf_op jit(solution)/shard_map/ppermute | solution.py:260
  60.7 37.5 %copy-start.12 = (bf16[2,64,1024]{2,1,0:T(8,128)(2,1)}, bf16[2,64,1024]{2,1,0:T(8,128)(2,1)S(1)}, u32[]{:S(2)}) copy-start(bf16[2,64,1024]{2,1,0:T(8,128)(2,1)S(1)} %convolution_convert_fusion.4) | copy-start | bytes 786436
  60.8 20.6 %copy-start.22 = (f32[1024]{0:T(1024)S(1)}, f32[1024]{0:T(1024)}, u32[]{:S(2)}) copy-start(f32[1024]{0:T(1024)} %param.21) | copy-start | bytes 12292
  60.8 20.6 %copy-start.23 = (f32[1024]{0:T(1024)S(1)}, f32[1024]{0:T(1024)}, u32[]{:S(2)}) copy-start(f32[1024]{0:T(1024)} %param.22) | copy-start | bytes 12292
  62.9 35.3 %copy-start.16 = (bf16[1024,512]{1,0:T(8,128)(2,1)S(1)}, bf16[1024,512]{1,0:T(8,128)(2,1)}, u32[]{:S(2)}) copy-start(bf16[1024,512]{1,0:T(8,128)(2,1)} %constant_dynamic-update-slice_fusion.5) | copy-start | bytes 3145732
  239.4 28.6 %collective-permute-start.11 = (bf16[256,1024]{1,0:T(8,128)(2,1)}, bf16[256,1024]{1,0:T(8,128)(2,1)}, u32[]{:S(2)}, u32[]{:S(2)}) collective-permute-start(bf16[256,1024]{1,0:T(8,128)(2,1)} %slice.135), channel_id=1, source_target_pairs={{0,8},{1,9},{2,10},{3,11},{4,12},{5,13},{6,14},{7,15},{8,0},{9,1},... | collective-permute-start | bytes 1572872 | tf_op jit(solution)/shard_map/ppermute | solution.py:260
  239.9 18.9 %collective-permute-start.8 = (bf16[64,1024]{1,0:T(8,128)(2,1)S(1)}, bf16[64,1024]{1,0:T(8,128)(2,1)}, u32[]{:S(2)}, u32[]{:S(2)}) collective-permute-start(bf16[64,1024]{1,0:T(8,128)(2,1)S(1)} %slice.139), channel_id=1, source_target_pairs={{0,8},{1,9},{2,10},{3,11},{4,12},{5,13},{6,14},{7,15},{8,0},{9,1},... | collective-permute-start | bytes 393224 | tf_op jit(solution)/shard_map/ppermute | solution.py:260
  250.8 16.4 %collective-permute-start.6 = (bf16[3,1024,64]{1,2,0:T(8,128)(2,1)S(1)}, bf16[3,1024,64]{1,2,0:T(8,128)(2,1)S(1)}, u32[]{:S(2)}, u32[]{:S(2)}) collective-permute-start(bf16[3,1024,64]{1,2,0:T(8,128)(2,1)S(1)} %slice.137), channel_id=1, source_target_pairs={{0,8},{1,9},{2,10},{3,11},{4,12},{5,13},{6,14},{7,15},{8,0},{9,1},... | collective-permute-start | bytes 1179656 | tf_op jit(solution)/shard_map/ppermute | solution.py:260
  252.7 25.2 %collective-permute-start.9 = (bf16[1024,256]{1,0:T(8,128)(2,1)S(1)}, bf16[1024,256]{1,0:T(8,128)(2,1)S(1)}, u32[]{:S(2)}, u32[]{:S(2)}) collective-permute-start(bf16[1024,256]{1,0:T(8,128)(2,1)S(1)} %slice.136), channel_id=1, source_target_pairs={{0,8},{1,9},{2,10},{3,11},{4,12},{5,13},{6,14},{7,15},{8,0},{9,1},... | collective-permute-start | bytes 1572872 | tf_op jit(solution)/shard_map/ppermute | solution.py:260
  278.8 20.5 %copy-start.27 = (f32[1024]{0:T(1024)S(1)}, f32[1024]{0:T(1024)}, u32[]{:S(2)}) copy-start(f32[1024]{0:T(1024)} %get-tuple-element.19) | copy-start | bytes 12292
  278.8 20.6 %copy-start.28 = (f32[1024]{0:T(1024)S(1)}, f32[1024]{0:T(1024)}, u32[]{:S(2)}) copy-start(f32[1024]{0:T(1024)} %get-tuple-element.32) | copy-start | bytes 12292
  279.8 89.6 %copy-start.32 = (f32[512]{0:T(512)S(1)}, f32[512]{0:T(512)}, u32[]{:S(2)}) copy-start(f32[512]{0:T(512)} %get-tuple-element.58) | copy-start | bytes 6148
  279.8 91.8 %collective-permute-start.7 = (f32[2,64]{1,0:T(2,128)S(1)}, f32[2,64]{1,0:T(2,128)S(1)}, u32[]{:S(2)}, u32[]{:S(2)}) collective-permute-start(f32[2,64]{1,0:T(2,128)S(1)} %slice.82), channel_id=1, source_target_pairs={{0,8},{1,9},{2,10},{3,11},{4,12},{5,13},{6,14},{7,15},{8,0},{9,1},... | collective-permute-start | bytes 1544 | tf_op jit(solution)/shard_map/ppermute | solution.py:260
  284.1 116.8 %copy-start.1 = (s32[2,1024]{1,0:T(2,128)S(1)}, s32[2,1024]{1,0:T(2,128)}, u32[]{:S(2)}) copy-start(s32[2,1024]{1,0:T(2,128)} %param.16) | copy-start | bytes 24580
  369.4 5.2 %collective-permute-start.10 = (f32[256]{0:T(256)S(1)}, f32[256]{0:T(256)S(1)}, u32[]{:S(2)}, u32[]{:S(2)}) collective-permute-start(f32[256]{0:T(256)S(1)} %slice.91), channel_id=1, source_target_pairs={{0,8},{1,9},{2,10},{3,11},{4,12},{5,13},{6,14},{7,15},{8,0},{9,1},... | collective-permute-start | bytes 3080 | tf_op jit(solution)/shard_map/ppermute | solution.py:260
  (26 other events, 243.3 us)
Sparse Core Ops, SparseCore 0:
  279.0 77.9 all-reduce.3

commit v2 on v0

v2 whole, which is shorter than its diff:
```python
import functools

import jax
import jax.numpy as jnp
from jax import lax
from jax.experimental import pallas as pl
from jax.experimental.pallas import tpu as pltpu
from jax.sharding import PartitionSpec as P

HEAD_DIM = 64
RING = 8
BLOCK = 128
HALF = 64
CHIP = 2 * BLOCK
PIECES = 8
MESH = pl.DeviceIdType.MESH
VMEM_WHOLE = pl.BlockSpec(memory_space=pltpu.VMEM)
VMEM_BYTES = 60 * 1024 * 1024
half = jnp.bfloat16
wide = jnp.float32


EPS = 1e-12
MASKED = -1e30
ROOT_HALF = 0.7071067811865476
INV_ROOT_TAU = 0.3989422804014327


def ring_place():
    t = lax.axis_index("tensor")
    dp = lax.axis_index("dp")
    base = (t // RING) * RING
    j = t % RING
    x = j // 2
    c = j % 2

    def block_of(step, other=False):
        xx = lax.rem(x + step + 4, 4)
        return xx * 2 + ((1 - c) if other else c)

    def device_of(step, other=False):
        return (dp, base + block_of(step, other))

    return block_of, device_of


def ring_order(s):
    return s + s // 2 - 2 * (s // 3)


def greet(devices):
    barrier = pltpu.get_barrier_semaphore()
    for device in devices:
        pl.semaphore_signal(barrier, inc=1, device_id=device, device_id_type=MESH)
    pl.semaphore_wait(barrier, len(devices))


def greet_ring():
    _, device_of = ring_place()
    greet((device_of(1), device_of(-1), device_of(0, True)))


def remote(src, dst, send, recv, slot, device):
    return pltpu.make_async_remote_copy(
        src_ref=src,
        dst_ref=dst,
        send_sem=send.at[slot],
        recv_sem=recv.at[slot],
        device_id=device,
        device_id_type=MESH,
    )


FIRST = pl.ds(0, HALF)
SECOND = pl.ds(HALF, HALF)


class Gather:
    slots = 13

    def __init__(self, src, out, send, recv):
        self.src, self.out, self.send, self.recv = src, out, send, recv
        self.block_of, self.device_of = ring_place()
        self.partner = self.device_of(0, True)

    def copy(self, place, slot, device):
        return remote(place, place, self.send, self.recv, slot, device)

    def start(self):
        src, at = self.src, self.out.at
        mine, right, left = self.block_of(0), self.device_of(1), self.device_of(-1)
        for part, slot, device in ((FIRST, 0, right), (SECOND, 3, left), (SECOND, 1, right), (FIRST, 2, left)):
            remote(src.at[part], at[mine, part], self.send, self.recv, slot, device).start()
        remote(src, at[mine], self.send, self.recv, 6, self.partner).start()
        self.out[pl.ds(mine, 1)] = src[...].reshape(1, *src.shape)

    def pass_on(self, slot, step, part, share_slot, device=None, device_slot=None):
        place = self.out.at[self.block_of(step), part]
        self.copy(place, slot, self.partner).wait_recv()
        if device is not None:
            self.copy(place, device_slot, device).start()
        self.copy(place, share_slot, self.partner).start()

    def shared(self, step, slots):
        for slot, part in zip(slots, (FIRST, SECOND)):
            self.copy(self.out.at[self.block_of(step, True), part], slot, self.partner).wait_recv()

    def ready(self, s):
        @pl.when(s == 0)
        def _():
            self.copy(self.out.at[self.block_of(0, True)], 6, self.partner).wait_recv()

        @pl.when(s == 1)
        def _():
            self.pass_on(0, -1, FIRST, 7, self.device_of(1), 4)
            self.pass_on(3, 1, SECOND, 10, self.device_of(-1), 5)
            self.pass_on(2, 1, FIRST, 9)
            self.pass_on(1, -1, SECOND, 8)
            self.shared(1, (9, 10))

        @pl.when(s == 2)
        def _():
            self.shared(-1, (7, 8))

        @pl.when(s == 3)
        def _():
            self.pass_on(4, 2, FIRST, 11)
            self.pass_on(5, 2, SECOND, 12)
            self.shared(2, (11, 12))

    def finish(self):
        half_place = self.out.at[0, FIRST]
        for slot in range(13):
            self.copy(self.out.at[0] if slot == 6 else half_place, slot, self.partner).wait_send()


class Scatter:
    slots = 10

    @staticmethod
    def scratch(width):
        return [
            pltpu.VMEM((RING, BLOCK, width), half),
            pltpu.VMEM((4, BLOCK, width), half),
            pltpu.VMEM((6, HALF, width), half),
            pltpu.VMEM((2, HALF, width), half),
            pltpu.VMEM((2, 2, HALF, width), half),
            pltpu.SemaphoreType.DMA((10,)),
            pltpu.SemaphoreType.DMA((10,)),
        ]

    def __init__(self, y, pair, stage, transit, final, send, recv):
        self.y, self.pair, self.stage, self.transit, self.final = y, pair, stage, transit, final
        self.send, self.recv = send, recv
        self.block_of, self.device_of = ring_place()
        self.partner = self.device_of(0, True)

    def computed(self, k):
        remote(self.y.at[self.block_of(k, True)], self.pair.at[k], self.send, self.recv, k, self.partner).start()

    def arrived(self, place, slot):
        remote(place, place, self.send, self.recv, slot, self.partner).wait_recv()

    def chip_sum(self, k, part):
        return self.y[self.block_of(k), part].astype(wide) + self.pair[k, part].astype(wide)

    def forward(self, at, value, place, slot, device):
        self.stage[at] = value.astype(half)
        remote(self.stage.at[at], place, self.send, self.recv, slot, device).start()

    def sides(self):
        self.arrived(self.pair.at[1], 1)
        self.forward(2, self.chip_sum(1, SECOND), self.final.at[0, 1], 6, self.device_of(1))
        self.arrived(self.pair.at[3], 3)
        self.forward(3, self.chip_sum(3, FIRST), self.final.at[1, 0], 7, self.device_of(-1))

    def across(self):
        self.arrived(self.pair.at[2], 2)
        self.forward(0, self.chip_sum(2, FIRST), self.transit.at[0], 4, self.device_of(1))
        self.forward(1, self.chip_sum(2, SECOND), self.transit.at[1], 5, self.device_of(-1))

    def through(self):
        self.arrived(self.transit.at[0], 4)
        value = self.chip_sum(1, FIRST) + self.transit[0].astype(wide)
        self.forward(4, value, self.final.at[0, 0], 8, self.device_of(1))
        self.arrived(self.transit.at[1], 5)
        value = self.chip_sum(3, SECOND) + self.transit[1].astype(wide)
        self.forward(5, value, self.final.at[1, 1], 9, self.device_of(-1))

    def result(self):
        self.arrived(self.pair.at[0], 0)
        for slot, place in ((6, (0, 1)), (7, (1, 0)), (8, (0, 0)), (9, (1, 1))):
            self.arrived(self.final.at[place], slot)
        final = self.final
        rows = [
            self.chip_sum(0, part) + final[0, h].astype(wide) + final[1, h].astype(wide)
            for h, part in enumerate((FIRST, SECOND))
        ]
        return jnp.concatenate(rows, axis=0)

    def finish(self):
        for slot in range(10):
            place = self.pair.at[0] if slot < 4 else self.transit.at[0]
            remote(place, place, self.send, self.recv, slot, self.partner).wait_send()


def dot_nn(left, right):
    return lax.dot_general(left, right, (((1,), (0,)), ((), ())), preferred_element_type=wide)


def dot_nt(left, right):
    return lax.dot_general(left, right, (((1,), (1,)), ((), ())), preferred_element_type=wide)


def dot_tn(left, right):
    return lax.dot_general(left, right, (((0,), (0,)), ((), ())), preferred_element_type=wide)


def layer_norm(rows, gain, shift):
    center = rows - jnp.mean(rows, axis=-1, keepdims=True)
    inverse = lax.rsqrt(jnp.mean(center * center, axis=-1, keepdims=True) + EPS)
    normed = center * inverse
    return (normed * gain + shift, normed, inverse)


def norm_back(grad, normed, inverse, gain):
    scaled = grad * gain
    return inverse * (
        scaled
        - jnp.mean(scaled, axis=-1, keepdims=True)
        - normed * jnp.mean(scaled * normed, axis=-1, keepdims=True)
    )


def gelu_parts(pre):
    cumul = 0.5 * (1.0 + lax.erf(pre * ROOT_HALF))
    return (pre * cumul, cumul + pre * jnp.exp(-0.5 * pre * pre) * INV_ROOT_TAU)


def column_sum(rows):
    return jnp.sum(rows, axis=0, keepdims=True)


def chip_rows(ref, chip):
    block = ref[pl.ds(2 * chip, 2)]
    return block.reshape(CHIP, block.shape[2])


def all_rows(ref):
    block = ref[...]
    return block.reshape(RING * BLOCK, block.shape[2])


def feed_forward_kernel(
    attended, block_input, out_bias, gain1, bias1, up, up_bias, down, down_bias, gain2, bias2, cot,
    out, d_first, d_first_half, g_up, g_down, g_up_bias, vecs,
    hidden_half, hidden_all, act, slope, d_second_half, d_second_all, d_pre, gather_sems, *scatter_scratch,
):
    block_of, _ = ring_place()
    greet_ring()
    first = block_input[...].astype(wide) + attended[...] + out_bias[...]
    hidden, normed_one, inverse_one = layer_norm(first, gain1[...], bias1[...])
    hidden_half[...] = hidden.astype(half)
    gather = Gather(hidden_half, hidden_all, gather_sems.at[0], gather_sems.at[1])
    scatter = Scatter(*scatter_scratch[:7])
    gather.start()

    @pl.loop(0, 4)
    def _(s):
        gather.ready(s)
        k = ring_order(s)
        chip = block_of(k) // 2
        rows = pl.ds(chip * CHIP, CHIP)
        pre = dot_nn(chip_rows(hidden_all, chip), up[...]) + up_bias[...]
        value, gelu_slope = gelu_parts(pre)
        value = value.astype(half)
        act[rows] = value
        slope[rows] = gelu_slope
        term = dot_nn(value, down[...]).astype(half)
        scatter.y[pl.ds(2 * chip, 2)] = term.reshape(2, BLOCK, term.shape[1])
        scatter.computed(k)

    scatter.sides()
    scatter.across()
    gather.finish()
    scatter.through()
    second = hidden + scatter.result() + down_bias[...]
    scatter.finish()
    output, normed_two, inverse_two = layer_norm(second, gain2[...], bias2[...])
    out[...] = output.astype(half)
    grad = cot[...].astype(wide)
    d_second = norm_back(grad, normed_two, inverse_two, gain2[...])
    d_second_half[...] = d_second.astype(half)
    gather = Gather(d_second_half, d_second_all, gather_sems.at[2], gather_sems.at[3])
    scatter = Scatter(*scatter_scratch[7:])
    gather.start()
    vecs[pl.ds(3, 1)] = column_sum(d_second)
    vecs[pl.ds(4, 1)] = column_sum(grad * normed_two)
    vecs[pl.ds(5, 1)] = column_sum(grad)
    vecs[pl.ds(6, 2)] = jnp.zeros((2, grad.shape[1]), wide)
    g_up_bias[...] = jnp.zeros_like(g_up_bias)

    @pl.loop(0, 4)
    def _(s):
        gather.ready(s)
        k = ring_order(s)
        chip = block_of(k) // 2
        rows = pl.ds(chip * CHIP, CHIP)
        grad_pre = dot_nt(chip_rows(d_second_all, chip), down[...]) * slope[rows]
        g_up_bias[...] += column_sum(grad_pre)
        grad_pre = grad_pre.astype(half)
        d_pre[rows] = grad_pre
        term = dot_nt(grad_pre, up[...]).astype(half)
        scatter.y[pl.ds(2 * chip, 2)] = term.reshape(2, BLOCK, term.shape[1])
        scatter.computed(k)

    scatter.sides()
    scatter.across()
    gather.finish()
    shard = up.shape[1] // 2
    for a in range(2):
        columns = pl.ds(a * shard, shard)
        g_down[a] = dot_tn(act[:, columns], all_rows(d_second_all)).astype(half)
    scatter.through()

    @pl.loop(0, 4)
    def _(i):
        columns = pl.ds(pl.multiple_of(i * 256, 256), 256)
        left = hidden_all[:, :, columns].reshape(RING * BLOCK, 256)
        part = dot_tn(left, d_pre[...]).astype(half)
        for a in range(2):
            g_up[a, columns] = part[:, a * shard : (a + 1) * shard]

    d_hidden = d_second + scatter.result()
    scatter.finish()
    grad_first = norm_back(d_hidden, normed_one, inverse_one, gain1[...])
    d_first[...] = grad_first
    d_first_half[...] = grad_first.astype(half)
    vecs[pl.ds(0, 1)] = column_sum(grad_first)
    vecs[pl.ds(1, 1)] = column_sum(d_hidden * normed_one)
    vecs[pl.ds(2, 1)] = column_sum(d_hidden)


def feed_forward(attended, block_input, out_bias, gain1, bias1, up, up_bias, down, down_bias, gain2, bias2, cot):
    rows, width = attended.shape
    hidden = up.shape[1]
    shard = hidden // 2
    return pl.pallas_call(
        feed_forward_kernel,
        out_shape=(
            jax.ShapeDtypeStruct((rows, width), half),
            jax.ShapeDtypeStruct((rows, width), wide),
            jax.ShapeDtypeStruct((rows, width), half),
            jax.ShapeDtypeStruct((2, width, shard), half),
            jax.ShapeDtypeStruct((2, shard, width), half),
            jax.ShapeDtypeStruct((1, hidden), wide),
            jax.ShapeDtypeStruct((8, width), wide),
        ),
        in_specs=[VMEM_WHOLE] * 12,
        out_specs=(VMEM_WHOLE,) * 7,
        scratch_shapes=[
            pltpu.VMEM((rows, width), half),
            pltpu.VMEM((RING, rows, width), half),
            pltpu.VMEM((RING * rows, hidden), half),
            pltpu.VMEM((RING * rows, hidden), wide),
            pltpu.VMEM((rows, width), half),
            pltpu.VMEM((RING, rows, width), half),
            pltpu.VMEM((RING * rows, hidden), half),
            pltpu.SemaphoreType.DMA((4, Gather.slots)),
        ]
        + Scatter.scratch(width)
        + Scatter.scratch(width),
        compiler_params=pltpu.CompilerParams(
            collective_id=2, has_side_effects=True, vmem_limit_bytes=VMEM_BYTES
        ),
    )(attended, block_input, out_bias, gain1, bias1, up, up_bias, down, down_bias, gain2, bias2, cot)


def gather_kernel(x_ref, o_ref, send, recv):
    greet_ring()
    gather = Gather(x_ref, o_ref, send, recv)
    gather.start()
    for s in range(4):
        gather.ready(s)
    gather.finish()


def gather_rows(x):
    rows, width = x.shape
    out = pl.pallas_call(
        gather_kernel,
        out_shape=jax.ShapeDtypeStruct((RING, rows, width), x.dtype),
        in_specs=[VMEM_WHOLE],
        out_specs=VMEM_WHOLE,
        scratch_shapes=[pltpu.SemaphoreType.DMA((13,)), pltpu.SemaphoreType.DMA((13,))],
        compiler_params=pltpu.CompilerParams(collective_id=0, has_side_effects=True),
    )(x)
    return out.reshape(RING * rows, width)


def scatter_kernel(y_ref, o_ref, y, *scratch):
    greet_ring()
    scatter = Scatter(y_ref, *scratch)
    for k in (1, 3, 2, 0):
        scatter.computed(k)
    scatter.sides()
    scatter.across()
    scatter.through()
    o_ref[...] = scatter.result()
    scatter.finish()


def scatter_rows(y):
    tokens, width = y.shape
    rows = tokens // RING
    return pl.pallas_call(
        scatter_kernel,
        out_shape=jax.ShapeDtypeStruct((rows, width), wide),
        in_specs=[VMEM_WHOLE],
        out_specs=VMEM_WHOLE,
        scratch_shapes=Scatter.scratch(width),
        compiler_params=pltpu.CompilerParams(collective_id=1, has_side_effects=True),
    )(y.reshape(RING, rows, width))


class PlaneSum:
    def __init__(self, land, full, send, recv):
        self.land, self.full, self.send, self.recv = land, full, send, recv
        t, dp = lax.axis_index("tensor"), lax.axis_index("dp")
        self.t, self.dp = t, dp

    @staticmethod
    def peer(a, r):
        t, dp = lax.axis_index("tensor"), lax.axis_index("dp")
        other = lax.rem(dp // 4 + r // 4, 2) * 4 + lax.rem(dp + r, 4)
        return other, (other, lax.rem(t + a * RING, 2 * RING))

    @staticmethod
    def peers():
        return [PlaneSum.peer(n // PIECES, n % PIECES)[1] for n in range(1, 2 * PIECES)]

    def scatter(self, grads):
        for n in range(1, 2 * PIECES):
            piece, device = self.peer(n // PIECES, n % PIECES)
            remote(grads.at[n // PIECES, piece], self.land.at[n - 1], self.send, self.recv, n - 1, device).start()

    def share(self, grads):
        total = grads[0, self.dp].astype(wide)
        for n in range(15):
            place = self.land.at[n]
            remote(place, place, self.send, self.recv, n, (self.dp, self.t)).wait_recv()
            total += self.land[n].astype(wide)
        self.full[pl.ds(self.dp, 1)] = total.astype(half).reshape(1, *total.shape)
        for r in range(1, PIECES):
            place = self.full.at[self.dp]
            remote(place, place, self.send, self.recv, 14 + r, self.peer(0, r)[1]).start()

    def result(self, out):
        for r in range(1, PIECES):
            piece = lax.rem(self.dp // 4 + r // 4, 2) * 4 + lax.rem(self.dp + 8 - r, 4)
            place = self.full.at[piece]
            remote(place, place, self.send, self.recv, 14 + r, (self.dp, self.t)).wait_recv()
        out[...] = self.full[...].astype(wide)
        for n in range(22):
            place = self.land.at[0]
            remote(place, place, self.send, self.recv, n, (self.dp, self.t)).wait_send()

    @staticmethod
    def scratch(rows, width):
        return [
            pltpu.VMEM((15, rows, width), half),
            pltpu.VMEM((PIECES, rows, width), half),
            pltpu.SemaphoreType.DMA((22,)),
            pltpu.SemaphoreType.DMA((22,)),
        ]


class SmallSum:
    scratch = [
        pltpu.VMEM((8, 8, 1024), wide),
        pltpu.VMEM((2, 8, 1024), wide),
        pltpu.VMEM((15, 8, 1024), wide),
        pltpu.SemaphoreType.DMA((22,)),
        pltpu.SemaphoreType.DMA((22,)),
    ]

    def __init__(self, line, base, land, send, recv):
        self.line, self.base, self.land, self.send, self.recv = line, base, land, send, recv
        self.t, self.dp = lax.axis_index("tensor"), lax.axis_index("dp")

    @staticmethod
    def line_peer(r):
        t, dp = lax.axis_index("tensor"), lax.axis_index("dp")
        return (dp, (t // RING) * RING + lax.rem(t + r, RING))

    @staticmethod
    def peers():
        return [SmallSum.line_peer(r) for r in range(1, RING)]

    def start(self, vecs):
        for r in range(1, RING):
            remote(vecs, self.line.at[r], self.send, self.recv, 14 + r, self.line_peer(r)).start()

    def plane(self, vecs, shards):
        total = vecs[...]
        for r in range(1, RING):
            place = self.line.at[r]
            remote(place, place, self.send, self.recv, 14 + r, (self.dp, self.t)).wait_recv()
            total += self.line[r]
        row = lax.broadcasted_iota(jnp.int32, total.shape, 0)
        for a in range(2):
            self.base[a] = jnp.where(row == 6, jnp.broadcast_to(shards[pl.ds(a, 1)], total.shape), total)
        for n in range(1, 2 * PIECES):
            _, device = PlaneSum.peer(n // PIECES, n % PIECES)
            remote(self.base.at[n // PIECES], self.land.at[n - 1], self.send, self.recv, n - 1, device).start()

    def result(self):
        total = self.base[0]
        for n in range(15):
            place = self.land.at[n]
            remote(place, place, self.send, self.recv, n, (self.dp, self.t)).wait_recv()
            total += self.land[n]
        for n in range(22):
            place = self.land.at[0]
            remote(place, place, self.send, self.recv, n, (self.dp, self.t)).wait_send()
        return total


def reduce_kernel(count, *refs):
    grads, rest = refs[:count], refs[count:]
    vecs, shards, rest = rest[0], rest[1], rest[2:]
    outs, rest = rest[:count], rest[count:]
    small_out, rest = rest[0], rest[1:]
    small = SmallSum(*rest[:5])
    planes = [PlaneSum(*rest[5 + 4 * i : 9 + 4 * i]) for i in range(count)]
    greet(PlaneSum.peers() + SmallSum.peers())
    small.start(vecs)
    for plane, grad in zip(planes, grads):
        plane.scatter(grad)
    small.plane(vecs, shards)
    for plane, grad in zip(planes, grads):
        plane.share(grad)
    for plane, out in zip(planes, outs):
        plane.result(out)
    small_out[...] = small.result()


def reduce_all(grads, vecs, shards):
    scratch = list(SmallSum.scratch)
    for grad in grads:
        scratch += PlaneSum.scratch(*grad.shape[2:])
    return pl.pallas_call(
        functools.partial(reduce_kernel, len(grads)),
        out_shape=tuple(jax.ShapeDtypeStruct(grad.shape[1:], wide) for grad in grads)
        + (jax.ShapeDtypeStruct((8, 1024), wide),),
        in_specs=[VMEM_WHOLE] * (len(grads) + 2),
        out_specs=(VMEM_WHOLE,) * (len(grads) + 1),
        scratch_shapes=scratch,
        compiler_params=pltpu.CompilerParams(
            collective_id=3, has_side_effects=True, vmem_limit_bytes=VMEM_BYTES
        ),
    )(*grads, vecs, shards)


def masked_scores(queries, keys, segs):
    scores = jnp.einsum("qhd,khd->hqk", queries, keys, preferred_element_type=wide) * HEAD_DIM ** (-0.5)
    allowed = segs[:, None] == segs[None, :]
    return jnp.where(allowed[None], scores, MASKED)


def forward_seq(items):
    queries, keys, values, segs = items
    masked = masked_scores(queries, keys, segs)
    top = jnp.max(masked, axis=-1, keepdims=True)
    lse = top + jnp.log(jnp.sum(jnp.exp(masked - top), axis=-1, keepdims=True))
    probs = jnp.exp(masked - lse).astype(half)
    context = jnp.einsum("hqk,khd->qhd", probs, values, preferred_element_type=wide)
    return (context.astype(half), lse)


def backward_seq(items):
    queries, keys, values, segs, lse, d_context = items
    masked = masked_scores(queries, keys, segs)
    probs = jnp.exp(masked - lse)
    probs_half = probs.astype(half)
    d_values = jnp.einsum("hqk,qhd->khd", probs_half, d_context, preferred_element_type=wide)
    d_probs = jnp.einsum("qhd,khd->hqk", d_context, values, preferred_element_type=wide)
    d_scores = (
        probs * (d_probs - jnp.sum(probs * d_probs, axis=-1, keepdims=True)) * HEAD_DIM ** (-0.5)
    )
    d_scores = d_scores.astype(half)
    d_queries = jnp.einsum("hqk,khd->qhd", d_scores, keys, preferred_element_type=wide)
    d_keys = jnp.einsum("hqk,qhd->khd", d_scores, queries, preferred_element_type=wide)
    return (d_queries, d_keys, d_values)


def trade(arr):
    return lax.ppermute(arr, "tensor", [(t, (t + RING) % (2 * RING)) for t in range(2 * RING)])


def row(vector):
    return vector.reshape(1, vector.shape[0])


def per_device(
    block_input,
    segment_ids,
    qkv_weight,
    qv_bias,
    out_weight,
    out_bias,
    norm1_gain,
    norm1_bias,
    up_weight,
    up_bias,
    down_weight,
    down_bias,
    norm2_gain,
    norm2_bias,
    cotangent,
):
    my_seq = lax.axis_index("tensor") // RING
    segs = lax.dynamic_index_in_dim(segment_ids, my_seq, 0, keepdims=False)
    seq_len = segs.shape[0]
    qkv_rows = jnp.swapaxes(qkv_weight, 1, 2)
    qkv_two = jnp.concatenate([qkv_rows, trade(qkv_rows)], axis=1)
    qv_bias_two = jnp.concatenate([qv_bias, trade(qv_bias)], axis=1)
    out_two = jnp.concatenate([out_weight, trade(out_weight)], axis=0)
    up_two = jnp.concatenate([up_weight, trade(up_weight)], axis=1)
    up_bias_two = jnp.concatenate([up_bias, trade(up_bias)], axis=0)
    down_two = jnp.concatenate([down_weight, trade(down_weight)], axis=0)

    gathered = gather_rows(block_input)
    projected = jnp.einsum("td,cwd->ctw", gathered, qkv_two, preferred_element_type=wide)
    queries = (projected[0] + qv_bias_two[0]).astype(half)
    keys = projected[1].astype(half)
    values = (projected[2] + qv_bias_two[1]).astype(half)
    width = queries.shape[1]

    def by_head(arr):
        return arr.reshape(seq_len, width // HEAD_DIM, HEAD_DIM)

    context, lse = forward_seq((by_head(queries), by_head(keys), by_head(values), segs))
    context = context.reshape(seq_len, width)
    attended = scatter_rows(jnp.dot(context, out_two, preferred_element_type=wide).astype(half))

    output, d_first, d_first_half, g_up, g_down, g_up_bias, vecs = feed_forward(
        attended, block_input, row(out_bias), row(norm1_gain), row(norm1_bias), up_two, row(up_bias_two),
        down_two, row(down_bias), row(norm2_gain), row(norm2_bias), cotangent,
    )

    d_first_all = gather_rows(d_first_half)
    g_out = jnp.einsum("tw,td->wd", context, d_first_all, preferred_element_type=wide)
    d_context = jnp.einsum("td,wd->tw", d_first_all, out_two, preferred_element_type=wide).astype(half)
    d_queries, d_keys, d_values = (
        arr.reshape(seq_len, width)
        for arr in backward_seq(
            (by_head(queries), by_head(keys), by_head(values), segs, lse, by_head(d_context))
        )
    )
    g_qv_bias = jnp.concatenate(
        [arr.reshape(2, HEAD_DIM) for arr in (jnp.sum(d_queries, axis=0), jnp.sum(d_values, axis=0))], axis=1
    )
    d_qkv = jnp.stack([d_queries, d_keys, d_values]).astype(half)
    g_qkv = jnp.einsum("ctw,td->cwd", d_qkv, gathered, preferred_element_type=wide)
    d_rows = jnp.einsum("ctw,cwd->td", d_qkv, qkv_two, preferred_element_type=wide)
    input_grad = (d_first + scatter_rows(d_rows.astype(half))).astype(half)

    pieces = g_up.reshape(2, PIECES, g_up.shape[1] // PIECES, g_up.shape[2])
    down_pieces = g_down.reshape(2, PIECES, g_down.shape[1] // PIECES, g_down.shape[2])
    g_qkv = g_qkv.astype(half).reshape(3, 2, HEAD_DIM, -1)
    g_out = g_out.astype(half).reshape(1, 2, HEAD_DIM, -1)
    late = jnp.swapaxes(jnp.concatenate([g_qkv, g_out], axis=0), 0, 1)
    late = late.reshape(2, PIECES, 4 * HEAD_DIM // PIECES, -1)
    shards = jnp.concatenate(
        [g_up_bias.reshape(2, -1), g_qv_bias, jnp.zeros((2, 1024 - g_up_bias.shape[1] // 2 - 2 * HEAD_DIM), wide)],
        axis=1,
    )
    up_sum, down_sum, late_sum, small = reduce_all((pieces, down_pieces, late), vecs, shards)
    ff = up_bias.shape[0]
    late_sum = late_sum.reshape(4, HEAD_DIM, -1)
    return (
        output,
        input_grad,
        jnp.swapaxes(late_sum[:3], 1, 2),
        small[6, ff : ff + 2 * HEAD_DIM].reshape(2, HEAD_DIM),
        late_sum[3],
        small[0],
        small[1],
        small[2],
        up_sum.reshape(up_weight.shape),
        small[6, :ff],
        down_sum.reshape(down_weight.shape),
        small[3],
        small[4],
        small[5],
    )


def solution(mesh):
    placed = (
        P(("dp", "tensor"), None),
        P("dp", None),
        P(None, None, "tensor"),
        P(None, "tensor"),
        P("tensor", None),
        P(),
        P(),
        P(),
        P(None, "tensor"),
        P("tensor"),
        P("tensor", None),
        P(),
        P(),
        P(),
        P(("dp", "tensor"), None),
    )
    return jax.shard_map(
        per_device,
        mesh=mesh,
        in_specs=placed,
        out_specs=(
            P(("dp", "tensor"), None),
            P(("dp", "tensor"), None),
            P(None, None, "tensor"),
            P(None, "tensor"),
            P("tensor", None),
            P(),
            P(),
            P(),
            P(None, "tensor"),
            P("tensor"),
            P("tensor", None),
            P(),
            P(),
            P(),
        ),
        check_vma=False,
    )
```

time: 736 us -> 306 us (0.42)
  waiting for transfers between devices: 543 us -> 0.02 us
  Pallas kernels: 0 us -> 203 us
  blocking collectives: 84.6 us -> 0 us
  other arithmetic: 29.4 us -> 13.2 us
  between operations: 14.4 us -> 1.03 us
  starting transfers between devices: 0.77 us -> 11.5 us
  local copies, waits for them, and re-layouts: 5.85 us -> 16.1 us
    reduce_scatter x4 -> x0, waiting for transfers between devices: 326 us -> none  [the longest x1 101 us: per_device(): lax.psum_scatter(contract_cols(piece, up_weight), 'tensor', scatter_dimen...]
    all_gather x4 -> x0, waiting for transfers between devices: 216 us -> none  [the longest x1 60.3 us: per_device(): gathered = lax.all_gather(block_input, 'tensor', axis=0, tiled=True)]
    pallas_call x0 -> x6, Pallas kernels: none -> 203 us  [the longest x1 75.4 us: reduce_all(): pl.pallas_call(functools.partial(reduce_kernel, len(grads)), out_shape=tu...]
    psum x2 -> x0, blocking collectives: 84.6 us -> none  [the longest x1 66.9 us: per_device(): lax.psum((g_out_bias, g_gain_one, g_bias_one, g_down_bias, g_gain_two, g_...]
    convert_element_type x14 -> x1, other arithmetic: 16.6 us -> 1.84 us  [per_device(): input_grad = (d_first + scatter_rows(d_rows.astype(half))).astype(half)]
    ppermute x0 -> x6, starting transfers between devices: none -> 11.5 us  [trade(): lax.ppermute(arr, 'tensor', [(t, (t + RING) % (2 * RING)) for t in range(...]
    reduce_sum x9 -> x0, other arithmetic: 10.7 us -> none  [the longest x1 2.5 us: per_device(): g_down_bias = jnp.sum(d_second, axis=0)]
    concatenate x0 -> x6, other arithmetic: none -> 8 us  [the longest x1 2.15 us: per_device(): down_two = jnp.concatenate([down_weight, trade(down_weight)], axis=0)]
  transfers between devices with their start and end apart: 9 -> 6, of which waited for: 8 -> 0; matrix products, arithmetic and copies ran while one was open for 3% -> 6% of each run, Pallas kernels for 0% -> 11%
where the time goes in v2:
time: 306 us; the launch traced here: 304 us
  Pallas kernels  203 us (66%)
  matrix products  59.2 us (19%)
  local copies, waits for them, and re-layouts  16.1 us (5%)
  other arithmetic  13.2 us (4%)
  starting transfers between devices  11.5 us (4%)
    pallas_call x1, Pallas kernels, reduce_all(): pl.pallas_call(functools.partial(reduce_kernel, len(grads)), out_shape=tu...  75.4 us
    pallas_call x1, Pallas kernels, feed_forward(): pl.pallas_call(feed_forward_kernel, out_shape=(jax.ShapeDtypeStruct((rows...  59.7 us
    pallas_call x2, Pallas kernels, scatter_rows(): pl.pallas_call(scatter_kernel, out_shape=jax.ShapeDtypeStruct((rows, widt...  35.8 us
    pallas_call x2, Pallas kernels, gather_rows(): pl.pallas_call(gather_kernel, out_shape=jax.ShapeDtypeStruct((RING, rows,...  32.1 us
    dot_general x1, matrix products, backward_seq(): jnp.einsum('hqk,khd->qhd', d_scores, keys, preferred_element_type=wide)  14.6 us
    dot_general x1, matrix products, backward_seq(): jnp.einsum('hqk,qhd->khd', d_scores, queries, preferred_element_type=wide)  14.5 us
    ppermute x6, starting transfers between devices, trade(): lax.ppermute(arr, 'tensor', [(t, (t + RING) % (2 * RING)) for t in range(...  11.5 us
    dot_general x1, matrix products, backward_seq(): jnp.einsum('hqk,qhd->khd', probs_half, d_context, preferred_element_type=...  6.6 us
  transfers between devices with their start and end apart: 6, of which 0 were waited for; matrix products, arithmetic and copies ran while one was open for 6% of the time, Pallas kernels for 11%

profile of v2, /device:TPU:0, one launch (start us, length us, event | category | flops | bytes accessed | tf_op | source)
XLA Modules:
  0.0 304.1 jit_solution(3826942850336788586)
XLA Ops:
  0.7 4.0 %collective-permute-start.1 = (f32[2,64]{1,0:T(2,128)}, f32[2,64]{1,0:T(2,128)S(1)}, u32[]{:S(2)}, u32[]{:S(2)}) collective-permute-start(f32[2,64]{1,0:T(2,128)} %param.18), channel_id=1, source_target_pairs={{0,8},{1,9},{2,10},{3,11},{4,12},{5,13},{6,14},{7,15},{8,0},{9,1},... | collective-permute-start | bytes 1544 | tf_op jit(solution)/shard_map/ppermute | solution.py:598
  4.8 3.4 %collective-permute-start.2 = (bf16[64,1024]{1,0:T(8,128)(2,1)}, bf16[64,1024]{1,0:T(8,128)(2,1)S(1)}, u32[]{:S(2)}, u32[]{:S(2)}) collective-permute-start(bf16[64,1024]{1,0:T(8,128)(2,1)} %param.19), channel_id=1, source_target_pairs={{0,8},{1,9},{2,10},{3,11},{4,12},{5,13},{6,14},{7,15},{8,0},{9,1},... | collective-permute-start | bytes 393224 | tf_op jit(solution)/shard_map/ppermute | solution.py:598
  8.3 3.4 %collective-permute-start.3 = (bf16[1024,256]{1,0:T(8,128)(2,1)}, bf16[1024,256]{1,0:T(8,128)(2,1)}, u32[]{:S(2)}, u32[]{:S(2)}) collective-permute-start(bf16[1024,256]{1,0:T(8,128)(2,1)} %param.23), channel_id=1, source_target_pairs={{0,8},{1,9},{2,10},{3,11},{4,12},{5,13},{6,14},{7,15},{8,0},{9,1},... | collective-permute-start | bytes 1572872 | tf_op jit(solution)/shard_map/ppermute | solution.py:598
  13.4 16.3 %shard_map.254 = bf16[8,128,1024]{2,1,0:T(8,128)(2,1)} custom-call(bf16[128,1024]{1,0:T(8,128)(2,1)} %block_input.1), custom_call_target="tpu_custom_call" | custom-call | tf_op jit(solution)/shard_map/pallas_call | solution.py:390
  32.3 2.9 convolution_bitcast_fusion
  35.3 1.9 fusion.2
  37.3 2.0 exponential_reduce_fusion
  39.4 2.6 convolution_convert_fusion.4
  41.9 2.1 convolution_convert_fusion
  44.1 17.9 %shard_map.255.attended = f32[128,1024]{1,0:T(8,128)} custom-call(bf16[8,128,1024]{2,1,0:T(8,128)(2,1)} %bitcast.71), custom_call_target="tpu_custom_call" | custom-call | tf_op jit(solution)/shard_map/pallas_call | solution.py:416
  62.0 2.1 pad_maximum_fusion.up
  64.1 2.1 pad_maximum_fusion.1.down
  66.2 59.7 %shard_map.256 = (bf16[128,1024]{1,0:T(8,128)(2,1)}, f32[128,1024]{1,0:T(8,128)}, bf16[128,1024]{1,0:T(8,128)(2,1)}, bf16[2,1024,256]{2,1,0:T(8,128)(2,1)}, bf16...) custom-call(f32[128,1024]{1,0:T(8,128)} %shard_map.255.attended, bf16[128,1024]{1,0:T(8,128)(2,1)} %block_input.1, ...), custom_call_target="tpu_custom_call" | custom-call | tf_op jit(solution)/shard_map/pallas_call | solution.py:348
  125.9 15.8 %shard_map.257 = bf16[8,128,1024]{2,1,0:T(8,128)(2,1)} custom-call(bf16[128,1024]{1,0:T(8,128)(2,1)} %get-tuple-element.27.x_ref), custom_call_target="tpu_custom_call" | custom-call | tf_op jit(solution)/shard_map/pallas_call | solution.py:390
  141.8 2.1 convolution_convert_fusion.2
  143.8 2.4 convolution_convert_fusion.3
  146.3 6.6 %fusion.53 = (f32[2,64]{1,0:T(2,128)S(1)}, bf16[1024,2,64]{0,2,1:T(8,128)(2,1)}) fusion(bf16[1024,2,64]{0,2,1:T(8,128)(2,1)S(1)} %bitcast.82, f32[2,1024,1024]{1,2,0:T(8,128)} %copy-done.1, f32[2,1024]{1,0:T(2,128)S(1)} %log_add_fusion, pred[1024,1024]{0,1:T(8,128)(4,1)S(1)} %broadcast_compare_fusion), kind=kOutput, calls=%fused_computation.62 | convolution fusion | flops 277086080 | bytes 9970176 | tf_op jit(solution)/shard_map/hqk,qhd->khd/dot_general | solution.py:586
  152.9 4.6 %fusion.34 = f32[2,1024,1024]{1,2,0:T(8,128)} fusion(bf16[1024,2,64]{0,2,1:T(8,128)(2,1)S(1)} %bitcast.83, f32[1024,2,64]{0,2,1:T(8,128)S(1)} %bitcast.77, f32[2,64]{1,0:T(2,128)S(1)} %add.38), kind=kOutput, calls=%fused_computation.39 | convolution fusion | flops 268697600 | bytes 9175552 | tf_op jit(solution)/shard_map/qhd,khd->hqk/dot_general | solution.py:587
  157.4 14.5 %fusion.31 = bf16[2,64,1024]{2,1,0:T(8,128)(2,1)} fusion(f32[2,1024,1024]{1,2,0:T(8,128)} %fusion.34, f32[2,1024,1024]{1,2,0:T(8,128)} %copy-done.1, f32[2,1024]{1,0:T(2,128)S(1)} %log_add_fusion, pred[1024,1024]{0,1:T(8,128)(4,1)S(1)} %broadcast_compare_fusion, f32[1024,2,64]{0,2,1:T(8,128)S(1)} %bitcast.90, f32[2,64]{1,0:T(2,128)S(1)} %add.42), kind=kOutput, calls=%fused_computation.29 | convolution fusion | flops 291900416 | bytes 18620928 | tf_op jit(solution)/shard_map/hqk,qhd->khd/dot_general | solution.py:593
  172.0 14.6 %fusion.52 = (f32[2,64]{1,0:T(2,128)S(1)}, bf16[1024,2,64]{0,2,1:T(8,128)(2,1)}) fusion(bf16[1024,2,64]{0,2,1:T(8,128)(2,1)} %bitcast.92, f32[2,1024,1024]{1,2,0:T(8,128)} %fusion.34, f32[2,1024,1024]{1,2,0:T(8,128)} %copy-done.1, f32[2,1024]{1,0:T(2,128)S(1)} %log_add_fusion, pred[1024,1024]{0,1:T(8,128)(4,1)S(1)} %broadcast_compare_fusion), kind=kOutput, calls=%fused_computation.61 | convolution fusion | flops 291769216 | bytes 18358784 | tf_op jit(solution)/shard_map/hqk,khd->qhd/dot_general | solution.py:592
  194.2 75.4 %shard_map.259 = (f32[8,128,256]{2,1,0:T(8,128)}, f32[8,32,1024]{2,1,0:T(8,128)}, f32[8,32,1024]{2,1,0:T(8,128)}, f32[8,1024]{1,0:T(8,128)}) custom-call(bf16[2,8,128,256]{3,2,1,0:T(8,128)(2,1)} %bitcast.78, bf16[2,8,32,1024]{3,2,1,0:T(8,128)(2,1)} %bitcast.79, bf16[2,8,32,1024]{3,2,1,0:T(8,128)(2,1)} %bitcast.72, f32[8,1024]{1,0:T(8,128)} %get-tuple-element.30.refs_3_, ...), custom_call_target="tpu_custom_call" | custom-call | tf_op jit(solution)/shard_map/pallas_call | solution.py:552
  275.0 2.1 slice.55
  277.7 3.9 %bitcast_convert_fusion = bf16[1024,1024]{1,0:T(8,128)(2,1)} fusion(bf16[3,64,1024]{2,1,0:T(8,128)(2,1)} %copy-done.16, bf16[3,64,1024]{2,1,0:T(8,128)(2,1)} %bitcast.114, bf16[1,1024,128]{2,1,0:T(8,128)(2,1)} %copy-done.12, bf16[1,1024,128]{2,1,0:T(8,128)(2,1)} %copy-done.14, bf16[1,1024,128]{2,1,0:T(8,128)(2,1)} %copy-done.13), kind=kOutput, calls=%fused_computation.11 | convolution fusion | flops 808714240 | bytes 3670016 | tf_op jit(solution)/shard_map/ctw,cwd->td/dot_general | solution.py:666
  281.6 17.9 %shard_map.258 = f32[128,1024]{1,0:T(8,128)} custom-call(bf16[8,128,1024]{2,1,0:T(8,128)(2,1)} %bitcast.73), custom_call_target="tpu_custom_call" | custom-call | tf_op jit(solution)/shard_map/pallas_call | solution.py:416
  (75 shorter events, 22.6 us)
Async XLA Ops:
  0.6 11.1 %copy-start = (s32[2,1024]{1,0:T(2,128)S(1)}, s32[2,1024]{1,0:T(2,128)}, u32[]{:S(2)}) copy-start(s32[2,1024]{1,0:T(2,128)} %param.16) | copy-start | bytes 24580
  0.7 29.0 %collective-permute-start.1 = (f32[2,64]{1,0:T(2,128)}, f32[2,64]{1,0:T(2,128)S(1)}, u32[]{:S(2)}, u32[]{:S(2)}) collective-permute-start(f32[2,64]{1,0:T(2,128)} %param.18), channel_id=1, source_target_pairs={{0,8},{1,9},{2,10},{3,11},{4,12},{5,13},{6,14},{7,15},{8,0},{9,1},... | collective-permute-start | bytes 1544 | tf_op jit(solution)/shard_map/ppermute | solution.py:598
  4.7 26.3 %collective-permute-start.4 = (f32[256]{0:T(256)}, f32[256]{0:T(256)S(1)}, u32[]{:S(2)}, u32[]{:S(2)}) collective-permute-start(f32[256]{0:T(256)} %param.24), channel_id=1, source_target_pairs={{0,8},{1,9},{2,10},{3,11},{4,12},{5,13},{6,14},{7,15},{8,0},{9,1},... | collective-permute-start | bytes 3080 | tf_op jit(solution)/shard_map/ppermute | solution.py:598
  4.8 27.5 %collective-permute-start.2 = (bf16[64,1024]{1,0:T(8,128)(2,1)}, bf16[64,1024]{1,0:T(8,128)(2,1)S(1)}, u32[]{:S(2)}, u32[]{:S(2)}) collective-permute-start(bf16[64,1024]{1,0:T(8,128)(2,1)} %param.19), channel_id=1, source_target_pairs={{0,8},{1,9},{2,10},{3,11},{4,12},{5,13},{6,14},{7,15},{8,0},{9,1},... | collective-permute-start | bytes 393224 | tf_op jit(solution)/shard_map/ppermute | solution.py:598
  8.2 24.1 %collective-permute-start = (bf16[3,64,1024]{2,1,0:T(8,128)(2,1)}, bf16[3,64,1024]{2,1,0:T(8,128)(2,1)S(1)}, u32[]{:S(2)}, u32[]{:S(2)}) collective-permute-start(bf16[3,64,1024]{2,1,0:T(8,128)(2,1)} %bitcast.112), channel_id=1, source_target_pairs={{0,8},{1,9},{2,10},{3,11},{4,12},{5,13},{6,14},{7,15},{8,0},{9,1},... | collective-permute-start | bytes 1179656 | tf_op jit(solution)/shard_map/ppermute | solution.py:598
  8.3 53.6 %collective-permute-start.3 = (bf16[1024,256]{1,0:T(8,128)(2,1)}, bf16[1024,256]{1,0:T(8,128)(2,1)}, u32[]{:S(2)}, u32[]{:S(2)}) collective-permute-start(bf16[1024,256]{1,0:T(8,128)(2,1)} %param.23), channel_id=1, source_target_pairs={{0,8},{1,9},{2,10},{3,11},{4,12},{5,13},{6,14},{7,15},{8,0},{9,1},... | collective-permute-start | bytes 1572872 | tf_op jit(solution)/shard_map/ppermute | solution.py:598
  29.7 34.4 %collective-permute-start.5 = (bf16[256,1024]{1,0:T(8,128)(2,1)}, bf16[256,1024]{1,0:T(8,128)(2,1)}, u32[]{:S(2)}, u32[]{:S(2)}) collective-permute-start(bf16[256,1024]{1,0:T(8,128)(2,1)} %param.25), channel_id=1, source_target_pairs={{0,8},{1,9},{2,10},{3,11},{4,12},{5,13},{6,14},{7,15},{8,0},{9,1},... | collective-permute-start | bytes 1572872 | tf_op jit(solution)/shard_map/ppermute | solution.py:598
  32.3 5.0 %copy-start.16 = (bf16[3,64,1024]{2,1,0:T(8,128)(2,1)}, bf16[3,64,1024]{2,1,0:T(8,128)(2,1)S(1)}, u32[]{:S(2)}) copy-start(bf16[3,64,1024]{2,1,0:T(8,128)(2,1)S(1)} %collective-permute-done) | copy-start | bytes 1179652
  35.2 4.1 %copy-start.11 = (bf16[1,1024,128]{1,2,0:T(8,128)(2,1)}, bf16[1,1024,128]{1,2,0:T(8,128)(2,1)S(1)}, u32[]{:S(2)}) copy-start(bf16[1,1024,128]{1,2,0:T(8,128)(2,1)S(1)} %slice.73) | copy-start | bytes 786436
  35.3 4.0 %copy-start.8 = (f32[1,1024,128]{1,2,0:T(8,128)}, f32[1,1024,128]{1,2,0:T(8,128)S(1)}, u32[]{:S(2)}) copy-start(f32[1,1024,128]{1,2,0:T(8,128)S(1)} %get-tuple-element.38) | copy-start | bytes 1572868
  37.3 4.6 %copy-start.1 = (f32[2,1024,1024]{1,2,0:T(8,128)}, f32[2,1024,1024]{1,2,0:T(8,128)S(1)}, u32[]{:S(2)}) copy-start(f32[2,1024,1024]{1,2,0:T(8,128)S(1)} %get-tuple-element.51) | copy-start | bytes 25165828
  39.4 22.6 %copy-start.6 = (bf16[1024,256]{1,0:T(8,128)(2,1)S(1)}, bf16[1024,256]{1,0:T(8,128)(2,1)}, u32[]{:S(2)}) copy-start(bf16[1024,256]{1,0:T(8,128)(2,1)} %param.23) | copy-start | bytes 1572868
  39.4 24.7 %copy-start.7 = (bf16[256,1024]{1,0:T(8,128)(2,1)S(1)}, bf16[256,1024]{1,0:T(8,128)(2,1)}, u32[]{:S(2)}) copy-start(bf16[256,1024]{1,0:T(8,128)(2,1)} %param.25) | copy-start | bytes 1572868
  146.2 11.2 %copy-start.9 = (f32[1,1024,128]{1,2,0:T(8,128)S(1)}, f32[1,1024,128]{1,2,0:T(8,128)}, u32[]{:S(2)}) copy-start(f32[1,1024,128]{1,2,0:T(8,128)} %copy-done.8) | copy-start | bytes 1572868
  172.0 15.1 %copy-start.15 = (f32[1,512]{1,0:T(1,128)S(1)}, f32[1,512]{1,0:T(1,128)}, u32[]{:S(2)}) copy-start(f32[1,512]{1,0:T(1,128)} %get-tuple-element.31) | copy-start | bytes 6148
  172.0 19.4 %copy-start.2 = (bf16[8,128,1024]{2,1,0:T(8,128)(2,1)S(1)}, bf16[8,128,1024]{2,1,0:T(8,128)(2,1)}, u32[]{:S(2)}) copy-start(bf16[8,128,1024]{2,1,0:T(8,128)(2,1)} %shard_map.254) | copy-start | bytes 6291460
  188.9 5.3 %copy-start.12 = (bf16[1,1024,128]{2,1,0:T(8,128)(2,1)}, bf16[1,1024,128]{2,1,0:T(8,128)(2,1)S(1)}, u32[]{:S(2)}) copy-start(bf16[1,1024,128]{2,1,0:T(8,128)(2,1)S(1)} %copy.35) | copy-start | bytes 786436
  190.1 4.0 %copy-start.13 = (bf16[1,1024,128]{2,1,0:T(8,128)(2,1)}, bf16[1,1024,128]{2,1,0:T(8,128)(2,1)S(1)}, u32[]{:S(2)}) copy-start(bf16[1,1024,128]{2,1,0:T(8,128)(2,1)S(1)} %copy.33) | copy-start | bytes 786436
  191.4 2.8 copy-start.14
  192.4 107.2 %copy-start.5 = (f32[128,1024]{1,0:T(8,128)S(1)}, f32[128,1024]{1,0:T(8,128)}, u32[]{:S(2)}) copy-start(f32[128,1024]{1,0:T(8,128)} %get-tuple-element.26) | copy-start | bytes 1572868
  192.4 109.0 %copy-start.10 = (bf16[128,1024]{1,0:T(8,128)(2,1)S(1)}, bf16[128,1024]{1,0:T(8,128)(2,1)}, u32[]{:S(2)}) copy-start(bf16[128,1024]{1,0:T(8,128)(2,1)} %get-tuple-element.68) | copy-start | bytes 786436
  269.6 32.5 %copy-start.4 = (f32[8,128,256]{2,1,0:T(8,128)S(1)}, f32[8,128,256]{2,1,0:T(8,128)}, u32[]{:S(2)}) copy-start(f32[8,128,256]{2,1,0:T(8,128)} %get-tuple-element.34) | copy-start | bytes 3145732
  269.6 33.5 %copy-start.3 = (f32[8,32,1024]{2,1,0:T(8,128)S(1)}, f32[8,32,1024]{2,1,0:T(8,128)}, u32[]{:S(2)}) copy-start(f32[8,32,1024]{2,1,0:T(8,128)} %get-tuple-element.35) | copy-start | bytes 3145732

commit v3 on v2

--- a/solution.py
+++ b/solution.py
@@ -1,5 +1,3 @@
-import functools
-
 import jax
 import jax.numpy as jnp
 from jax import lax
@@ -246,17 +244,18 @@
     return block.reshape(CHIP, block.shape[2])
 
 
-def all_rows(ref):
+def flat_rows(ref):
     block = ref[...]
-    return block.reshape(RING * BLOCK, block.shape[2])
+    return block.reshape(block.shape[0] * block.shape[1], block.shape[2])
 
 
 def feed_forward_kernel(
-    attended, block_input, out_bias, gain1, bias1, up, up_bias, down, down_bias, gain2, bias2, cot,
+    attended, block_input, out_bias, gain1, bias1, up, bias_two, down, down_bias, gain2, bias2, cot,
     out, d_first, d_first_half, g_up, g_down, g_up_bias, vecs,
     hidden_half, hidden_all, act, slope, d_second_half, d_second_all, d_pre, gather_sems, *scatter_scratch,
 ):
     block_of, _ = ring_place()
+    shard = up.shape[2]
     greet_ring()
     first = block_input[...].astype(wide) + attended[...] + out_bias[...]
     hidden, normed_one, inverse_one = layer_norm(first, gain1[...], bias1[...])
@@ -271,12 +270,12 @@
         k = ring_order(s)
         chip = block_of(k) // 2
         rows = pl.ds(chip * CHIP, CHIP)
-        pre = dot_nn(chip_rows(hidden_all, chip), up[...]) + up_bias[...]
-        value, gelu_slope = gelu_parts(pre)
-        value = value.astype(half)
-        act[rows] = value
-        slope[rows] = gelu_slope
-        term = dot_nn(value, down[...]).astype(half)
+        for a in range(2):
+            pre = dot_nn(chip_rows(hidden_all, chip), up[a]) + bias_two[a, :, :shard]
+            value, gelu_slope = gelu_parts(pre)
+            act[rows, a * shard : (a + 1) * shard] = value.astype(half)
+            slope[rows, a * shard : (a + 1) * shard] = gelu_slope
+        term = dot_nn(act[rows], flat_rows(down)).astype(half)
         scatter.y[pl.ds(2 * chip, 2)] = term.reshape(2, BLOCK, term.shape[1])
         scatter.computed(k)
 
@@ -306,21 +305,21 @@
         k = ring_order(s)
         chip = block_of(k) // 2
         rows = pl.ds(chip * CHIP, CHIP)
-        grad_pre = dot_nt(chip_rows(d_second_all, chip), down[...]) * slope[rows]
+        grad_pre = dot_nt(chip_rows(d_second_all, chip), flat_rows(down)) * slope[rows]
         g_up_bias[...] += column_sum(grad_pre)
         grad_pre = grad_pre.astype(half)
         d_pre[rows] = grad_pre
-        term = dot_nt(grad_pre, up[...]).astype(half)
+        term = dot_nt(grad_pre[:, :shard], up[0]) + dot_nt(grad_pre[:, shard:], up[1])
+        term = term.astype(half)
         scatter.y[pl.ds(2 * chip, 2)] = term.reshape(2, BLOCK, term.shape[1])
         scatter.computed(k)
 
     scatter.sides()
     scatter.across()
     gather.finish()
-    shard = up.shape[1] // 2
     for a in range(2):
-        columns = pl.ds(a * shard, shard)
-        g_down[a] = dot_tn(act[:, columns], all_rows(d_second_all)).astype(half)
+        part = dot_tn(act[:, a * shard : (a + 1) * shard], flat_rows(d_second_all)).astype(half)
+        g_down[a] = part.reshape(PIECES, shard // PIECES, part.shape[1])
     scatter.through()
 
     @pl.loop(0, 4)
@@ -329,7 +328,7 @@
         left = hidden_all[:, :, columns].reshape(RING * BLOCK, 256)
         part = dot_tn(left, d_pre[...]).astype(half)
         for a in range(2):
-            g_up[a, columns] = part[:, a * shard : (a + 1) * shard]
+            g_up[a, pl.ds(2 * i, 2)] = part[:, a * shard : (a + 1) * shard].reshape(2, BLOCK, shard)
 
     d_hidden = d_second + scatter.result()
     scatter.finish()
@@ -341,18 +340,18 @@
     vecs[pl.ds(2, 1)] = column_sum(d_hidden)
 
 
-def feed_forward(attended, block_input, out_bias, gain1, bias1, up, up_bias, down, down_bias, gain2, bias2, cot):
+def feed_forward(attended, block_input, out_bias, gain1, bias1, up, bias_two, down, down_bias, gain2, bias2, cot):
     rows, width = attended.shape
-    hidden = up.shape[1]
-    shard = hidden // 2
+    shard = up.shape[2]
+    hidden = 2 * shard
     return pl.pallas_call(
         feed_forward_kernel,
         out_shape=(
             jax.ShapeDtypeStruct((rows, width), half),
             jax.ShapeDtypeStruct((rows, width), wide),
             jax.ShapeDtypeStruct((rows, width), half),
-            jax.ShapeDtypeStruct((2, width, shard), half),
-            jax.ShapeDtypeStruct((2, shard, width), half),
+            jax.ShapeDtypeStruct((2, PIECES, width // PIECES, shard), half),
+            jax.ShapeDtypeStruct((2, PIECES, shard // PIECES, width), half),
             jax.ShapeDtypeStruct((1, hidden), wide),
             jax.ShapeDtypeStruct((8, width), wide),
         ),
@@ -373,54 +372,7 @@
         compiler_params=pltpu.CompilerParams(
             collective_id=2, has_side_effects=True, vmem_limit_bytes=VMEM_BYTES
         ),
-    )(attended, block_input, out_bias, gain1, bias1, up, up_bias, down, down_bias, gain2, bias2, cot)
-
-
-def gather_kernel(x_ref, o_ref, send, recv):
-    greet_ring()
-    gather = Gather(x_ref, o_ref, send, recv)
-    gather.start()
-    for s in range(4):
-        gather.ready(s)
-    gather.finish()
-
-
-def gather_rows(x):
-    rows, width = x.shape
-    out = pl.pallas_call(
-        gather_kernel,
-        out_shape=jax.ShapeDtypeStruct((RING, rows, width), x.dtype),
-        in_specs=[VMEM_WHOLE],
-        out_specs=VMEM_WHOLE,
-        scratch_shapes=[pltpu.SemaphoreType.DMA((13,)), pltpu.SemaphoreType.DMA((13,))],
-        compiler_params=pltpu.CompilerParams(collective_id=0, has_side_effects=True),
-    )(x)
-    return out.reshape(RING * rows, width)
-
-
-def scatter_kernel(y_ref, o_ref, y, *scratch):
-    greet_ring()
-    scatter = Scatter(y_ref, *scratch)
-    for k in (1, 3, 2, 0):
-        scatter.computed(k)
-    scatter.sides()
-    scatter.across()
-    scatter.through()
-    o_ref[...] = scatter.result()
-    scatter.finish()
-
-
-def scatter_rows(y):
-    tokens, width = y.shape
-    rows = tokens // RING
-    return pl.pallas_call(
-        scatter_kernel,
-        out_shape=jax.ShapeDtypeStruct((rows, width), wide),
-        in_specs=[VMEM_WHOLE],
-        out_specs=VMEM_WHOLE,
-        scratch_shapes=Scatter.scratch(width),
-        compiler_params=pltpu.CompilerParams(collective_id=1, has_side_effects=True),
-    )(y.reshape(RING, rows, width))
+    )(attended, block_input, out_bias, gain1, bias1, up, bias_two, down, down_bias, gain2, bias2, cot)
 
 
 class PlaneSum:
@@ -501,7 +453,7 @@
         for r in range(1, RING):
             remote(vecs, self.line.at[r], self.send, self.recv, 14 + r, self.line_peer(r)).start()
 
-    def plane(self, vecs, shards):
+    def plane(self, vecs, shard_rows):
         total = vecs[...]
         for r in range(1, RING):
             place = self.line.at[r]
@@ -509,7 +461,7 @@
             total += self.line[r]
         row = lax.broadcasted_iota(jnp.int32, total.shape, 0)
         for a in range(2):
-            self.base[a] = jnp.where(row == 6, jnp.broadcast_to(shards[pl.ds(a, 1)], total.shape), total)
+            self.base[a] = jnp.where(row == 6, jnp.broadcast_to(shard_rows[a], total.shape), total)
         for n in range(1, 2 * PIECES):
             _, device = PlaneSum.peer(n // PIECES, n % PIECES)
             remote(self.base.at[n // PIECES], self.land.at[n - 1], self.send, self.recv, n - 1, device).start()
@@ -526,76 +478,264 @@
         return total
 
 
-def reduce_kernel(count, *refs):
-    grads, rest = refs[:count], refs[count:]
-    vecs, shards, rest = rest[0], rest[1], rest[2:]
-    outs, rest = rest[:count], rest[count:]
-    small_out, rest = rest[0], rest[1:]
-    small = SmallSum(*rest[:5])
-    planes = [PlaneSum(*rest[5 + 4 * i : 9 + 4 * i]) for i in range(count)]
+def pair_of(shape):
+    return jax.ShapeDtypeStruct((2, *shape.shape), shape.dtype)
+
+
+def segment_column(ids, column):
+    upper = lax.axis_index("tensor") // RING
+    numbers = jnp.where(upper == 0, ids[pl.ds(0, 1)], ids[pl.ds(1, 1)])
+    column[...] = jnp.transpose(jnp.broadcast_to(numbers, (128, numbers.shape[1])))
+    return numbers
+
+
+def attention_kernel(
+    x, ids, qkv, out_weight, up, down, bias,
+    attended, x_all, queries, keys, values, lse, context, qkv_two, out_two, up_two, down_two, bias_two,
+    column, gather_sems, trade_sems, *scatter_scratch,
+):
+    block_of, device_of = ring_place()
+    across_z = (lax.axis_index("dp"), lax.rem(lax.axis_index("tensor") + RING, 2 * RING))
+    greet((device_of(1), device_of(-1), device_of(0, True), across_z))
+    gather = Gather(x, x_all, gather_sems.at[0], gather_sems.at[1])
+    scatter = Scatter(*scatter_scratch)
+    gather.start()
+    pairs = ((bias, bias_two), (qkv, qkv_two), (out_weight, out_two), (up, up_two), (down, down_two))
+    trades = [
+        remote(mine, two.at[1], trade_sems.at[0], trade_sems.at[1], slot, across_z)
+        for slot, (mine, two) in enumerate(pairs)
+    ]
+    for trade in trades:
+        trade.start()
+    for mine, two in pairs:
+        two[0] = mine[...]
+    numbers = segment_column(ids, column)
+    ff = up.shape[1]
+
+    def project(a, chip):
+        rows = pl.ds(chip * CHIP, CHIP)
+        product = dot_nt(chip_rows(x_all, chip), qkv_two[a].reshape(3 * HEAD_DIM, x.shape[1]))
+        parts = [product[:, i * HEAD_DIM : (i + 1) * HEAD_DIM] for i in range(3)]
+        queries[a, rows] = (parts[0] + bias_two[a, :, ff : ff + HEAD_DIM]).astype(half)
+        keys[a, rows] = parts[1].astype(half)
+        values[a, rows] = (parts[2] + bias_two[a, :, ff + HEAD_DIM : ff + 2 * HEAD_DIM]).astype(half)
+
+    @pl.loop(0, 4)
+    def _(s):
+        gather.ready(s)
+        project(0, block_of(ring_order(s)) // 2)
+
+    trades[0].wait_recv()
+    trades[1].wait_recv()
+
+    @pl.loop(0, 4)
+    def _(chip):
+        project(1, chip)
+
+    trades[2].wait_recv()
+
+    @pl.loop(0, 4)
+    def _(i):
+        k = ring_order(3 - i)
+        chip = block_of(k) // 2
+        rows = pl.ds(chip * CHIP, CHIP)
+        allowed = column[rows, 0:1] == numbers
+        for a in range(2):
+            scores = dot_nt(queries[a, rows] * HEAD_DIM ** (-0.5), keys[a])
+            masked = jnp.where(allowed, scores, MASKED)
+            top = jnp.max(masked, axis=-1, keepdims=True)
+            weights = jnp.exp(masked - top)
+            mass = jnp.sum(weights, axis=-1, keepdims=True)
+            lse[a, rows] = top + jnp.log(mass)
+            probs = (weights * (1.0 / mass)).astype(half)
+            context[rows, a * HEAD_DIM : (a + 1) * HEAD_DIM] = dot_nn(probs, values[a]).astype(half)
+        term = dot_nn(context[rows], flat_rows(out_two)).astype(half)
+        scatter.y[pl.ds(2 * chip, 2)] = term.reshape(2, BLOCK, term.shape[1])
+        scatter.computed(k)
+
+        @pl.when(i == 1)
+        def _():
+            scatter.across()
+
+    scatter.sides()
+    gather.finish()
+    scatter.through()
+    attended[...] = scatter.result()
+    scatter.finish()
+    trades[3].wait_recv()
+    trades[4].wait_recv()
+    for trade in trades:
+        trade.wait_send()
+
+
+def attention(x, ids, qkv, out_weight, up, down, bias):
+    rows, width = x.shape
+    tokens = RING * rows
+    head = jax.ShapeDtypeStruct((2, tokens, HEAD_DIM), half)
+    return pl.pallas_call(
+        attention_kernel,
+        out_shape=(
+            jax.ShapeDtypeStruct((rows, width), wide),
+            jax.ShapeDtypeStruct((RING, rows, width), half),
+            head,
+            head,
+            head,
+            jax.ShapeDtypeStruct((2, tokens, 1), wide),
+            jax.ShapeDtypeStruct((tokens, 2 * HEAD_DIM), half),
+            pair_of(qkv),
+            pair_of(out_weight),
+            pair_of(up),
+            pair_of(down),
+            pair_of(bias),
+        ),
+        in_specs=[VMEM_WHOLE] * 7,
+        out_specs=(VMEM_WHOLE,) * 12,
+        scratch_shapes=[
+            pltpu.VMEM((tokens, 128), jnp.int32),
+            pltpu.SemaphoreType.DMA((2, Gather.slots)),
+            pltpu.SemaphoreType.DMA((2, 5)),
+        ]
+        + Scatter.scratch(width),
+        compiler_params=pltpu.CompilerParams(
+            collective_id=0, has_side_effects=True, vmem_limit_bytes=VMEM_BYTES
+        ),
+    )(x, ids, qkv, out_weight, up, down, bias)
+
+
+def attention_back_kernel(
+    d_first, d_first_half, x_all, ids, queries, keys, values, lse, context, qkv_two, out_two,
+    g_up, g_down, g_up_bias, vecs,
+    input_grad, up_sum, down_sum, late_sum, small_out,
+    d_first_all, column, d_keys, d_values, d_qkv, query_sum, late, gather_sems, *scratch,
+):
+    block_of, _ = ring_place()
+    scatter, scratch = Scatter(*scratch[:7]), scratch[7:]
+    small, scratch = SmallSum(*scratch[:5]), scratch[5:]
+    early = [(PlaneSum(*scratch[:4]), g_up, up_sum), (PlaneSum(*scratch[4:8]), g_down, down_sum)]
+    last = PlaneSum(*scratch[8:])
     greet(PlaneSum.peers() + SmallSum.peers())
+    gather = Gather(d_first_half, d_first_all, gather_sems.at[0], gather_sems.at[1])
+    gather.start()
     small.start(vecs)
-    for plane, grad in zip(planes, grads):
-        plane.scatter(grad)
-    small.plane(vecs, shards)
-    for plane, grad in zip(planes, grads):
-        plane.share(grad)
-    for plane, out in zip(planes, outs):
-        plane.result(out)
+    for plane, grads, _ in early:
+        plane.scatter(grads)
+    numbers = segment_column(ids, column)
+    d_keys[...] = jnp.zeros_like(d_keys)
+    d_values[...] = jnp.zeros_like(d_values)
+    query_sum[...] = jnp.zeros_like(query_sum)
+    group = 3 * HEAD_DIM
+
+    @pl.loop(0, 4)
+    def _(s):
+        gather.ready(s)
+        chip = block_of(ring_order(s)) // 2
+        rows = pl.ds(chip * CHIP, CHIP)
+        d_context = dot_nt(chip_rows(d_first_all, chip), flat_rows(out_two)).astype(half)
+        allowed = column[rows, 0:1] == numbers
+        for a in range(2):
+            d_head = d_context[:, a * HEAD_DIM : (a + 1) * HEAD_DIM]
+            query = queries[a, rows]
+            scores = dot_nt(query * HEAD_DIM ** (-0.5), keys[a])
+            probs = jnp.exp(jnp.where(allowed, scores, MASKED) - lse[a, rows])
+            d_values[a] += dot_tn(d_head, probs.astype(half))
+            d_probs = dot_nt(d_head * HEAD_DIM ** (-0.5), values[a])
+            mean = jnp.sum(probs * d_probs, axis=-1, keepdims=True)
+            d_scores = (probs * (d_probs - mean)).astype(half)
+            d_query = dot_nn(d_scores, keys[a])
+            query_sum[a] += column_sum(d_query)
+            d_qkv[rows, a * group : a * group + HEAD_DIM] = d_query.astype(half)
+            d_keys[a] += dot_tn(query, d_scores)
+
+    gather.finish()
+    shard_rows = []
+    shard = g_up_bias.shape[1] // 2
+    for a in range(2):
+        at = a * group + HEAD_DIM
+        d_qkv[:, at : at + HEAD_DIM] = jnp.transpose(d_keys[a].astype(half))
+        d_qkv[:, at + HEAD_DIM : at + 2 * HEAD_DIM] = jnp.transpose(d_values[a].astype(half))
+        value_sum = jnp.sum(d_values[a], axis=1, keepdims=True)
+        value_sum = jnp.transpose(jnp.broadcast_to(value_sum, (HEAD_DIM, 128)))[0:1]
+        shard_rows.append(
+            jnp.concatenate(
+                [
+                    g_up_bias[:, a * shard : (a + 1) * shard],
+                    query_sum[a],
+                    value_sum,
+                    jnp.zeros((1, vecs.shape[1] - shard - 2 * HEAD_DIM), wide),
+                ],
+                axis=1,
+            )
+        )
+    grad_out = dot_tn(context[...], flat_rows(d_first_all)).astype(half)
+    piece = late.shape[2]
+    for a in range(2):
+        part = dot_tn(d_qkv[:, a * group : (a + 1) * group], flat_rows(x_all)).astype(half)
+        late[a, pl.ds(0, 6)] = part.reshape(6, piece, part.shape[1])
+        part = grad_out[a * HEAD_DIM : (a + 1) * HEAD_DIM]
+        late[a, pl.ds(6, 2)] = part.reshape(2, piece, part.shape[1])
+    last.scatter(late)
+    small.plane(vecs, shard_rows)
+
+    @pl.loop(0, 4)
+    def _(i):
+        k = ring_order(3 - i)
+        chip = block_of(k) // 2
+        weight = qkv_two[...].reshape(2 * group, d_first.shape[1])
+        term = dot_nn(d_qkv[pl.ds(chip * CHIP, CHIP)], weight).astype(half)
+        scatter.y[pl.ds(2 * chip, 2)] = term.reshape(2, BLOCK, term.shape[1])
+        scatter.computed(k)
+
+        @pl.when(i == 1)
+        def _():
+            scatter.across()
+
+    scatter.sides()
+    scatter.through()
+    for plane, grads, _ in early:
+        plane.share(grads)
+    input_grad[...] = (d_first[...] + scatter.result()).astype(half)
+    scatter.finish()
+    last.share(late)
+    for plane, _, total in early:
+        plane.result(total)
+    last.result(late_sum)
     small_out[...] = small.result()
 
 
-def reduce_all(grads, vecs, shards):
-    scratch = list(SmallSum.scratch)
-    for grad in grads:
-        scratch += PlaneSum.scratch(*grad.shape[2:])
+def attention_back(d_first, d_first_half, x_all, ids, heads, lse, context, qkv_two, out_two, g_up, g_down, g_up_bias, vecs):
+    rows, width = d_first.shape
+    tokens = RING * rows
+    late = (PIECES, 4 * HEAD_DIM // PIECES, width)
     return pl.pallas_call(
-        functools.partial(reduce_kernel, len(grads)),
-        out_shape=tuple(jax.ShapeDtypeStruct(grad.shape[1:], wide) for grad in grads)
-        + (jax.ShapeDtypeStruct((8, 1024), wide),),
-        in_specs=[VMEM_WHOLE] * (len(grads) + 2),
-        out_specs=(VMEM_WHOLE,) * (len(grads) + 1),
-        scratch_shapes=scratch,
+        attention_back_kernel,
+        out_shape=(
+            jax.ShapeDtypeStruct((rows, width), half),
+            jax.ShapeDtypeStruct(g_up.shape[1:], wide),
+            jax.ShapeDtypeStruct(g_down.shape[1:], wide),
+            jax.ShapeDtypeStruct(late, wide),
+            jax.ShapeDtypeStruct(vecs.shape, wide),
+        ),
+        in_specs=[VMEM_WHOLE] * 15,
+        out_specs=(VMEM_WHOLE,) * 5,
+        scratch_shapes=[
+            pltpu.VMEM((RING, rows, width), half),
+            pltpu.VMEM((tokens, 128), jnp.int32),
+            pltpu.VMEM((2, HEAD_DIM, tokens), wide),
+            pltpu.VMEM((2, HEAD_DIM, tokens), wide),
+            pltpu.VMEM((tokens, 6 * HEAD_DIM), half),
+            pltpu.VMEM((2, 1, HEAD_DIM), wide),
+            pltpu.VMEM((2, *late), half),
+            pltpu.SemaphoreType.DMA((2, Gather.slots)),
+        ]
+        + Scatter.scratch(width)
+        + SmallSum.scratch
+        + PlaneSum.scratch(*g_up.shape[2:])
+        + PlaneSum.scratch(*g_down.shape[2:])
+        + PlaneSum.scratch(*late[1:]),
         compiler_params=pltpu.CompilerParams(
-            collective_id=3, has_side_effects=True, vmem_limit_bytes=VMEM_BYTES
+            collective_id=1, has_side_effects=True, vmem_limit_bytes=VMEM_BYTES
         ),
-    )(*grads, vecs, shards)
-
-
-def masked_scores(queries, keys, segs):
-    scores = jnp.einsum("qhd,khd->hqk", queries, keys, preferred_element_type=wide) * HEAD_DIM ** (-0.5)
-    allowed = segs[:, None] == segs[None, :]
-    return jnp.where(allowed[None], scores, MASKED)
-
-
-def forward_seq(items):
-    queries, keys, values, segs = items
-    masked = masked_scores(queries, keys, segs)
-    top = jnp.max(masked, axis=-1, keepdims=True)
-    lse = top + jnp.log(jnp.sum(jnp.exp(masked - top), axis=-1, keepdims=True))
-    probs = jnp.exp(masked - lse).astype(half)
-    context = jnp.einsum("hqk,khd->qhd", probs, values, preferred_element_type=wide)
-    return (context.astype(half), lse)
-
-
-def backward_seq(items):
-    queries, keys, values, segs, lse, d_context = items
-    masked = masked_scores(queries, keys, segs)
-    probs = jnp.exp(masked - lse)
-    probs_half = probs.astype(half)
-    d_values = jnp.einsum("hqk,qhd->khd", probs_half, d_context, preferred_element_type=wide)
-    d_probs = jnp.einsum("qhd,khd->hqk", d_context, values, preferred_element_type=wide)
-    d_scores = (
-        probs * (d_probs - jnp.sum(probs * d_probs, axis=-1, keepdims=True)) * HEAD_DIM ** (-0.5)
-    )
-    d_scores = d_scores.astype(half)
-    d_queries = jnp.einsum("hqk,khd->qhd", d_scores, keys, preferred_element_type=wide)
-    d_keys = jnp.einsum("hqk,qhd->khd", d_scores, queries, preferred_element_type=wide)
-    return (d_queries, d_keys, d_values)
-
-
-def trade(arr):
-    return lax.ppermute(arr, "tensor", [(t, (t + RING) % (2 * RING)) for t in range(2 * RING)])
+    )(d_first, d_first_half, x_all, ids, *heads, lse, context, qkv_two, out_two, g_up, g_down, g_up_bias, vecs)
 
 
 def row(vector):
@@ -619,64 +759,18 @@
     norm2_bias,
     cotangent,
 ):
-    my_seq = lax.axis_index("tensor") // RING
-    segs = lax.dynamic_index_in_dim(segment_ids, my_seq, 0, keepdims=False)
-    seq_len = segs.shape[0]
-    qkv_rows = jnp.swapaxes(qkv_weight, 1, 2)
-    qkv_two = jnp.concatenate([qkv_rows, trade(qkv_rows)], axis=1)
-    qv_bias_two = jnp.concatenate([qv_bias, trade(qv_bias)], axis=1)
-    out_two = jnp.concatenate([out_weight, trade(out_weight)], axis=0)
-    up_two = jnp.concatenate([up_weight, trade(up_weight)], axis=1)
-    up_bias_two = jnp.concatenate([up_bias, trade(up_bias)], axis=0)
-    down_two = jnp.concatenate([down_weight, trade(down_weight)], axis=0)
-
-    gathered = gather_rows(block_input)
-    projected = jnp.einsum("td,cwd->ctw", gathered, qkv_two, preferred_element_type=wide)
-    queries = (projected[0] + qv_bias_two[0]).astype(half)
-    keys = projected[1].astype(half)
-    values = (projected[2] + qv_bias_two[1]).astype(half)
-    width = queries.shape[1]
-
-    def by_head(arr):
-        return arr.reshape(seq_len, width // HEAD_DIM, HEAD_DIM)
-
-    context, lse = forward_seq((by_head(queries), by_head(keys), by_head(values), segs))
-    context = context.reshape(seq_len, width)
-    attended = scatter_rows(jnp.dot(context, out_two, preferred_element_type=wide).astype(half))
-
+    bias = row(jnp.concatenate([up_bias, qv_bias.reshape(-1)]))
+    attended, x_all, queries, keys, values, lse, context, qkv_two, out_two, up_two, down_two, bias_two = attention(
+        block_input, segment_ids, jnp.swapaxes(qkv_weight, 1, 2), out_weight, up_weight, down_weight, bias
+    )
     output, d_first, d_first_half, g_up, g_down, g_up_bias, vecs = feed_forward(
-        attended, block_input, row(out_bias), row(norm1_gain), row(norm1_bias), up_two, row(up_bias_two),
+        attended, block_input, row(out_bias), row(norm1_gain), row(norm1_bias), up_two, bias_two,
         down_two, row(down_bias), row(norm2_gain), row(norm2_bias), cotangent,
     )
-
-    d_first_all = gather_rows(d_first_half)
-    g_out = jnp.einsum("tw,td->wd", context, d_first_all, preferred_element_type=wide)
-    d_context = jnp.einsum("td,wd->tw", d_first_all, out_two, preferred_element_type=wide).astype(half)
-    d_queries, d_keys, d_values = (
-        arr.reshape(seq_len, width)
-        for arr in backward_seq(
-            (by_head(queries), by_head(keys), by_head(values), segs, lse, by_head(d_context))
-        )
+    input_grad, up_sum, down_sum, late_sum, small = attention_back(
+        d_first, d_first_half, x_all, segment_ids, (queries, keys, values), lse, context, qkv_two, out_two,
+        g_up, g_down, g_up_bias, vecs,
     )
-    g_qv_bias = jnp.concatenate(
-        [arr.reshape(2, HEAD_DIM) for arr in (jnp.sum(d_queries, axis=0), jnp.sum(d_values, axis=0))], axis=1
-    )
-    d_qkv = jnp.stack([d_queries, d_keys, d_values]).astype(half)
-    g_qkv = jnp.einsum("ctw,td->cwd", d_qkv, gathered, preferred_element_type=wide)
-    d_rows = jnp.einsum("ctw,cwd->td", d_qkv, qkv_two, preferred_element_type=wide)
-    input_grad = (d_first + scatter_rows(d_rows.astype(half))).astype(half)
-
-    pieces = g_up.reshape(2, PIECES, g_up.shape[1] // PIECES, g_up.shape[2])
-    down_pieces = g_down.reshape(2, PIECES, g_down.shape[1] // PIECES, g_down.shape[2])
-    g_qkv = g_qkv.astype(half).reshape(3, 2, HEAD_DIM, -1)
-    g_out = g_out.astype(half).reshape(1, 2, HEAD_DIM, -1)
-    late = jnp.swapaxes(jnp.concatenate([g_qkv, g_out], axis=0), 0, 1)
-    late = late.reshape(2, PIECES, 4 * HEAD_DIM // PIECES, -1)
-    shards = jnp.concatenate(
-        [g_up_bias.reshape(2, -1), g_qv_bias, jnp.zeros((2, 1024 - g_up_bias.shape[1] // 2 - 2 * HEAD_DIM), wide)],
-        axis=1,
-    )
-    up_sum, down_sum, late_sum, small = reduce_all((pieces, down_pieces, late), vecs, shards)
     ff = up_bias.shape[0]
     late_sum = late_sum.reshape(4, HEAD_DIM, -1)
     return (

time: 306 us -> 194 us (0.63)
  matrix products: 59.2 us -> 0 us
  Pallas kernels: 203 us -> 181 us
  other arithmetic: 13.2 us -> 0.68 us
  starting transfers between devices: 11.5 us -> 0 us
  local copies, waits for them, and re-layouts: 16.1 us -> 11.2 us
    dot_general x12 -> x0, matrix products: 59.2 us -> none  [the longest x1 14.6 us: backward_seq(): jnp.einsum('hqk,khd->qhd', d_scores, keys, preferred_element_type=wide)]
    pallas_call x5 -> x2, Pallas kernels: 143 us -> 123 us  [the longest x1 76.4 us: attention_back(): pl.pallas_call(attention_back_kernel, out_shape=(jax.ShapeDtypeStruct((ro...]
    ppermute x6 -> x0, starting transfers between devices: 11.5 us -> none  [trade(): lax.ppermute(arr, 'tensor', [(t, (t + RING) % (2 * RING)) for t in range(...]
    concatenate x6 -> x1, other arithmetic: 8 us -> 0.68 us  [per_device(): bias = row(jnp.concatenate([up_bias, qv_bias.reshape(-1)]))]
    another operation x3 -> x0, local copies, waits for them, and re-layouts: 3.54 us -> none  [per_device(): d_qkv = jnp.stack([d_queries, d_keys, d_values]).astype(half)]
  transfers between devices with their start and end apart: 6 -> 0, of which waited for: 0 -> 0; matrix products, arithmetic and copies ran while one was open for 6% -> 0% of each run, Pallas kernels for 11% -> 0%
where the time goes in v3:
time: 194 us
  Pallas kernels  181 us (93%)
  local copies, waits for them, and re-layouts  11.2 us (6%)
    pallas_call x1, Pallas kernels, attention_back(): pl.pallas_call(attention_back_kernel, out_shape=(jax.ShapeDtypeStruct((ro...  76.4 us
    pallas_call x1, Pallas kernels, feed_forward(): pl.pallas_call(feed_forward_kernel, out_shape=(jax.ShapeDtypeStruct((rows...  58.3 us
    pallas_call x1, Pallas kernels, attention(): pl.pallas_call(attention_kernel, out_shape=(jax.ShapeDtypeStruct((rows, w...  46.2 us

profile of v3, /device:TPU:0, one launch (start us, length us, event | category | flops | bytes accessed | tf_op | source)
XLA Modules:
  0.0 193.5 jit_solution(14245462778195427408)
XLA Ops:
  0.6 0.8 reshape.62
  1.4 0.7 pad_maximum_fusion
  2.1 0.6 reshape.63.bias
  2.7 46.2 %shard_map.254 = (f32[128,1024]{1,0:T(8,128)}, bf16[8,128,1024]{2,1,0:T(8,128)(2,1)}, bf16[2,1024,64]{2,1,0:T(8,128)(2,1)}, bf16[2,1024,64]{2,1,0:T(8,128)(2,1)}...) custom-call(bf16[128,1024]{1,0:T(8,128)(2,1)} %block_input.1, ...), custom_call_target="tpu_custom_call" | custom-call | tf_op jit(solution)/shard_map/pallas_call | solution.py:575
  48.9 58.3 %shard_map.255 = (bf16[128,1024]{1,0:T(8,128)(2,1)}, f32[128,1024]{1,0:T(8,128)}, bf16[128,1024]{1,0:T(8,128)(2,1)}, bf16[2,8,128,256]{3,2,1,0:T(8,128)(2,1)}, b...) custom-call(f32[128,1024]{1,0:T(8,128)} %get-tuple-element.38.attended, ...), custom_call_target="tpu_custom_call" | custom-call | tf_op jit(solution)/shard_map/pallas_call | solution.py:347
  107.2 76.4 %shard_map.256 = (bf16[128,1024]{1,0:T(8,128)(2,1)}, f32[8,128,256]{2,1,0:T(8,128)}, f32[8,32,1024]{2,1,0:T(8,128)}, f32[8,32,1024]{2,1,0:T(8,128)}, f32[8,1024]{1,0:T(8,128)}) custom-call(f32[128,1024]{1,0:T(8,128)} %get-tuple-element.43.d_first, bf16[128,1024]{1,0:T(8,128)(2,1)} %get-tuple-element.44.d_first_half, ...), custom_call_target="tpu_custom_call" | custom-call | tf_op jit(solution)/shard_map/pallas_call | solution.py:709
  183.6 0.0 copy-start.4
  183.6 0.0 copy-start.2
  183.7 0.0 copy-start.3
  183.7 0.0 copy-start.1
  183.7 2.2 %slice.34 = f32[6,32,1024]{2,1,0:T(8,128)} slice(f32[8,32,1024]{2,1,0:T(8,128)} %get-tuple-element.58), slice={[0:6], [0:32], [0:1024]} | slice | bytes 1572864 | tf_op jit(solution)/shard_map/slice | solution.py:779
  185.9 0.8 slice_reduce_fusion
  186.7 0.6 reshape_squeeze.3
  187.3 1.7 slice.37
  189.0 0.0 copy-done.4
  189.0 0.6 fusion
  189.6 0.6 slice.41
  190.2 0.0 copy-done.2
  190.2 0.7 copy.33
  190.9 0.0 copy-done.3
  190.9 0.7 copy.34
  191.6 0.0 copy-done.1
  191.6 1.0 copy.35
  192.6 1.0 copy.36
  (2 shorter events, 0.0 us)
Async XLA Ops:
  183.6 5.3 %copy-start.4 = (f32[8,1024]{1,0:T(8,128)S(1)}, f32[8,1024]{1,0:T(8,128)}, u32[]{:S(2)}) copy-start(f32[8,1024]{1,0:T(8,128)} %get-tuple-element.59) | copy-start | bytes 98308
  183.6 6.5 %copy-start.2 = (bf16[128,1024]{1,0:T(8,128)(2,1)S(1)}, bf16[128,1024]{1,0:T(8,128)(2,1)}, u32[]{:S(2)}) copy-start(bf16[128,1024]{1,0:T(8,128)(2,1)} %get-tuple-element.82) | copy-start | bytes 786436
  183.7 7.2 %copy-start.3 = (bf16[128,1024]{1,0:T(8,128)(2,1)S(1)}, bf16[128,1024]{1,0:T(8,128)(2,1)}, u32[]{:S(2)}) copy-start(bf16[128,1024]{1,0:T(8,128)(2,1)} %get-tuple-element.83) | copy-start | bytes 786436
  183.7 7.9 %copy-start.1 = (f32[8,128,256]{2,1,0:T(8,128)S(1)}, f32[8,128,256]{2,1,0:T(8,128)}, u32[]{:S(2)}) copy-start(f32[8,128,256]{2,1,0:T(8,128)} %get-tuple-element.60) | copy-start | bytes 3145732
  185.9 6.7 %copy-start = (f32[8,32,1024]{2,1,0:T(8,128)S(1)}, f32[8,32,1024]{2,1,0:T(8,128)}, u32[]{:S(2)}) copy-start(f32[8,32,1024]{2,1,0:T(8,128)} %get-tuple-element.61) | copy-start | bytes 3145732

commit v4 on v3

--- a/solution.py
+++ b/solution.py
@@ -249,132 +249,6 @@
     return block.reshape(block.shape[0] * block.shape[1], block.shape[2])
 
 
-def feed_forward_kernel(
-    attended, block_input, out_bias, gain1, bias1, up, bias_two, down, down_bias, gain2, bias2, cot,
-    out, d_first, d_first_half, g_up, g_down, g_up_bias, vecs,
-    hidden_half, hidden_all, act, slope, d_second_half, d_second_all, d_pre, gather_sems, *scatter_scratch,
-):
-    block_of, _ = ring_place()
-    shard = up.shape[2]
-    greet_ring()
-    first = block_input[...].astype(wide) + attended[...] + out_bias[...]
-    hidden, normed_one, inverse_one = layer_norm(first, gain1[...], bias1[...])
-    hidden_half[...] = hidden.astype(half)
-    gather = Gather(hidden_half, hidden_all, gather_sems.at[0], gather_sems.at[1])
-    scatter = Scatter(*scatter_scratch[:7])
-    gather.start()
-
-    @pl.loop(0, 4)
-    def _(s):
-        gather.ready(s)
-        k = ring_order(s)
-        chip = block_of(k) // 2
-        rows = pl.ds(chip * CHIP, CHIP)
-        for a in range(2):
-            pre = dot_nn(chip_rows(hidden_all, chip), up[a]) + bias_two[a, :, :shard]
-            value, gelu_slope = gelu_parts(pre)
-            act[rows, a * shard : (a + 1) * shard] = value.astype(half)
-            slope[rows, a * shard : (a + 1) * shard] = gelu_slope
-        term = dot_nn(act[rows], flat_rows(down)).astype(half)
-        scatter.y[pl.ds(2 * chip, 2)] = term.reshape(2, BLOCK, term.shape[1])
-        scatter.computed(k)
-
-    scatter.sides()
-    scatter.across()
-    gather.finish()
-    scatter.through()
-    second = hidden + scatter.result() + down_bias[...]
-    scatter.finish()
-    output, normed_two, inverse_two = layer_norm(second, gain2[...], bias2[...])
-    out[...] = output.astype(half)
-    grad = cot[...].astype(wide)
-    d_second = norm_back(grad, normed_two, inverse_two, gain2[...])
-    d_second_half[...] = d_second.astype(half)
-    gather = Gather(d_second_half, d_second_all, gather_sems.at[2], gather_sems.at[3])
-    scatter = Scatter(*scatter_scratch[7:])
-    gather.start()
-    vecs[pl.ds(3, 1)] = column_sum(d_second)
-    vecs[pl.ds(4, 1)] = column_sum(grad * normed_two)
-    vecs[pl.ds(5, 1)] = column_sum(grad)
-    vecs[pl.ds(6, 2)] = jnp.zeros((2, grad.shape[1]), wide)
-    g_up_bias[...] = jnp.zeros_like(g_up_bias)
-
-    @pl.loop(0, 4)
-    def _(s):
-        gather.ready(s)
-        k = ring_order(s)
-        chip = block_of(k) // 2
-        rows = pl.ds(chip * CHIP, CHIP)
-        grad_pre = dot_nt(chip_rows(d_second_all, chip), flat_rows(down)) * slope[rows]
-        g_up_bias[...] += column_sum(grad_pre)
-        grad_pre = grad_pre.astype(half)
-        d_pre[rows] = grad_pre
-        term = dot_nt(grad_pre[:, :shard], up[0]) + dot_nt(grad_pre[:, shard:], up[1])
-        term = term.astype(half)
-        scatter.y[pl.ds(2 * chip, 2)] = term.reshape(2, BLOCK, term.shape[1])
-        scatter.computed(k)
-
-    scatter.sides()
-    scatter.across()
-    gather.finish()
-    for a in range(2):
-        part = dot_tn(act[:, a * shard : (a + 1) * shard], flat_rows(d_second_all)).astype(half)
-        g_down[a] = part.reshape(PIECES, shard // PIECES, part.shape[1])
-    scatter.through()
-
-    @pl.loop(0, 4)
-    def _(i):
-        columns = pl.ds(pl.multiple_of(i * 256, 256), 256)
-        left = hidden_all[:, :, columns].reshape(RING * BLOCK, 256)
-        part = dot_tn(left, d_pre[...]).astype(half)
-        for a in range(2):
-            g_up[a, pl.ds(2 * i, 2)] = part[:, a * shard : (a + 1) * shard].reshape(2, BLOCK, shard)
-
-    d_hidden = d_second + scatter.result()
-    scatter.finish()
-    grad_first = norm_back(d_hidden, normed_one, inverse_one, gain1[...])
-    d_first[...] = grad_first
-    d_first_half[...] = grad_first.astype(half)
-    vecs[pl.ds(0, 1)] = column_sum(grad_first)
-    vecs[pl.ds(1, 1)] = column_sum(d_hidden * normed_one)
-    vecs[pl.ds(2, 1)] = column_sum(d_hidden)
-
-
-def feed_forward(attended, block_input, out_bias, gain1, bias1, up, bias_two, down, down_bias, gain2, bias2, cot):
-    rows, width = attended.shape
-    shard = up.shape[2]
-    hidden = 2 * shard
-    return pl.pallas_call(
-        feed_forward_kernel,
-        out_shape=(
-            jax.ShapeDtypeStruct((rows, width), half),
-            jax.ShapeDtypeStruct((rows, width), wide),
-            jax.ShapeDtypeStruct((rows, width), half),
-            jax.ShapeDtypeStruct((2, PIECES, width // PIECES, shard), half),
-            jax.ShapeDtypeStruct((2, PIECES, shard // PIECES, width), half),
-            jax.ShapeDtypeStruct((1, hidden), wide),
-            jax.ShapeDtypeStruct((8, width), wide),
-        ),
-        in_specs=[VMEM_WHOLE] * 12,
-        out_specs=(VMEM_WHOLE,) * 7,
-        scratch_shapes=[
-            pltpu.VMEM((rows, width), half),
-            pltpu.VMEM((RING, rows, width), half),
-            pltpu.VMEM((RING * rows, hidden), half),
-            pltpu.VMEM((RING * rows, hidden), wide),
-            pltpu.VMEM((rows, width), half),
-            pltpu.VMEM((RING, rows, width), half),
-            pltpu.VMEM((RING * rows, hidden), half),
-            pltpu.SemaphoreType.DMA((4, Gather.slots)),
-        ]
-        + Scatter.scratch(width)
-        + Scatter.scratch(width),
-        compiler_params=pltpu.CompilerParams(
-            collective_id=2, has_side_effects=True, vmem_limit_bytes=VMEM_BYTES
-        ),
-    )(attended, block_input, out_bias, gain1, bias1, up, bias_two, down, down_bias, gain2, bias2, cot)
-
-
 class PlaneSum:
     def __init__(self, land, full, send, recv):
         self.land, self.full, self.send, self.recv = land, full, send, recv
@@ -407,12 +281,11 @@
             place = self.full.at[self.dp]
             remote(place, place, self.send, self.recv, 14 + r, self.peer(0, r)[1]).start()
 
-    def result(self, out):
+    def result(self):
         for r in range(1, PIECES):
             piece = lax.rem(self.dp // 4 + r // 4, 2) * 4 + lax.rem(self.dp + 8 - r, 4)
             place = self.full.at[piece]
             remote(place, place, self.send, self.recv, 14 + r, (self.dp, self.t)).wait_recv()
-        out[...] = self.full[...].astype(wide)
         for n in range(22):
             place = self.land.at[0]
             remote(place, place, self.send, self.recv, n, (self.dp, self.t)).wait_send()
@@ -421,7 +294,6 @@
     def scratch(rows, width):
         return [
             pltpu.VMEM((15, rows, width), half),
-            pltpu.VMEM((PIECES, rows, width), half),
             pltpu.SemaphoreType.DMA((22,)),
             pltpu.SemaphoreType.DMA((22,)),
         ]
@@ -478,10 +350,6 @@
         return total
 
 
-def pair_of(shape):
-    return jax.ShapeDtypeStruct((2, *shape.shape), shape.dtype)
-
-
 def segment_column(ids, column):
     upper = lax.axis_index("tensor") // RING
     numbers = jnp.where(upper == 0, ids[pl.ds(0, 1)], ids[pl.ds(1, 1)])
@@ -489,18 +357,43 @@
     return numbers
 
 
-def attention_kernel(
-    x, ids, qkv, out_weight, up, down, bias,
-    attended, x_all, queries, keys, values, lse, context, qkv_two, out_two, up_two, down_two, bias_two,
-    column, gather_sems, trade_sems, *scatter_scratch,
+def put_term(scatter, chip, term):
+    scatter.y[pl.ds(2 * chip, 2)] = term.astype(half).reshape(2, BLOCK, term.shape[1])
+
+
+def layer_kernel(
+    x, ids, qkv, qv_bias, out_weight, out_bias, gain1, bias1, up, up_bias, down, down_bias, gain2, bias2, cot,
+    out, input_grad, up_full, down_full, late_full, small_out,
+    x_all, hidden_all, d_second_all, d_first_all, own_rows, hidden, normed_one, d_second,
+    queries, keys, values, lse, context, column,
+    qkv_two, qv_bias_two, out_two, up_two, up_bias_two, down_two,
+    act, slope, d_pre, g_up, g_down, g_up_bias, vecs,
+    d_keys, d_values, d_qkv, query_sum, late,
+    gather_sems, trade_sems, *scratch,
 ):
     block_of, device_of = ring_place()
-    across_z = (lax.axis_index("dp"), lax.rem(lax.axis_index("tensor") + RING, 2 * RING))
-    greet((device_of(1), device_of(-1), device_of(0, True), across_z))
-    gather = Gather(x, x_all, gather_sems.at[0], gather_sems.at[1])
-    scatter = Scatter(*scatter_scratch)
+    shard = up.shape[1]
+    group = 3 * HEAD_DIM
+    scatters = [Scatter(*scratch[7 * i : 7 * i + 7]) for i in range(4)]
+    scratch = scratch[28:]
+    small, scratch = SmallSum(*scratch[:5]), scratch[5:]
+    up_plane, down_plane, late_plane = (
+        PlaneSum(scratch[3 * i], full, scratch[3 * i + 1], scratch[3 * i + 2])
+        for i, full in enumerate((up_full, down_full, late_full))
+    )
+
+    def gather_of(i, src, dst):
+        return Gather(src, dst, gather_sems.at[2 * i], gather_sems.at[2 * i + 1])
+
+    greet(PlaneSum.peers() + SmallSum.peers())
+
+    gather = gather_of(0, x, x_all)
     gather.start()
-    pairs = ((bias, bias_two), (qkv, qkv_two), (out_weight, out_two), (up, up_two), (down, down_two))
+    across_z = PlaneSum.peer(1, 0)[1]
+    pairs = (
+        (qv_bias, qv_bias_two), (qkv, qkv_two), (out_weight, out_two),
+        (up_bias, up_bias_two), (up, up_two), (down, down_two),
+    )
     trades = [
         remote(mine, two.at[1], trade_sems.at[0], trade_sems.at[1], slot, across_z)
         for slot, (mine, two) in enumerate(pairs)
@@ -510,15 +403,14 @@
     for mine, two in pairs:
         two[0] = mine[...]
     numbers = segment_column(ids, column)
-    ff = up.shape[1]
 
     def project(a, chip):
         rows = pl.ds(chip * CHIP, CHIP)
-        product = dot_nt(chip_rows(x_all, chip), qkv_two[a].reshape(3 * HEAD_DIM, x.shape[1]))
+        product = dot_nt(chip_rows(x_all, chip), qkv_two[a].reshape(group, x.shape[1]))
         parts = [product[:, i * HEAD_DIM : (i + 1) * HEAD_DIM] for i in range(3)]
-        queries[a, rows] = (parts[0] + bias_two[a, :, ff : ff + HEAD_DIM]).astype(half)
+        queries[a, rows] = (parts[0] + qv_bias_two[a, 0:1]).astype(half)
         keys[a, rows] = parts[1].astype(half)
-        values[a, rows] = (parts[2] + bias_two[a, :, ff + HEAD_DIM : ff + 2 * HEAD_DIM]).astype(half)
+        values[a, rows] = (parts[2] + qv_bias_two[a, 1:2]).astype(half)
 
     @pl.loop(0, 4)
     def _(s):
@@ -533,6 +425,7 @@
         project(1, chip)
 
     trades[2].wait_recv()
+    scatter = scatters[0]
 
     @pl.loop(0, 4)
     def _(i):
@@ -549,8 +442,7 @@
             lse[a, rows] = top + jnp.log(mass)
             probs = (weights * (1.0 / mass)).astype(half)
             context[rows, a * HEAD_DIM : (a + 1) * HEAD_DIM] = dot_nn(probs, values[a]).astype(half)
-        term = dot_nn(context[rows], flat_rows(out_two)).astype(half)
-        scatter.y[pl.ds(2 * chip, 2)] = term.reshape(2, BLOCK, term.shape[1])
+        put_term(scatter, chip, dot_nn(context[rows], flat_rows(out_two)))
         scatter.computed(k)
 
         @pl.when(i == 1)
@@ -558,72 +450,103 @@
             scatter.across()
 
     scatter.sides()
-    gather.finish()
     scatter.through()
-    attended[...] = scatter.result()
-    scatter.finish()
-    trades[3].wait_recv()
-    trades[4].wait_recv()
-    for trade in trades:
-        trade.wait_send()
-
-
-def attention(x, ids, qkv, out_weight, up, down, bias):
-    rows, width = x.shape
-    tokens = RING * rows
-    head = jax.ShapeDtypeStruct((2, tokens, HEAD_DIM), half)
-    return pl.pallas_call(
-        attention_kernel,
-        out_shape=(
-            jax.ShapeDtypeStruct((rows, width), wide),
-            jax.ShapeDtypeStruct((RING, rows, width), half),
-            head,
-            head,
-            head,
-            jax.ShapeDtypeStruct((2, tokens, 1), wide),
-            jax.ShapeDtypeStruct((tokens, 2 * HEAD_DIM), half),
-            pair_of(qkv),
-            pair_of(out_weight),
-            pair_of(up),
-            pair_of(down),
-            pair_of(bias),
-        ),
-        in_specs=[VMEM_WHOLE] * 7,
-        out_specs=(VMEM_WHOLE,) * 12,
-        scratch_shapes=[
-            pltpu.VMEM((tokens, 128), jnp.int32),
-            pltpu.SemaphoreType.DMA((2, Gather.slots)),
-            pltpu.SemaphoreType.DMA((2, 5)),
-        ]
-        + Scatter.scratch(width),
-        compiler_params=pltpu.CompilerParams(
-            collective_id=0, has_side_effects=True, vmem_limit_bytes=VMEM_BYTES
-        ),
-    )(x, ids, qkv, out_weight, up, down, bias)
-
-
-def attention_back_kernel(
-    d_first, d_first_half, x_all, ids, queries, keys, values, lse, context, qkv_two, out_two,
-    g_up, g_down, g_up_bias, vecs,
-    input_grad, up_sum, down_sum, late_sum, small_out,
-    d_first_all, column, d_keys, d_values, d_qkv, query_sum, late, gather_sems, *scratch,
-):
-    block_of, _ = ring_place()
-    scatter, scratch = Scatter(*scratch[:7]), scratch[7:]
-    small, scratch = SmallSum(*scratch[:5]), scratch[5:]
-    early = [(PlaneSum(*scratch[:4]), g_up, up_sum), (PlaneSum(*scratch[4:8]), g_down, down_sum)]
-    last = PlaneSum(*scratch[8:])
-    greet(PlaneSum.peers() + SmallSum.peers())
-    gather = Gather(d_first_half, d_first_all, gather_sems.at[0], gather_sems.at[1])
+    first = x[...].astype(wide) + scatter.result() + out_bias[...]
+    normal, normed, inverse_one = layer_norm(first, gain1[...], bias1[...])
+    own_rows[0] = normal.astype(half)
+
+    gather = gather_of(1, own_rows.at[0], hidden_all)
     gather.start()
+    hidden[...] = normal
+    normed_one[...] = normed
+    scatter = scatters[1]
+    for trade in trades[3:]:
+        trade.wait_recv()
+
+    @pl.loop(0, 4)
+    def _(s):
+        @pl.when(s == 3)
+        def _():
+            scatter.sides()
+
+        gather.ready(s)
+        k = ring_order(s)
+        chip = block_of(k) // 2
+        rows = pl.ds(chip * CHIP, CHIP)
+        for a in range(2):
+            pre = dot_nn(chip_rows(hidden_all, chip), up_two[a]) + up_bias_two[a]
+            value, gelu_slope = gelu_parts(pre)
+            act[rows, a * shard : (a + 1) * shard] = value.astype(half)
+            slope[rows, a * shard : (a + 1) * shard] = gelu_slope
+        put_term(scatter, chip, dot_nn(act[rows], flat_rows(down_two)))
+        scatter.computed(k)
+
+    scatter.across()
+    scatter.through()
+    second = hidden[...] + scatter.result() + down_bias[...]
+    output, normed_two, inverse_two = layer_norm(second, gain2[...], bias2[...])
+    grad = cot[...].astype(wide)
+    grad_second = norm_back(grad, normed_two, inverse_two, gain2[...])
+    own_rows[1] = grad_second.astype(half)
+
+    gather = gather_of(2, own_rows.at[1], d_second_all)
+    gather.start()
+    d_second[...] = grad_second
+    out[...] = output.astype(half)
+    vecs[pl.ds(3, 1)] = column_sum(grad_second)
+    vecs[pl.ds(4, 1)] = column_sum(grad * normed_two)
+    vecs[pl.ds(5, 1)] = column_sum(grad)
+    vecs[pl.ds(6, 2)] = jnp.zeros((2, grad.shape[1]), wide)
+    g_up_bias[...] = jnp.zeros_like(g_up_bias)
+    scatter = scatters[2]
+
+    @pl.loop(0, 4)
+    def _(s):
+        @pl.when(s == 3)
+        def _():
+            scatter.sides()
+
+        gather.ready(s)
+        k = ring_order(s)
+        chip = block_of(k) // 2
+        rows = pl.ds(chip * CHIP, CHIP)
+        grad_pre = dot_nt(chip_rows(d_second_all, chip), flat_rows(down_two)) * slope[rows]
+        g_up_bias[...] += column_sum(grad_pre)
+        grad_pre = grad_pre.astype(half)
+        d_pre[rows] = grad_pre
+        put_term(scatter, chip, dot_nt(grad_pre[:, :shard], up_two[0]) + dot_nt(grad_pre[:, shard:], up_two[1]))
+        scatter.computed(k)
+
+    scatter.across()
+    for a in range(2):
+        part = dot_tn(act[:, a * shard : (a + 1) * shard], flat_rows(d_second_all)).astype(half)
+        g_down[a] = part.reshape(PIECES, shard // PIECES, part.shape[1])
+    down_plane.scatter(g_down)
+    scatter.through()
+
+    @pl.loop(0, 4)
+    def _(i):
+        columns = pl.ds(pl.multiple_of(i * 256, 256), 256)
+        left = hidden_all[:, :, columns].reshape(RING * BLOCK, 256)
+        part = dot_tn(left, d_pre[...]).astype(half)
+        for a in range(2):
+            g_up[a, pl.ds(2 * i, 2)] = part[:, a * shard : (a + 1) * shard].reshape(2, BLOCK, shard)
+
+    d_hidden = d_second[...] + scatter.result()
+    grad_first = norm_back(d_hidden, normed_one[...], inverse_one, gain1[...])
+    own_rows[2] = grad_first.astype(half)
+
+    gather = gather_of(3, own_rows.at[2], d_first_all)
+    gather.start()
+    up_plane.scatter(g_up)
+    vecs[pl.ds(0, 1)] = column_sum(grad_first)
+    vecs[pl.ds(1, 1)] = column_sum(d_hidden * normed_one[...])
+    vecs[pl.ds(2, 1)] = column_sum(d_hidden)
+    hidden[...] = grad_first
     small.start(vecs)
-    for plane, grads, _ in early:
-        plane.scatter(grads)
-    numbers = segment_column(ids, column)
     d_keys[...] = jnp.zeros_like(d_keys)
     d_values[...] = jnp.zeros_like(d_values)
     query_sum[...] = jnp.zeros_like(query_sum)
-    group = 3 * HEAD_DIM
 
     @pl.loop(0, 4)
     def _(s):
@@ -646,9 +569,7 @@
             d_qkv[rows, a * group : a * group + HEAD_DIM] = d_query.astype(half)
             d_keys[a] += dot_tn(query, d_scores)
 
-    gather.finish()
     shard_rows = []
-    shard = g_up_bias.shape[1] // 2
     for a in range(2):
         at = a * group + HEAD_DIM
         d_qkv[:, at : at + HEAD_DIM] = jnp.transpose(d_keys[a].astype(half))
@@ -673,16 +594,16 @@
         late[a, pl.ds(0, 6)] = part.reshape(6, piece, part.shape[1])
         part = grad_out[a * HEAD_DIM : (a + 1) * HEAD_DIM]
         late[a, pl.ds(6, 2)] = part.reshape(2, piece, part.shape[1])
-    last.scatter(late)
+    late_plane.scatter(late)
     small.plane(vecs, shard_rows)
+    scatter = scatters[3]
 
     @pl.loop(0, 4)
     def _(i):
         k = ring_order(3 - i)
         chip = block_of(k) // 2
-        weight = qkv_two[...].reshape(2 * group, d_first.shape[1])
-        term = dot_nn(d_qkv[pl.ds(chip * CHIP, CHIP)], weight).astype(half)
-        scatter.y[pl.ds(2 * chip, 2)] = term.reshape(2, BLOCK, term.shape[1])
+        weight = qkv_two[...].reshape(2 * group, x.shape[1])
+        put_term(scatter, chip, dot_nn(d_qkv[pl.ds(chip * CHIP, CHIP)], weight))
         scatter.computed(k)
 
         @pl.when(i == 1)
@@ -690,52 +611,116 @@
             scatter.across()
 
     scatter.sides()
+    down_plane.share(g_down)
     scatter.through()
-    for plane, grads, _ in early:
-        plane.share(grads)
-    input_grad[...] = (d_first[...] + scatter.result()).astype(half)
-    scatter.finish()
-    last.share(late)
-    for plane, _, total in early:
-        plane.result(total)
-    last.result(late_sum)
+    up_plane.share(g_up)
+    input_grad[...] = (hidden[...] + scatter.result()).astype(half)
+    late_plane.share(late)
+    for plane in (down_plane, up_plane, late_plane):
+        plane.result()
     small_out[...] = small.result()
-
-
-def attention_back(d_first, d_first_half, x_all, ids, heads, lse, context, qkv_two, out_two, g_up, g_down, g_up_bias, vecs):
-    rows, width = d_first.shape
+    for i, (src, dst) in enumerate(((x, x_all), (x, hidden_all), (x, d_second_all), (x, d_first_all))):
+        gather_of(i, src, dst).finish()
+    for scatter in scatters:
+        scatter.finish()
+    for trade in trades:
+        trade.wait_send()
+
+
+def layer(x, ids, qkv, qv_bias, out_weight, out_bias, gain1, bias1, up, up_bias, down, down_bias, gain2, bias2, cot):
+    rows, width = x.shape
     tokens = RING * rows
+    shard = up.shape[1]
     late = (PIECES, 4 * HEAD_DIM // PIECES, width)
+    up_pieces = (PIECES, width // PIECES, shard)
+    down_pieces = (PIECES, shard // PIECES, width)
+    gathered = pltpu.VMEM((RING, rows, width), half)
+    full_rows = pltpu.VMEM((rows, width), wide)
+    head = pltpu.VMEM((2, tokens, HEAD_DIM), half)
+    ff = pltpu.VMEM((tokens, 2 * shard), half)
+    turned = pltpu.VMEM((2, HEAD_DIM, tokens), wide)
+    scratch = [gathered] * 4 + [pltpu.VMEM((3, rows, width), half)] + [full_rows] * 3
+    scratch += [head] * 3
+    scratch += [
+        pltpu.VMEM((2, tokens, 1), wide),
+        pltpu.VMEM((tokens, 2 * HEAD_DIM), half),
+        pltpu.VMEM((tokens, 128), jnp.int32),
+    ]
+    scratch += [pltpu.VMEM((2, *arr.shape), arr.dtype) for arr in (qkv, qv_bias, out_weight, up, up_bias, down)]
+    scratch += [ff, pltpu.VMEM((tokens, 2 * shard), wide), ff]
+    scratch += [pltpu.VMEM((2, *up_pieces), half), pltpu.VMEM((2, *down_pieces), half)]
+    scratch += [pltpu.VMEM((1, 2 * shard), wide), pltpu.VMEM((8, width), wide)]
+    scratch += [turned, turned, pltpu.VMEM((tokens, 6 * HEAD_DIM), half), pltpu.VMEM((2, 1, HEAD_DIM), wide)]
+    scratch += [pltpu.VMEM((2, *late), half)]
+    scratch += [pltpu.SemaphoreType.DMA((8, Gather.slots)), pltpu.SemaphoreType.DMA((2, 6))]
+    scratch += Scatter.scratch(width) * 4 + SmallSum.scratch
+    for pieces in (up_pieces, down_pieces, late):
+        scratch += PlaneSum.scratch(*pieces[1:])
     return pl.pallas_call(
-        attention_back_kernel,
+        layer_kernel,
         out_shape=(
             jax.ShapeDtypeStruct((rows, width), half),
-            jax.ShapeDtypeStruct(g_up.shape[1:], wide),
-            jax.ShapeDtypeStruct(g_down.shape[1:], wide),
-            jax.ShapeDtypeStruct(late, wide),
-            jax.ShapeDtypeStruct(vecs.shape, wide),
+            jax.ShapeDtypeStruct((rows, width), half),
+            jax.ShapeDtypeStruct(up_pieces, half),
+            jax.ShapeDtypeStruct(down_pieces, half),
+            jax.ShapeDtypeStruct(late, half),
+            jax.ShapeDtypeStruct((8, width), wide),
         ),
         in_specs=[VMEM_WHOLE] * 15,
-        out_specs=(VMEM_WHOLE,) * 5,
-        scratch_shapes=[
-            pltpu.VMEM((RING, rows, width), half),
-            pltpu.VMEM((tokens, 128), jnp.int32),
-            pltpu.VMEM((2, HEAD_DIM, tokens), wide),
-            pltpu.VMEM((2, HEAD_DIM, tokens), wide),
-            pltpu.VMEM((tokens, 6 * HEAD_DIM), half),
-            pltpu.VMEM((2, 1, HEAD_DIM), wide),
-            pltpu.VMEM((2, *late), half),
-            pltpu.SemaphoreType.DMA((2, Gather.slots)),
-        ]
-        + Scatter.scratch(width)
-        + SmallSum.scratch
-        + PlaneSum.scratch(*g_up.shape[2:])
-        + PlaneSum.scratch(*g_down.shape[2:])
-        + PlaneSum.scratch(*late[1:]),
+        out_specs=(VMEM_WHOLE,) * 6,
+        scratch_shapes=scratch,
         compiler_params=pltpu.CompilerParams(
-            collective_id=1, has_side_effects=True, vmem_limit_bytes=VMEM_BYTES
+            collective_id=0, has_side_effects=True, vmem_limit_bytes=VMEM_BYTES
         ),
-    )(d_first, d_first_half, x_all, ids, *heads, lse, context, qkv_two, out_two, g_up, g_down, g_up_bias, vecs)
+    )(x, ids, qkv, qv_bias, out_weight, out_bias, gain1, bias1, up, up_bias, down, down_bias, gain2, bias2, cot)
+
+
+def outputs_kernel(
+    out_in, grad_in, up_full, down_full, late_full, small,
+    out, input_grad, g_qkv, g_qv_bias, g_out, g_out_bias, g_gain1, g_bias1, g_up, g_up_bias, g_down, g_down_bias,
+    g_gain2, g_bias2,
+):
+    out[...] = out_in[...]
+    input_grad[...] = grad_in[...]
+    g_up[...] = flat_rows(up_full).astype(wide)
+    g_down[...] = flat_rows(down_full).astype(wide)
+    late = flat_rows(late_full).astype(wide).reshape(4, HEAD_DIM, out.shape[1])
+    g_qkv[...] = late[:3]
+    g_out[...] = late[3]
+    for i, ref in enumerate((g_out_bias, g_gain1, g_bias1, g_down_bias, g_gain2, g_bias2)):
+        ref[...] = small[pl.ds(i, 1)]
+    ff = g_up_bias.shape[1]
+    g_up_bias[...] = small[pl.ds(6, 1), 0:ff]
+    for i in range(2):
+        g_qv_bias[pl.ds(i, 1)] = small[pl.ds(6, 1), ff + i * HEAD_DIM : ff + (i + 1) * HEAD_DIM]
+
+
+def write_outputs(results):
+    rows, width = results[0].shape
+    ff = results[2].shape[2]
+    vector = jax.ShapeDtypeStruct((1, width), wide)
+    block = jax.ShapeDtypeStruct((rows, width), half)
+    return pl.pallas_call(
+        outputs_kernel,
+        out_shape=(
+            block,
+            block,
+            jax.ShapeDtypeStruct((3, HEAD_DIM, width), wide),
+            jax.ShapeDtypeStruct((2, HEAD_DIM), wide),
+            jax.ShapeDtypeStruct((HEAD_DIM, width), wide),
+            vector,
+            vector,
+            vector,
+            jax.ShapeDtypeStruct((width, ff), wide),
+            jax.ShapeDtypeStruct((1, ff), wide),
+            jax.ShapeDtypeStruct((ff, width), wide),
+            vector,
+            vector,
+            vector,
+        ),
+        in_specs=[VMEM_WHOLE] * 6,
+        out_specs=(VMEM_WHOLE,) * 14,
+    )(*results)
 
 
 def row(vector):
@@ -759,35 +744,18 @@
     norm2_bias,
     cotangent,
 ):
-    bias = row(jnp.concatenate([up_bias, qv_bias.reshape(-1)]))
-    attended, x_all, queries, keys, values, lse, context, qkv_two, out_two, up_two, down_two, bias_two = attention(
-        block_input, segment_ids, jnp.swapaxes(qkv_weight, 1, 2), out_weight, up_weight, down_weight, bias
+    results = layer(
+        block_input, segment_ids, jnp.swapaxes(qkv_weight, 1, 2), qv_bias, out_weight, row(out_bias),
+        row(norm1_gain), row(norm1_bias), up_weight, row(up_bias), down_weight, row(down_bias),
+        row(norm2_gain), row(norm2_bias), cotangent,
     )
-    output, d_first, d_first_half, g_up, g_down, g_up_bias, vecs = feed_forward(
-        attended, block_input, row(out_bias), row(norm1_gain), row(norm1_bias), up_two, bias_two,
-        down_two, row(down_bias), row(norm2_gain), row(norm2_bias), cotangent,
+    out, input_grad, g_qkv, g_qv_bias, g_out, *vectors = write_outputs(results)
+    g_out_bias, g_gain1, g_bias1, g_up, g_up_bias, g_down, g_down_bias, g_gain2, g_bias2 = (
+        arr.reshape(-1) if arr.shape[0] == 1 else arr for arr in vectors
     )
-    input_grad, up_sum, down_sum, late_sum, small = attention_back(
-        d_first, d_first_half, x_all, segment_ids, (queries, keys, values), lse, context, qkv_two, out_two,
-        g_up, g_down, g_up_bias, vecs,
-    )
-    ff = up_bias.shape[0]
-    late_sum = late_sum.reshape(4, HEAD_DIM, -1)
     return (
-        output,
-        input_grad,
-        jnp.swapaxes(late_sum[:3], 1, 2),
-        small[6, ff : ff + 2 * HEAD_DIM].reshape(2, HEAD_DIM),
-        late_sum[3],
-        small[0],
-        small[1],
-        small[2],
-        up_sum.reshape(up_weight.shape),
-        small[6, :ff],
-        down_sum.reshape(down_weight.shape),
-        small[3],
-        small[4],
-        small[5],
+        out, input_grad, jnp.swapaxes(g_qkv, 1, 2), g_qv_bias, g_out, g_out_bias, g_gain1, g_bias1,
+        g_up, g_up_bias, g_down, g_down_bias, g_gain2, g_bias2,
     )
 
 

time: 194 us -> 157 us (0.81)
  Pallas kernels: 181 us -> 155 us
  local copies, waits for them, and re-layouts: 11.2 us -> 0 us
    pallas_call x3 -> x2, Pallas kernels: 181 us -> 155 us  [the longest x1 151 us: layer(): pl.pallas_call(layer_kernel, out_shape=(jax.ShapeDtypeStruct((rows, width...]
    slice x5 -> x0, local copies, waits for them, and re-layouts: 5.84 us -> none  [the longest x1 2.2 us: per_device(): late_sum[:3]]
    unnamed x14 -> x0, local copies, waits for them, and re-layouts: 3.37 us -> none
where the time goes in v4:
time: 157 us; the launch traced here: 155 us
  Pallas kernels  155 us (99%)
    pallas_call x1, Pallas kernels, layer(): pl.pallas_call(layer_kernel, out_shape=(jax.ShapeDtypeStruct((rows, width...  151 us
    pallas_call x1, Pallas kernels, write_outputs(): pl.pallas_call(outputs_kernel, out_shape=(block, block, jax.ShapeDtypeStr...  3.45 us

profile of v4, /device:TPU:0, one launch (start us, length us, event | category | flops | bytes accessed | tf_op | source)
XLA Modules:
  0.0 155.3 jit_solution(9796381307329164014)
XLA Ops:
  0.7 151.1 %shard_map.254 = (bf16[128,1024]{1,0:T(8,128)(2,1)}, bf16[128,1024]{1,0:T(8,128)(2,1)}, bf16[8,128,256]{2,1,0:T(8,128)(2,1)}, bf16[8,32,1024]{2,1,0:T(8,128)(2,1...) custom-call(bf16[128,1024]{1,0:T(8,128)(2,1)} %x.1, s32[2,1024]{1,0:T(2,128)} %ids.1, bf16[3,64,1024]{2,1,0:T(8,128)(2,1)} %bitcast.16, ...), custom_call_target="tpu_custom_call" | custom-call | tf_op jit(solution)/shard_map/pallas_call | solution.py:659
  151.7 3.4 %shard_map.255 = (bf16[128,1024]{1,0:T(8,128)(2,1)}, bf16[128,1024]{1,0:T(8,128)(2,1)}, f32[3,64,1024]{2,1,0:T(8,128)}, f32[2,64]{1,0:T(2,128)}, f32[64,1024]{1,...) custom-call(bf16[128,1024]{1,0:T(8,128)(2,1)} %get-tuple-element.34., ...), custom_call_target="tpu_custom_call" | custom-call | tf_op jit(solution)/shard_map/pallas_call | solution.py:703

commit v5 on v4

--- a/solution.py
+++ b/solution.py
@@ -265,17 +265,7 @@
     def peers():
         return [PlaneSum.peer(n // PIECES, n % PIECES)[1] for n in range(1, 2 * PIECES)]
 
-    def scatter(self, grads):
-        for n in range(1, 2 * PIECES):
-            piece, device = self.peer(n // PIECES, n % PIECES)
-            remote(grads.at[n // PIECES, piece], self.land.at[n - 1], self.send, self.recv, n - 1, device).start()
-
-    def share(self, grads):
-        total = grads[0, self.dp].astype(wide)
-        for n in range(15):
-            place = self.land.at[n]
-            remote(place, place, self.send, self.recv, n, (self.dp, self.t)).wait_recv()
-            total += self.land[n].astype(wide)
+    def hand_out(self, total):
         self.full[pl.ds(self.dp, 1)] = total.astype(half).reshape(1, *total.shape)
         for r in range(1, PIECES):
             place = self.full.at[self.dp]
@@ -286,14 +276,83 @@
             piece = lax.rem(self.dp // 4 + r // 4, 2) * 4 + lax.rem(self.dp + 8 - r, 4)
             place = self.full.at[piece]
             remote(place, place, self.send, self.recv, 14 + r, (self.dp, self.t)).wait_recv()
-        for n in range(22):
+        self.sent()
+
+
+class TwoLevelSum(PlaneSum):
+    def __init__(self, z_first, near, mid, far, full, send, recv):
+        super().__init__(far, full, send, recv)
+        self.z_first, self.near, self.mid = z_first, near, mid
+
+    @staticmethod
+    def peer_z(n):
+        dp, t = lax.axis_index("dp"), lax.axis_index("tensor")
+        z_lo = lax.rem(dp // 4 + n % 2, 2)
+        return z_lo, (z_lo * 4 + lax.rem(dp, 4), lax.rem(t + (n // 2) * RING, 2 * RING))
+
+    @staticmethod
+    def peer_y(r):
+        dp, t = lax.axis_index("dp"), lax.axis_index("tensor")
+        y = lax.rem(dp + r, 4)
+        return y, ((dp // 4) * 4 + y, t)
+
+    def here(self):
+        return (self.dp, self.t)
+
+    def scatter(self, grads):
+        for n in range(1, 4):
+            if self.z_first:
+                z_lo, device = self.peer_z(n)
+                remote(grads.at[n // 2, pl.ds(4 * z_lo, 4)], self.near.at[n - 1], self.send, self.recv, n - 1, device).start()
+            else:
+                y, device = self.peer_y(n)
+                for m in range(4):
+                    source = grads.at[m // 2, 4 * (m % 2) + y]
+                    remote(source, self.near.at[n - 1, m], self.send, self.recv, 4 * (n - 1) + m, device).start()
+
+    def turn(self, grads):
+        count = 3 if self.z_first else 12
+        for slot in range(count):
+            place = self.near.at[slot] if self.z_first else self.near.at[slot // 4, slot % 4]
+            remote(place, place, self.send, self.recv, slot, self.here()).wait_recv()
+        y, z_lo = lax.rem(self.dp, 4), self.dp // 4
+        for m in range(4):
+            mine = grads[0, 4 * z_lo + m] if self.z_first else grads[m // 2, 4 * (m % 2) + y]
+            total = mine.astype(wide)
+            for n in range(3):
+                total += self.near[n, m].astype(wide)
+            self.mid[m] = total.astype(half)
+        for n in range(1, 4):
+            if self.z_first:
+                at, device = self.peer_y(n)
+            else:
+                z_lo_there, device = self.peer_z(n)
+                at = 2 * (n // 2) + z_lo_there
+            remote(self.mid.at[at], self.land.at[n - 1], self.send, self.recv, 11 + n, device).start()
+
+    def share(self):
+        at = lax.rem(self.dp, 4) if self.z_first else self.dp // 4
+        total = self.mid[at].astype(wide)
+        for n in range(3):
+            place = self.land.at[n]
+            remote(place, place, self.send, self.recv, 12 + n, self.here()).wait_recv()
+            total += self.land[n].astype(wide)
+        self.hand_out(total)
+
+    def sent(self):
+        for slot in range(3 if self.z_first else 12):
+            place = self.near.at[0] if self.z_first else self.near.at[0, 0]
+            remote(place, place, self.send, self.recv, slot, self.here()).wait_send()
+        for slot in range(12, 22):
             place = self.land.at[0]
-            remote(place, place, self.send, self.recv, n, (self.dp, self.t)).wait_send()
+            remote(place, place, self.send, self.recv, slot, self.here()).wait_send()
 
     @staticmethod
     def scratch(rows, width):
         return [
-            pltpu.VMEM((15, rows, width), half),
+            pltpu.VMEM((3, 4, rows, width), half),
+            pltpu.VMEM((4, rows, width), half),
+            pltpu.VMEM((3, rows, width), half),
             pltpu.SemaphoreType.DMA((22,)),
             pltpu.SemaphoreType.DMA((22,)),
         ]
@@ -301,11 +360,11 @@
 
 class SmallSum:
     scratch = [
-        pltpu.VMEM((8, 8, 1024), wide),
-        pltpu.VMEM((2, 8, 1024), wide),
-        pltpu.VMEM((15, 8, 1024), wide),
-        pltpu.SemaphoreType.DMA((22,)),
-        pltpu.SemaphoreType.DMA((22,)),
+        pltpu.VMEM((RING, 8, 128), wide),
+        pltpu.VMEM((2, 16, 128), wide),
+        pltpu.VMEM((15, 16, 128), wide),
+        pltpu.SemaphoreType.DMA((29,)),
+        pltpu.SemaphoreType.DMA((29,)),
     ]
 
     def __init__(self, line, base, land, send, recv):
@@ -321,33 +380,45 @@
     def peers():
         return [SmallSum.line_peer(r) for r in range(1, RING)]
 
+    def slab(self, ref, r):
+        return ref.at[:, pl.ds(pl.multiple_of(lax.rem(self.t + r, RING) * 128, 128), 128)]
+
+    def arrived(self, place, slot):
+        remote(place, place, self.send, self.recv, slot, (self.dp, self.t)).wait_recv()
+
     def start(self, vecs):
         for r in range(1, RING):
-            remote(vecs, self.line.at[r], self.send, self.recv, 14 + r, self.line_peer(r)).start()
-
-    def plane(self, vecs, shard_rows):
-        total = vecs[...]
+            remote(self.slab(vecs, r), self.line.at[r], self.send, self.recv, 14 + r, self.line_peer(r)).start()
+
+    def plane(self, vecs, shards):
+        total = self.slab(vecs, 0)[...]
         for r in range(1, RING):
-            place = self.line.at[r]
-            remote(place, place, self.send, self.recv, 14 + r, (self.dp, self.t)).wait_recv()
+            self.arrived(self.line.at[r], 14 + r)
             total += self.line[r]
-        row = lax.broadcasted_iota(jnp.int32, total.shape, 0)
         for a in range(2):
-            self.base[a] = jnp.where(row == 6, jnp.broadcast_to(shard_rows[a], total.shape), total)
+            self.base[a, 0:8] = total
+            self.base[a, 8:16] = shards[a]
         for n in range(1, 2 * PIECES):
             _, device = PlaneSum.peer(n // PIECES, n % PIECES)
             remote(self.base.at[n // PIECES], self.land.at[n - 1], self.send, self.recv, n - 1, device).start()
 
-    def result(self):
+    def share(self, sums, shard_sums):
         total = self.base[0]
         for n in range(15):
-            place = self.land.at[n]
-            remote(place, place, self.send, self.recv, n, (self.dp, self.t)).wait_recv()
+            self.arrived(self.land.at[n], n)
             total += self.land[n]
-        for n in range(22):
-            place = self.land.at[0]
-            remote(place, place, self.send, self.recv, n, (self.dp, self.t)).wait_send()
-        return total
+        mine = self.slab(sums, 0)
+        mine[...] = total[0:8]
+        shard_sums[...] = total[8:16]
+        for r in range(1, RING):
+            remote(mine, mine, self.send, self.recv, 21 + r, self.line_peer(r)).start()
+
+    def finish(self, sums):
+        for r in range(1, RING):
+            self.arrived(self.slab(sums, RING - r), 21 + r)
+        for slot in range(29):
+            place = self.land.at[0] if slot < 15 else self.line.at[0]
+            remote(place, place, self.send, self.recv, slot, (self.dp, self.t)).wait_send()
 
 
 def segment_column(ids, column):
@@ -363,12 +434,12 @@
 
 def layer_kernel(
     x, ids, qkv, qv_bias, out_weight, out_bias, gain1, bias1, up, up_bias, down, down_bias, gain2, bias2, cot,
-    out, input_grad, up_full, down_full, late_full, small_out,
+    out, input_grad, up_full, down_full, query_full, pair_full, out_full, sums, shard_sums,
     x_all, hidden_all, d_second_all, d_first_all, own_rows, hidden, normed_one, d_second,
     queries, keys, values, lse, context, column,
     qkv_two, qv_bias_two, out_two, up_two, up_bias_two, down_two,
     act, slope, d_pre, g_up, g_down, g_up_bias, vecs,
-    d_keys, d_values, d_qkv, query_sum, late,
+    d_keys, d_values, d_qkv, query_sum, g_query, g_pair, g_out,
     gather_sems, trade_sems, *scratch,
 ):
     block_of, device_of = ring_place()
@@ -377,10 +448,11 @@
     scatters = [Scatter(*scratch[7 * i : 7 * i + 7]) for i in range(4)]
     scratch = scratch[28:]
     small, scratch = SmallSum(*scratch[:5]), scratch[5:]
-    up_plane, down_plane, late_plane = (
-        PlaneSum(scratch[3 * i], full, scratch[3 * i + 1], scratch[3 * i + 2])
-        for i, full in enumerate((up_full, down_full, late_full))
-    )
+    up_plane = TwoLevelSum(False, *scratch[0:3], up_full, *scratch[3:5])
+    down_plane = TwoLevelSum(True, *scratch[5:8], down_full, *scratch[8:10])
+    query_plane = TwoLevelSum(False, *scratch[10:13], query_full, *scratch[13:15])
+    pair_plane = TwoLevelSum(True, *scratch[15:18], pair_full, *scratch[18:20])
+    out_plane = TwoLevelSum(True, *scratch[20:23], out_full, *scratch[23:25])
 
     def gather_of(i, src, dst):
         return Gather(src, dst, gather_sems.at[2 * i], gather_sems.at[2 * i + 1])
@@ -550,7 +622,16 @@
 
     @pl.loop(0, 4)
     def _(s):
+        @pl.when(s == 2)
+        def _():
+            down_plane.turn(g_down)
+
         gather.ready(s)
+
+        @pl.when(s == 3)
+        def _():
+            up_plane.turn(g_up)
+
         chip = block_of(ring_order(s)) // 2
         rows = pl.ds(chip * CHIP, CHIP)
         d_context = dot_nt(chip_rows(d_first_all, chip), flat_rows(out_two)).astype(half)
@@ -569,33 +650,37 @@
             d_qkv[rows, a * group : a * group + HEAD_DIM] = d_query.astype(half)
             d_keys[a] += dot_tn(query, d_scores)
 
-    shard_rows = []
+    down_plane.share()
+    shards = []
+    for a in range(2):
+        part = dot_tn(d_qkv[:, a * group : a * group + HEAD_DIM], flat_rows(x_all)).astype(half)
+        g_query[a] = part.reshape(g_query.shape[1:])
+    query_plane.scatter(g_query)
     for a in range(2):
         at = a * group + HEAD_DIM
         d_qkv[:, at : at + HEAD_DIM] = jnp.transpose(d_keys[a].astype(half))
         d_qkv[:, at + HEAD_DIM : at + 2 * HEAD_DIM] = jnp.transpose(d_values[a].astype(half))
+        part = dot_tn(d_qkv[:, at : at + 2 * HEAD_DIM], flat_rows(x_all)).astype(half)
+        g_pair[a] = part.reshape(g_pair.shape[1:])
         value_sum = jnp.sum(d_values[a], axis=1, keepdims=True)
         value_sum = jnp.transpose(jnp.broadcast_to(value_sum, (HEAD_DIM, 128)))[0:1]
-        shard_rows.append(
+        shards.append(
             jnp.concatenate(
                 [
-                    g_up_bias[:, a * shard : (a + 1) * shard],
-                    query_sum[a],
-                    value_sum,
-                    jnp.zeros((1, vecs.shape[1] - shard - 2 * HEAD_DIM), wide),
+                    g_up_bias[:, a * shard : a * shard + 128],
+                    g_up_bias[:, a * shard + 128 : (a + 1) * shard],
+                    jnp.concatenate([query_sum[a], value_sum], axis=1),
+                    jnp.zeros((5, 128), wide),
                 ],
-                axis=1,
+                axis=0,
             )
         )
-    grad_out = dot_tn(context[...], flat_rows(d_first_all)).astype(half)
-    piece = late.shape[2]
+    pair_plane.scatter(g_pair)
+    part = dot_tn(context[...], flat_rows(d_first_all)).astype(half)
     for a in range(2):
-        part = dot_tn(d_qkv[:, a * group : (a + 1) * group], flat_rows(x_all)).astype(half)
-        late[a, pl.ds(0, 6)] = part.reshape(6, piece, part.shape[1])
-        part = grad_out[a * HEAD_DIM : (a + 1) * HEAD_DIM]
-        late[a, pl.ds(6, 2)] = part.reshape(2, piece, part.shape[1])
-    late_plane.scatter(late)
-    small.plane(vecs, shard_rows)
+        g_out[a] = part[a * HEAD_DIM : (a + 1) * HEAD_DIM].reshape(g_out.shape[1:])
+    out_plane.scatter(g_out)
+    small.plane(vecs, shards)
     scatter = scatters[3]
 
     @pl.loop(0, 4)
@@ -611,14 +696,19 @@
             scatter.across()
 
     scatter.sides()
-    down_plane.share(g_down)
+    up_plane.share()
     scatter.through()
-    up_plane.share(g_up)
+    query_plane.turn(g_query)
+    pair_plane.turn(g_pair)
+    out_plane.turn(g_out)
     input_grad[...] = (hidden[...] + scatter.result()).astype(half)
-    late_plane.share(late)
-    for plane in (down_plane, up_plane, late_plane):
+    small.share(sums, shard_sums)
+    late = (query_plane, pair_plane, out_plane)
+    for plane in late:
+        plane.share()
+    for plane in (down_plane, up_plane, *late):
         plane.result()
-    small_out[...] = small.result()
+    small.finish(sums)
     for i, (src, dst) in enumerate(((x, x_all), (x, hidden_all), (x, d_second_all), (x, d_first_all))):
         gather_of(i, src, dst).finish()
     for scatter in scatters:
@@ -631,7 +721,8 @@
     rows, width = x.shape
     tokens = RING * rows
     shard = up.shape[1]
-    late = (PIECES, 4 * HEAD_DIM // PIECES, width)
+    one_head = (PIECES, HEAD_DIM // PIECES, width)
+    two_heads = (PIECES, 2 * HEAD_DIM // PIECES, width)
     up_pieces = (PIECES, width // PIECES, shard)
     down_pieces = (PIECES, shard // PIECES, width)
     gathered = pltpu.VMEM((RING, rows, width), half)
@@ -651,11 +742,11 @@
     scratch += [pltpu.VMEM((2, *up_pieces), half), pltpu.VMEM((2, *down_pieces), half)]
     scratch += [pltpu.VMEM((1, 2 * shard), wide), pltpu.VMEM((8, width), wide)]
     scratch += [turned, turned, pltpu.VMEM((tokens, 6 * HEAD_DIM), half), pltpu.VMEM((2, 1, HEAD_DIM), wide)]
-    scratch += [pltpu.VMEM((2, *late), half)]
+    scratch += [pltpu.VMEM((2, *pieces), half) for pieces in (one_head, two_heads, one_head)]
     scratch += [pltpu.SemaphoreType.DMA((8, Gather.slots)), pltpu.SemaphoreType.DMA((2, 6))]
     scratch += Scatter.scratch(width) * 4 + SmallSum.scratch
-    for pieces in (up_pieces, down_pieces, late):
-        scratch += PlaneSum.scratch(*pieces[1:])
+    for pieces in (up_pieces, down_pieces, one_head, two_heads, one_head):
+        scratch += TwoLevelSum.scratch(*pieces[1:])
     return pl.pallas_call(
         layer_kernel,
         out_shape=(
@@ -663,11 +754,14 @@
             jax.ShapeDtypeStruct((rows, width), half),
             jax.ShapeDtypeStruct(up_pieces, half),
             jax.ShapeDtypeStruct(down_pieces, half),
-            jax.ShapeDtypeStruct(late, half),
+            jax.ShapeDtypeStruct(one_head, half),
+            jax.ShapeDtypeStruct(two_heads, half),
+            jax.ShapeDtypeStruct(one_head, half),
             jax.ShapeDtypeStruct((8, width), wide),
+            jax.ShapeDtypeStruct((8, 128), wide),
         ),
         in_specs=[VMEM_WHOLE] * 15,
-        out_specs=(VMEM_WHOLE,) * 6,
+        out_specs=(VMEM_WHOLE,) * 9,
         scratch_shapes=scratch,
         compiler_params=pltpu.CompilerParams(
             collective_id=0, has_side_effects=True, vmem_limit_bytes=VMEM_BYTES
@@ -676,7 +770,7 @@
 
 
 def outputs_kernel(
-    out_in, grad_in, up_full, down_full, late_full, small,
+    out_in, grad_in, up_full, down_full, query_full, pair_full, out_full, small, shard_sums,
     out, input_grad, g_qkv, g_qv_bias, g_out, g_out_bias, g_gain1, g_bias1, g_up, g_up_bias, g_down, g_down_bias,
     g_gain2, g_bias2,
 ):
@@ -684,15 +778,14 @@
     input_grad[...] = grad_in[...]
     g_up[...] = flat_rows(up_full).astype(wide)
     g_down[...] = flat_rows(down_full).astype(wide)
-    late = flat_rows(late_full).astype(wide).reshape(4, HEAD_DIM, out.shape[1])
-    g_qkv[...] = late[:3]
-    g_out[...] = late[3]
+    g_qkv[0] = flat_rows(query_full).astype(wide)
+    g_qkv[1:] = flat_rows(pair_full).astype(wide).reshape(2, HEAD_DIM, out.shape[1])
+    g_out[...] = flat_rows(out_full).astype(wide)
     for i, ref in enumerate((g_out_bias, g_gain1, g_bias1, g_down_bias, g_gain2, g_bias2)):
         ref[...] = small[pl.ds(i, 1)]
-    ff = g_up_bias.shape[1]
-    g_up_bias[...] = small[pl.ds(6, 1), 0:ff]
     for i in range(2):
-        g_qv_bias[pl.ds(i, 1)] = small[pl.ds(6, 1), ff + i * HEAD_DIM : ff + (i + 1) * HEAD_DIM]
+        g_up_bias[:, i * 128 : (i + 1) * 128] = shard_sums[pl.ds(i, 1)]
+        g_qv_bias[pl.ds(i, 1)] = shard_sums[pl.ds(2, 1), i * HEAD_DIM : (i + 1) * HEAD_DIM]
 
 
 def write_outputs(results):
@@ -718,7 +811,7 @@
             vector,
             vector,
         ),
-        in_specs=[VMEM_WHOLE] * 6,
+        in_specs=[VMEM_WHOLE] * 9,
         out_specs=(VMEM_WHOLE,) * 14,
     )(*results)
 

time: 157 us -> 147 us (0.936); the launches traced: 155 us -> 147 us
  Pallas kernels: 155 us -> 146 us
    pallas_call x1, Pallas kernels: 151 us -> 143 us  [layer(): pl.pallas_call(layer_kernel, out_shape=(jax.ShapeDtypeStruct((rows, width...]
where the time goes in v5:
time: 147 us
  Pallas kernels  146 us (99%)
    pallas_call x1, Pallas kernels, layer(): pl.pallas_call(layer_kernel, out_shape=(jax.ShapeDtypeStruct((rows, width...  143 us
    pallas_call x1, Pallas kernels, write_outputs(): pl.pallas_call(outputs_kernel, out_shape=(block, block, jax.ShapeDtypeStr...  3.45 us

profile of v5, /device:TPU:0, one launch (start us, length us, event | category | flops | bytes accessed | tf_op | source)
XLA Modules:
  0.0 147.2 jit_solution(4207002641717771555)
XLA Ops:
  0.7 142.9 %shard_map.254 = (bf16[128,1024]{1,0:T(8,128)(2,1)}, bf16[128,1024]{1,0:T(8,128)(2,1)}, bf16[8,128,256]{2,1,0:T(8,128)(2,1)}, bf16[8,32,1024]{2,1,0:T(8,128)(2,1...) custom-call(bf16[128,1024]{1,0:T(8,128)(2,1)} %x.1, ...), custom_call_target="tpu_custom_call" | custom-call | tf_op jit(solution)/shard_map/pallas_call | solution.py:750
  143.6 3.4 %shard_map.255 = (bf16[128,1024]{1,0:T(8,128)(2,1)}, bf16[128,1024]{1,0:T(8,128)(2,1)}, f32[3,64,1024]{2,1,0:T(8,128)}, f32[2,64]{1,0:T(2,128)}, f32[64,1024]{1,...) custom-call(bf16[128,1024]{1,0:T(8,128)(2,1)} %get-tuple-element.37., ...), custom_call_target="tpu_custom_call" | custom-call | tf_op jit(solution)/shard_map/pallas_call | solution.py:796

commit v6 on v5

--- a/solution.py
+++ b/solution.py
@@ -267,15 +267,31 @@
 
     def hand_out(self, total):
         self.full[pl.ds(self.dp, 1)] = total.astype(half).reshape(1, *total.shape)
-        for r in range(1, PIECES):
-            place = self.full.at[self.dp]
-            remote(place, place, self.send, self.recv, 14 + r, self.peer(0, r)[1]).start()
+        self.send_piece(self.dp, 15, lax.rem(self.dp + 4, PIECES))
+        for r in range(1, 4):
+            self.send_piece(self.dp, 15 + r, self.along_y(r))
+
+    def send_piece(self, piece, slot, other):
+        place = self.full.at[piece]
+        remote(place, place, self.send, self.recv, slot, (other, self.t)).start()
+
+    def along_y(self, r):
+        return (self.dp // 4) * 4 + lax.rem(self.dp + r, 4)
+
+    def got(self, piece, slot):
+        place = self.full.at[piece]
+        remote(place, place, self.send, self.recv, slot, (self.dp, self.t)).wait_recv()
+
+    def pass_along(self):
+        neighbour = lax.rem(self.dp + 4, PIECES)
+        self.got(neighbour, 15)
+        for r in range(1, 4):
+            self.send_piece(neighbour, 18 + r, self.along_y(r))
 
     def result(self):
-        for r in range(1, PIECES):
-            piece = lax.rem(self.dp // 4 + r // 4, 2) * 4 + lax.rem(self.dp + 8 - r, 4)
-            place = self.full.at[piece]
-            remote(place, place, self.send, self.recv, 14 + r, (self.dp, self.t)).wait_recv()
+        for r in range(1, 4):
+            self.got(self.along_y(4 - r), 15 + r)
+            self.got(lax.rem(self.along_y(4 - r) + 4, PIECES), 18 + r)
         self.sent()
 
 
@@ -681,6 +697,7 @@
         g_out[a] = part[a * HEAD_DIM : (a + 1) * HEAD_DIM].reshape(g_out.shape[1:])
     out_plane.scatter(g_out)
     small.plane(vecs, shards)
+    down_plane.pass_along()
     scatter = scatters[3]
 
     @pl.loop(0, 4)
@@ -698,6 +715,7 @@
     scatter.sides()
     up_plane.share()
     scatter.through()
+    up_plane.pass_along()
     query_plane.turn(g_query)
     pair_plane.turn(g_pair)
     out_plane.turn(g_out)
@@ -706,6 +724,8 @@
     late = (query_plane, pair_plane, out_plane)
     for plane in late:
         plane.share()
+    for plane in late:
+        plane.pass_along()
     for plane in (down_plane, up_plane, *late):
         plane.result()
     small.finish(sums)

time: 147 us -> 145 us (0.986)
  Pallas kernels: 146 us -> 144 us
    pallas_call x1, Pallas kernels: 143 us -> 141 us  [layer(): pl.pallas_call(layer_kernel, out_shape=(jax.ShapeDtypeStruct((rows, width...]
where the time goes in v6:
time: 145 us
  Pallas kernels  144 us (99%)
    pallas_call x1, Pallas kernels, layer(): pl.pallas_call(layer_kernel, out_shape=(jax.ShapeDtypeStruct((rows, width...  141 us
    pallas_call x1, Pallas kernels, write_outputs(): pl.pallas_call(outputs_kernel, out_shape=(block, block, jax.ShapeDtypeStr...  3.45 us

profile of v6, /device:TPU:0, one launch (start us, length us, event | category | flops | bytes accessed | tf_op | source)
XLA Modules:
  0.0 145.0 jit_solution(6555767320065032357)
XLA Ops:
  0.7 140.7 %shard_map.254 = (bf16[128,1024]{1,0:T(8,128)(2,1)}, bf16[128,1024]{1,0:T(8,128)(2,1)}, bf16[8,128,256]{2,1,0:T(8,128)(2,1)}, bf16[8,32,1024]{2,1,0:T(8,128)(2,1...) custom-call(bf16[128,1024]{1,0:T(8,128)(2,1)} %x.1, ...), custom_call_target="tpu_custom_call" | custom-call | tf_op jit(solution)/shard_map/pallas_call | solution.py:770
  141.4 3.4 %shard_map.255 = (bf16[128,1024]{1,0:T(8,128)(2,1)}, bf16[128,1024]{1,0:T(8,128)(2,1)}, f32[3,64,1024]{2,1,0:T(8,128)}, f32[2,64]{1,0:T(2,128)}, f32[64,1024]{1,...) custom-call(bf16[128,1024]{1,0:T(8,128)(2,1)} %get-tuple-element.37., ...), custom_call_target="tpu_custom_call" | custom-call | tf_op jit(solution)/shard_map/pallas_call | solution.py:816
